TPU v7x, 32 devices: a whole 2x2x4 slice. The times are simulated.
32 devices in a mesh: seq: 8 (over z, core), span: 4 (over y, x).
Axes of the slice: x: 2, y: 2, z: 4, core: 2. Of those that a mesh axis runs over, the one named last changes fastest.
Arguments:
- q_prefill: bfloat16 [4, 1024, 64, 192], P('span', 'seq'), may hold values from -3000 to 3000
- kv_latent: bfloat16 [4, 1024, 512], P('span', 'seq'), may hold values from -200 to 200
- key_rope: bfloat16 [4, 1024, 64], P('span', 'seq'), may hold values from -6 to 6
- segment_ids: int32 [4, 1024], replicated, may hold values from 0 to 15, never falling along the last dimension, each value on 1 to 512 neighbouring positions
- assignment: int32 [64], replicated, may hold values from 0 to 63, each once
- absorb_key: bfloat16 [64, 128, 512], replicated, may hold values from -0.5 to 0.5
- absorb_value: bfloat16 [64, 512, 128], replicated, may hold values from -0.25 to 0.25
- q_decode: bfloat16 [2, 64, 64, 192], P(None, 'span'), may hold values from -3000 to 3000
- new_latent: bfloat16 [2, 64, 512], P(None, 'span'), may hold values from -6 to 6
- new_rope: bfloat16 [2, 64, 64], P(None, 'span'), may hold values from -6 to 6
Outputs:
- prefill_out: bfloat16 [4, 1024, 8192], P('span', 'seq')
- decode_out: bfloat16 [2, 64, 8192], P(None, 'span')
Inputs may be any that keep to these rules, and one draw needn't show every extreme that they name: `segment_ids`: within a span the numbers never fall; each of the 16 numbers appears, on 1 to 512 positions. `assignment`: each sequence number appears once; entry c * 16 + d is the sequence of prompt d of span c, and sequence g is decoded at span index g // 16, slot g % 16.
All inputs are finite; a program needn't handle non-finite values.
Results may differ from a plain program's by a relative error of at most 0.014.
Values may be sent and summed in bfloat16 or wider, within the bound.
No kernel may reach another device: no remote copies, remote signals or barrier semaphores. Data moves between devices by JAX's collectives and lax.ppermute only.
A program may use at most 192 MiB of HBM per device.

v0:
```python
import functools
import math

import jax
import jax.numpy as jnp
from jax import lax
from jax.experimental import pallas as pl
from jax.experimental.pallas import tpu as pltpu
from jax.sharding import PartitionSpec as P


NOPE = 128
ROPE = 64
LAT = 512
VHEAD = 128
WIDTH = LAT + 2 * ROPE

NEG = -1e30
EPS = 1e-06
SCALE2 = (NOPE + ROPE) ** (-0.5) * math.log2(math.e)
TOK = 16
PARTS = 2
CHUNK = 512
VMEM_LIMIT = 60 << 20

NT = (((1,), (1,)), ((), ()))
ANY = pl.BlockSpec(memory_space=pltpu.HBM)


def normed(values):
    values = values.astype(jnp.float32)
    mean = jnp.sum(values * values, axis=-1, keepdims=True) * (1.0 / values.shape[-1])
    return (values * lax.rsqrt(mean + EPS)).astype(jnp.bfloat16)


def prepare_kernel(info_ref, lat_ref, rope_ref, q_ref, nl_ref, nr_ref, cache_ref, pack_ref, *, group):
    steps, docs, block, _ = q_ref.shape
    cache_ref[:, :LAT] = normed(lat_ref[...])
    rope = jnp.transpose(rope_ref[...].astype(jnp.float32))
    rope = rope.astype(jnp.bfloat16)
    cache_ref[:, LAT:] = jnp.concatenate([rope, jnp.zeros_like(rope)], axis=1)
    wide = group * NOPE
    for t in range(steps):
        row = pl.ds(t * docs, docs)
        q = jnp.swapaxes(q_ref[t].astype(jnp.float32), 0, 1)
        part = q[:group]
        for k in range(1, block // group):
            chosen = lax.rem(info_ref[0], block // group) == k
            part = jnp.where(chosen, q[k * group : (k + 1) * group], part)
        part = part.astype(jnp.bfloat16)
        pack_ref[row, wide : wide + LAT] = normed(nl_ref[t])
        base = wide + LAT
        for h in range(group):
            pack_ref[row, h * NOPE : (h + 1) * NOPE] = part[h, :, :NOPE]
            pack_ref[row, base + h * ROPE : base + (h + 1) * ROPE] = part[h, :, NOPE:]
        rope = nr_ref[t]
        pack_ref[row, base + group * ROPE :] = jnp.concatenate([rope, jnp.zeros_like(rope)], axis=1)


def prepare(info, latent, rope, q_decode, new_latent, new_rope, group):
    tokens = latent.shape[0]
    steps, docs, _, size = q_decode.shape
    block = max(group, 8)
    ratio = block // group
    full = lambda x: pl.BlockSpec(x.shape, lambda i, info: (0,) * x.ndim)
    out_shape = (
        jax.ShapeDtypeStruct((tokens, WIDTH), jnp.bfloat16),
        jax.ShapeDtypeStruct((steps * docs, group * size + WIDTH), jnp.bfloat16),
    )
    return pl.pallas_call(
        functools.partial(prepare_kernel, group=group),
        grid_spec=pltpu.PrefetchScalarGridSpec(
            num_scalar_prefetch=1,
            grid=(1,),
            in_specs=[
                full(latent),
                full(rope),
                pl.BlockSpec((steps, docs, block, size), lambda i, info: (0, 0, info[0] // ratio, 0)),
                full(new_latent),
                full(new_rope),
            ],
            out_specs=tuple(full(s) for s in out_shape),
        ),
        out_shape=out_shape,
        name="prepare",
    )(info, latent, rope, q_decode, new_latent, new_rope)


def absorb_kernel(q_hbm, ak_hbm, o_hbm, q_buf, ak_buf, o_buf, q_sem, ak_sem, o_sem, *, group):
    heads, _, tokens = q_buf.shape
    number = heads // group

    def copies(i):
        part = pl.ds(i * group, group)
        return (
            pltpu.make_async_copy(q_hbm.at[part], q_buf.at[part], q_sem.at[i]),
            pltpu.make_async_copy(ak_hbm.at[part], ak_buf.at[part], ak_sem.at[i]),
        )

    def result(i):
        part = pl.ds(pl.multiple_of(i * group * TOK, group * TOK), group * TOK)
        return pltpu.make_async_copy(o_buf.at[:, part], o_hbm.at[:, part], o_sem.at[i])

    for i in range(number):
        for copy in copies(i):
            copy.start()

    @pl.loop(0, number)
    def _(i):
        for copy in copies(i):
            copy.wait()
        for j in range(group):
            h = i * group + j
            q = jnp.transpose(q_buf[h])
            lat = jnp.dot(q[:, :NOPE], ak_buf[h], preferred_element_type=jnp.float32)
            row = pl.ds(pl.multiple_of(h * TOK, TOK), TOK)
            o_buf[:, row, :LAT] = lat.astype(jnp.bfloat16).reshape(tokens // TOK, TOK, LAT)
            rope = jnp.concatenate([q[:, NOPE:], jnp.zeros_like(q[:, NOPE:])], axis=1)
            o_buf[:, row, LAT:] = rope.reshape(tokens // TOK, TOK, 2 * ROPE)
        result(i).start()

    for i in range(number):
        result(i).wait()


def absorb_prefill(q, absorb_key, group=8):
    heads, size, tokens = q.shape
    shape = (tokens // TOK, heads * TOK, WIDTH)
    return pl.pallas_call(
        functools.partial(absorb_kernel, group=group),
        in_specs=[ANY, ANY],
        out_specs=ANY,
        out_shape=jax.ShapeDtypeStruct(shape, jnp.bfloat16),
        scratch_shapes=[
            pltpu.VMEM(q.shape, jnp.bfloat16),
            pltpu.VMEM(absorb_key.shape, jnp.bfloat16),
            pltpu.VMEM(shape, jnp.bfloat16),
            pltpu.SemaphoreType.DMA((heads // group,)),
            pltpu.SemaphoreType.DMA((heads // group,)),
            pltpu.SemaphoreType.DMA((heads // group,)),
        ],
        cost_estimate=pl.CostEstimate(
            flops=2 * tokens * heads * NOPE * LAT,
            bytes_accessed=2 * heads * (tokens * (size + WIDTH) + NOPE * LAT),
            transcendentals=0,
        ),
        compiler_params=pltpu.CompilerParams(vmem_limit_bytes=VMEM_LIMIT),
        name="absorb_prefill",
    )(q, absorb_key)


def source_of(i, seq_idx, count):
    half = count // 2
    origin = seq_idx if i < half else seq_idx + 1 - 2 * lax.rem(seq_idx, 2)
    return lax.rem(origin - 2 * (i % half) + count, count)


def direct_source(i, seq_idx, count):
    return lax.rem(seq_idx - i + count, count)


def gather_copies(pieces, kbuf, sems, seq_idx):
    rows = pieces[0].shape[0]
    copies = []
    for i, piece in enumerate(pieces):
        start = pl.multiple_of(source_of(i, seq_idx, len(pieces)) * rows, TOK)
        copies.append(pltpu.make_async_copy(piece, kbuf.at[pl.ds(start, rows)], sems.at[i]))
    return copies


def prefill_kernel(
    info_ref, segs_ref, seg_ref, qa_hbm, *refs, count, part, fast, slow, heads, chunk, aliased
):
    pieces = refs[:count]
    refs = refs[count + (1 if aliased else 0) :]
    av_hbm, o_ref, kbuf, olat, av, qa_buf, ksem, qsem, vsem = refs
    blocks, rows, _ = qa_buf.shape
    tokens = olat.shape[1]
    length = kbuf.shape[0]
    seq_idx = info_ref[0]
    span_idx = info_ref[1]
    av_copy = pltpu.make_async_copy(av_hbm.at[pl.ds(part * heads, heads)], av, vsem)
    copies = gather_copies(pieces, kbuf, ksem, seq_idx)

    def qa_copy(i):
        return pltpu.make_async_copy(
            qa_hbm.at[i, pl.ds(part * rows, rows)], qa_buf.at[i], qsem.at[i]
        )

    ahead = min(2, blocks)
    near = fast // tokens + 1
    used = []
    for i in range(count):
        gap = seq_idx - source_of(i, seq_idx, count)
        used.append((gap >= 0) & (gap <= near) | (seq_idx < near))
    for copy, use in zip(copies, used):
        pl.when(use)(copy.start)
    for i in range(ahead):
        qa_copy(i).start()
    for copy, use in zip(copies, used):
        pl.when(use)(copy.wait)
    seg = seg_ref[pl.ds(span_idx, 1), :]
    row = lax.broadcasted_iota(jnp.int32, (TOK, 1), 0)

    @pl.loop(0, blocks)
    def _(tb):
        base = seq_idx * tokens + tb * TOK
        qa_copy(tb).wait()

        @pl.when(tb + ahead < blocks)
        def _():
            qa_copy(tb + ahead).start()

        @pl.when(tb == blocks // 2)
        def _():
            av_copy.start()

        def attend(window, begin, chunk):
            begin = pl.multiple_of(begin, TOK)
            seg_q = jnp.zeros((TOK, 1), jnp.int32)
            for i in range(TOK):
                seg_q = jnp.where(row == i, segs_ref[span_idx, base + i], seg_q)
            start = jnp.sum((seg < seg_q).astype(jnp.int32), axis=1, keepdims=True)
            pos_k = begin + lax.broadcasted_iota(jnp.int32, (TOK, window), 1)
            keep = (pos_k >= start) & (pos_k <= base + row)
            bias = jnp.where(keep, 0.0, NEG)[None]
            for c in range(0, heads * TOK, chunk):
                q = qa_buf[tb, pl.ds(c, chunk), :]
                keys = kbuf[pl.ds(begin, window), :]
                s = lax.dot_general(q, keys, NT, preferred_element_type=jnp.float32)
                s = (s.reshape(chunk // TOK, TOK, window) + bias).reshape(chunk, window)
                m = jnp.max(s, axis=1, keepdims=True)
                p = jnp.exp2((s - m) * SCALE2)
                den = jnp.sum(p, axis=1, keepdims=True)
                o = jnp.dot(
                    p.astype(jnp.bfloat16),
                    kbuf[pl.ds(begin, window), :LAT],
                    preferred_element_type=jnp.float32,
                )
                o = (o * (1.0 / den)).astype(jnp.bfloat16)
                place = pl.ds(pl.multiple_of(tb * TOK, TOK), TOK)
                olat[pl.ds(c // TOK, chunk // TOK), place, :] = o.reshape(chunk // TOK, TOK, LAT)

        fast_begin = jnp.clip(base + TOK - fast, 0, length - fast)
        slow_begin = jnp.clip(base + TOK - slow, 0, length - slow)

        ahead_seg = segs_ref[span_idx, jnp.maximum(fast_begin - 1, 0)]
        reaches = (fast_begin > 0) & (ahead_seg == segs_ref[span_idx, base])

        @pl.when(jnp.logical_not(reaches))
        def _():
            attend(fast, fast_begin, chunk)

        @pl.when(reaches)
        def _():
            attend(slow, slow_begin, 128)

    av_copy.wait()
    for h in range(heads):
        r = jnp.dot(olat[h], av[h], preferred_element_type=jnp.float32)
        o_ref[:, h * VHEAD : (h + 1) * VHEAD] = r.astype(jnp.bfloat16)


def attend_prefill(info, segment_ids, qa, pieces, absorb_value, part, parts, most, out=None):
    blocks, rows, _ = qa.shape
    tokens = blocks * TOK
    heads = rows // TOK // parts
    count = len(pieces)
    length = count * tokens
    fast = min(most, length)
    slow = min(most + 128, length)
    aliased = out is not None
    args = [info, segment_ids, segment_ids, qa, *pieces, *([out] if aliased else []), absorb_value]
    return pl.pallas_call(
        functools.partial(
            prefill_kernel,
            count=count,
            part=part,
            fast=fast,
            slow=slow,
            heads=heads,
            chunk=CHUNK,
            aliased=aliased,
        ),
        grid_spec=pltpu.PrefetchScalarGridSpec(
            num_scalar_prefetch=2,
            grid=(1,),
            in_specs=[
                pl.BlockSpec(segment_ids.shape, lambda i, *_: (0, 0)),
                *([ANY] * (count + aliased + 2)),
            ],
            out_specs=pl.BlockSpec((tokens, heads * VHEAD), lambda i, *_: (0, part)),
            scratch_shapes=[
                pltpu.VMEM((length, WIDTH), jnp.bfloat16),
                pltpu.VMEM((heads, tokens, LAT), jnp.bfloat16),
                pltpu.VMEM((heads, LAT, VHEAD), jnp.bfloat16),
                pltpu.VMEM((blocks, heads * TOK, WIDTH), jnp.bfloat16),
                pltpu.SemaphoreType.DMA((count,)),
                pltpu.SemaphoreType.DMA((blocks,)),
                pltpu.SemaphoreType.DMA,
            ],
        ),
        out_shape=jax.ShapeDtypeStruct((tokens, parts * heads * VHEAD), jnp.bfloat16),
        input_output_aliases={4 + count: 0} if aliased else {},
        cost_estimate=pl.CostEstimate(
            flops=2 * tokens * heads * (fast * (WIDTH + LAT) + LAT * VHEAD),
            bytes_accessed=2 * heads * (tokens * (WIDTH + VHEAD) + LAT * VHEAD),
            transcendentals=tokens * heads * fast,
        ),
        compiler_params=pltpu.CompilerParams(vmem_limit_bytes=VMEM_LIMIT),
    )(*args)


def decode_kernel(info_ref, assign_ref, seg_ref, *refs, count, spans, docs, steps, group):
    pieces = refs[:count]
    packs = refs[count : count + spans]
    ak_hbm, av_hbm, _, o_ref, kbuf, qa, pack_ref, ak_ref, av_ref, ksem, sems = refs[count + spans :]
    seq_idx = info_ref[0]
    span_idx = info_ref[1]
    near = steps * docs
    rows = near * group
    copies = gather_copies(pieces, kbuf, ksem, seq_idx)
    own = pl.ds(seq_idx * group, group)
    early = [
        pltpu.make_async_copy(pack, pack_ref.at[pl.ds(i * near, near)], sems.at[i])
        for i, pack in enumerate(packs)
    ]
    early.append(pltpu.make_async_copy(ak_hbm.at[own], ak_ref, sems.at[spans]))
    late = pltpu.make_async_copy(av_hbm.at[own], av_ref, sems.at[spans + 1])
    for copy in (*early, *copies, late):
        copy.start()
    row = lax.broadcasted_iota(jnp.int32, (near, 1), 0)
    want = jnp.zeros((near, 1), jnp.int32)
    for d in range(docs):
        want = jnp.where(lax.rem(row, docs) == d, assign_ref[span_idx * docs + d], want)
    want = want * steps
    step = row // docs
    lane = lax.broadcasted_iota(jnp.int32, (1, spans * near), 1)
    place = lax.rem(lane, near)
    owner = lax.rem(span_idx - lane // near + spans, spans)
    number = (owner * docs + lax.rem(place, docs)) * steps + place // docs
    pick = jnp.where(number == want + step, 1.0, 0.0).astype(jnp.bfloat16)
    wide = group * NOPE
    for copy in early:
        copy.wait()
    pack = pack_ref[...]
    nope = jnp.dot(pick, pack[:, :wide], preferred_element_type=jnp.float32).astype(jnp.bfloat16)
    rope = jnp.dot(
        pick, pack[:, wide + LAT : wide + LAT + group * ROPE], preferred_element_type=jnp.float32
    ).astype(jnp.bfloat16)
    fresh = jnp.concatenate(
        [pack[:, wide : wide + LAT], pack[:, wide + LAT + group * ROPE :]], axis=1
    )
    for h in range(group):
        lat = jnp.dot(
            nope[:, h * NOPE : (h + 1) * NOPE], ak_ref[h], preferred_element_type=jnp.float32
        )
        qa[pl.ds(h * near, near), :LAT] = lat.astype(jnp.bfloat16)
        part = rope[:, h * ROPE : (h + 1) * ROPE]
        qa[pl.ds(h * near, near), LAT:] = jnp.concatenate([part, jnp.zeros_like(part)], axis=1)
    for copy in copies:
        copy.wait()
    keys = kbuf[...]
    seg = seg_ref[pl.ds(span_idx, 1), :]
    old_bias = jnp.where(seg == lax.rem(row, docs), 0.0, NEG)[None]
    new_bias = jnp.where((number >= want) & (number <= want + step), 0.0, NEG)[None]
    query = qa[...]
    old = lax.dot_general(query, keys, NT, preferred_element_type=jnp.float32)
    old = (old.reshape(group, near, -1) + old_bias).reshape(rows, -1)
    new = lax.dot_general(query, fresh, NT, preferred_element_type=jnp.float32)
    new = (new.reshape(group, near, -1) + new_bias).reshape(rows, -1)
    m = jnp.maximum(jnp.max(old, axis=1, keepdims=True), jnp.max(new, axis=1, keepdims=True))
    old = jnp.exp2((old - m) * SCALE2)
    new = jnp.exp2((new - m) * SCALE2)
    den = jnp.sum(old, axis=1, keepdims=True) + jnp.sum(new, axis=1, keepdims=True)
    o = jnp.dot(old.astype(jnp.bfloat16), keys[:, :LAT], preferred_element_type=jnp.float32)
    o = o + jnp.dot(new.astype(jnp.bfloat16), fresh[:, :LAT], preferred_element_type=jnp.float32)
    o = o * (1.0 / den)
    high = o.astype(jnp.bfloat16)
    low = (o - high.astype(jnp.float32)).astype(jnp.bfloat16)
    late.wait()
    for h in range(group):
        both = jnp.concatenate(
            [high[h * near : (h + 1) * near], low[h * near : (h + 1) * near]], axis=0
        )
        r = jnp.dot(both, av_ref[h], preferred_element_type=jnp.float32)
        o_ref[:, h * VHEAD : (h + 1) * VHEAD] = (r[:near] + r[near:]).astype(jnp.bfloat16)


def attend_decode(info, assignment, segment_ids, pieces, packs, absorb_key, absorb_value, after, steps):
    near, size = packs[0].shape
    docs = near // steps
    count, spans = len(pieces), len(packs)
    tokens = pieces[0].shape[0]
    heads = absorb_key.shape[0]
    group = heads // count
    rows = near * group
    length = count * tokens
    return pl.pallas_call(
        functools.partial(
            decode_kernel, count=count, spans=spans, docs=docs, steps=steps, group=group
        ),
        grid_spec=pltpu.PrefetchScalarGridSpec(
            num_scalar_prefetch=2,
            grid=(1,),
            in_specs=[
                pl.BlockSpec(segment_ids.shape, lambda i, *_: (0, 0)),
                *([ANY] * (count + spans + 3)),
            ],
            out_specs=pl.BlockSpec((near, group * VHEAD), lambda i, *_: (0, 0)),
            scratch_shapes=[
                pltpu.VMEM((length, WIDTH), jnp.bfloat16),
                pltpu.VMEM((rows, WIDTH), jnp.bfloat16),
                pltpu.VMEM((spans * near, size), jnp.bfloat16),
                pltpu.VMEM((group, NOPE, LAT), jnp.bfloat16),
                pltpu.VMEM((group, LAT, VHEAD), jnp.bfloat16),
                pltpu.SemaphoreType.DMA((count,)),
                pltpu.SemaphoreType.DMA((spans + 2,)),
            ],
        ),
        out_shape=jax.ShapeDtypeStruct((near, group * VHEAD), jnp.bfloat16),
        cost_estimate=pl.CostEstimate(
            flops=2 * rows * length * (WIDTH + LAT),
            bytes_accessed=2 * (length * WIDTH + group * LAT * VHEAD * 2),
            transcendentals=rows * length,
        ),
        compiler_params=pltpu.CompilerParams(vmem_limit_bytes=VMEM_LIMIT),
        name="attend_decode",
    )(info, assignment, segment_ids, *pieces, *packs, absorb_key, absorb_value, after)


def select_kernel(info_ref, assign_ref, *refs, spans, docs, steps):
    parts = refs[:spans]
    o_ref, value, sems = refs[spans + 1 :]
    span_idx = info_ref[1]
    near = steps * docs
    copies = [
        pltpu.make_async_copy(part, value.at[pl.ds(i * near, near)], sems.at[i])
        for i, part in enumerate(parts)
    ]
    for copy in copies:
        copy.start()
    lane = lax.broadcasted_iota(jnp.int32, (1, spans * near), 1)
    number = jnp.zeros((1, spans * near), jnp.int32)
    for j in range(spans):
        source = lax.rem(span_idx - j + spans, spans)
        for d in range(docs):
            here = (lane // near == j) & (lax.rem(lane, docs) == d)
            number = jnp.where(here, assign_ref[source * docs + d], number)
    number = number * steps + lax.rem(lane, near) // docs
    row = lax.broadcasted_iota(jnp.int32, (near, 1), 0)
    want = (span_idx * docs + lax.rem(row, docs)) * steps + row // docs
    pick = jnp.where(number == want, 1.0, 0.0).astype(jnp.bfloat16)
    for copy in copies:
        copy.wait()
    o_ref[...] = jnp.dot(pick, value[...], preferred_element_type=jnp.float32).astype(jnp.bfloat16)


def select_rows(info, assignment, parts, after, steps):
    near, size = parts[0].shape
    spans = len(parts)
    return pl.pallas_call(
        functools.partial(select_kernel, spans=spans, docs=near // steps, steps=steps),
        grid_spec=pltpu.PrefetchScalarGridSpec(
            num_scalar_prefetch=2,
            grid=(1,),
            in_specs=[ANY] * (spans + 1),
            out_specs=pl.BlockSpec((near, size), lambda i, *_: (0, 0)),
            scratch_shapes=[
                pltpu.VMEM((spans * near, size), jnp.bfloat16),
                pltpu.SemaphoreType.DMA((spans,)),
            ],
        ),
        out_shape=jax.ShapeDtypeStruct((near, size), jnp.bfloat16),
        name="select_rows",
    )(info, assignment, *parts, after)


def assemble_kernel(info_ref, *refs):
    parts, o_ref, sems = refs[:-2], refs[-2], refs[-1]
    _, size = parts[0].shape
    copies = []
    for i, part in enumerate(parts):
        start = pl.multiple_of(direct_source(i, info_ref[0], len(parts)) * size, 128)
        copies.append(pltpu.make_async_copy(part, o_ref.at[:, pl.ds(start, size)], sems.at[i]))
    for copy in copies:
        copy.start()
    for copy in copies:
        copy.wait()


def assemble(info, parts):
    near, size = parts[0].shape
    shape = (near, len(parts) * size)
    return pl.pallas_call(
        assemble_kernel,
        grid_spec=pltpu.PrefetchScalarGridSpec(
            num_scalar_prefetch=1,
            grid=(1,),
            in_specs=[ANY] * len(parts),
            out_specs=pl.BlockSpec(shape, lambda i, info: (0, 0)),
            scratch_shapes=[pltpu.SemaphoreType.DMA((len(parts),))],
        ),
        out_shape=jax.ShapeDtypeStruct(shape, jnp.bfloat16),
        name="assemble",
    )(info, *parts)


def spread_far(value, count):
    return [value] + [
        lax.ppermute(value, "seq", [(i, (i + 2 * k) % count) for i in range(count)])
        for k in range(1, count // 2)
    ]


def spread_near(pieces, count):
    swap = [(i, i ^ 1) for i in range(count)]
    return pieces + [lax.ppermute(p, "seq", swap) for p in pieces]


def spread(value, axis, count):
    return [value] + [
        lax.ppermute(value, axis, [(i, (i + k) % count) for i in range(count)])
        for k in range(1, count)
    ]


def body(
    q_prefill,
    kv_latent,
    key_rope,
    segment_ids,
    assignment,
    absorb_key,
    absorb_value,
    q_decode,
    new_latent,
    new_rope,
):
    steps, docs, heads, _ = q_decode.shape
    count = lax.axis_size("seq")
    spans = lax.axis_size("span")
    group = heads // count
    most = segment_ids.shape[1] // 2
    info = jnp.stack([lax.axis_index("seq"), lax.axis_index("span")]).astype(jnp.int32)

    cache, pack = prepare(
        info, kv_latent[0], key_rope[0].T, q_decode, new_latent, new_rope, group
    )
    pieces = spread_far(cache, count)
    packs = spread(pack, "span", spans)
    qa = absorb_prefill(q_prefill[0].transpose(1, 2, 0), absorb_key)
    far, qa = lax.optimization_barrier((pieces[1:], qa))
    pieces = spread_near([cache, *far], count)
    decoded = attend_decode(
        info, assignment, segment_ids, pieces, packs, absorb_key, absorb_value, qa, steps
    )
    returned = spread(decoded, "span", spans)
    out = attend_prefill(info, segment_ids, qa, pieces, absorb_value, 0, PARTS, most)
    chosen = select_rows(info, assignment, returned, out, steps)
    finals = spread(chosen, "seq", count)
    for part in range(1, PARTS):
        out = attend_prefill(info, segment_ids, qa, pieces, absorb_value, part, PARTS, most, out)
    decode_out = assemble(info, finals)
    return (out[None], decode_out.reshape(steps, docs, heads * VHEAD))


def solution(mesh):
    in_specs = (
        P("span", "seq", None, None),
        P("span", "seq", None),
        P("span", "seq", None),
        P(),
        P(),
        P(),
        P(),
        P(None, "span", None, None),
        P(None, "span", None),
        P(None, "span", None),
    )
    out_specs = (P("span", "seq", None), P(None, "span", None))
    return jax.shard_map(body, mesh=mesh, in_specs=in_specs, out_specs=out_specs, check_vma=False)
```

profile of v0, /device:TPU:17, one launch (start us, length us, event | category | flops | bytes accessed | tf_op | source)
XLA Modules:
  0.0 87.0 jit_solution(17465868914704451844)
XLA Ops:
  0.6 0.7 pad_add_fusion.info_ref
  1.3 2.6 %prepare.1 = (bf16[128,640]{1,0:T(8,128)(2,1)}, bf16[32,2176]{1,0:T(8,128)(2,1)}) custom-call(s32[2]{0:T(128)} %pad_add_fusion.info_ref, bf16[128,512]{1,0:T(8,128)(2,1)} %bitcast.14, bf16[64,128]{1,0:T(8,128)(2,1)} %bitcast.15, bf16[2,16,64,192]{3,2,1,0:T(8,128)(2,1)} %q_ref.1, bf16[2,16,512]{2,1,0:T(8,128)(2,1)} %nl_ref.1, bf16[2,16,64]{2,1,0:T(8,128)(2,1)} %nr_ref.1), custom_call_target="tpu_custom_call" | custom-call | tf_op jit(solution)/shard_map/prepare/pallas_call | solution.py:70
  4.0 3.2 %collective-permute-start.1 = (bf16[128,640]{1,0:T(8,128)(2,1)}, bf16[128,640]{1,0:T(8,128)(2,1)S(1)}, u32[]{:S(2)}, u32[]{:S(2)}) collective-permute-start(bf16[128,640]{1,0:T(8,128)(2,1)} %get-tuple-element.8.refs_0_), channel_id=1, source_target_pairs={{0,16},{4,20},{8,24},{12,28},{16,0},{20,4},{24,8},{28,12},{1,17},{... | collective-permute-start | bytes 491528 | tf_op jit(solution)/shard_map/ppermute | solution.py:511
  7.2 2.2 %collective-permute-start.9 = (bf16[32,2176]{1,0:T(8,128)(2,1)}, bf16[32,2176]{1,0:T(8,128)(2,1)S(1)}, u32[]{:S(2)}, u32[]{:S(2)}) collective-permute-start(bf16[32,2176]{1,0:T(8,128)(2,1)} %get-tuple-element.13.refs_8_), channel_id=1, source_target_pairs={{0,3},{1,0},{2,1},{3,2},{4,7},{5,4},{6,5},{7,6},{8,11},{9,8},{10,9... | collective-permute-start | bytes 417800 | tf_op jit(solution)/shard_map/ppermute | solution.py:523
  9.4 0.2 collective-permute-start.8
  9.6 8.5 %absorb_prefill.1.qa_hbm.refs_14_ = bf16[8,1024,640]{2,1,0:T(8,128)(2,1)} custom-call(bf16[64,192,128]{2,1,0:T(8,128)(2,1)} %bitcast.12, bf16[64,128,512]{2,1,0:T(8,128)(2,1)} %refs_12_.1), custom_call_target="tpu_custom_call" | custom-call | flops 1073741824 | bytes 22020096 | tf_op jit(solution)/shard_map/absorb_prefill/pallas_call | solution.py:129
  18.2 1.9 %collective-permute-start.3 = (bf16[128,640]{1,0:T(8,128)(2,1)S(1)}, bf16[128,640]{1,0:T(8,128)(2,1)S(1)}, u32[]{:S(2)}, u32[]{:S(2)}) collective-permute-start(bf16[128,640]{1,0:T(8,128)(2,1)S(1)} %copy-done), channel_id=1, source_target_pairs={{0,4},{4,0},{8,12},{12,8},{16,20},{20,16},{24,28},{28,24},{1,5},{5... | collective-permute-start | bytes 491528 | tf_op jit(solution)/shard_map/ppermute | solution.py:518
  20.1 1.1 %collective-permute-done.refs_1_ = bf16[128,640]{1,0:T(8,128)(2,1)S(1)} collective-permute-done((bf16[128,640]{1,0:T(8,128)(2,1)}, bf16[128,640]{1,0:T(8,128)(2,1)S(1)}, u32[]{:S(2)}, u32[]{:S(2)}) %collective-permute-start) | collective-permute-done | bytes 163872 | tf_op jit(solution)/shard_map/ppermute | solution.py:511
  21.2 1.2 %collective-permute-start.4 = (bf16[128,640]{1,0:T(8,128)(2,1)S(1)}, bf16[128,640]{1,0:T(8,128)(2,1)S(1)}, u32[]{:S(2)}, u32[]{:S(2)}) collective-permute-start(bf16[128,640]{1,0:T(8,128)(2,1)S(1)} %collective-permute-done.refs_1_), channel_id=1, source_target_pairs={{0,4},{4,0},{8,12},{12,8},{16,20},{20,16},{24,28},{28,24},{1,5},{5... | collective-permute-start | bytes 491528 | tf_op jit(solution)/shard_map/ppermute | solution.py:518
  22.5 0.5 collective-permute-start.6
  23.0 1.3 %collective-permute-start.7 = (bf16[32,2176]{1,0:T(8,128)(2,1)S(1)}, bf16[32,2176]{1,0:T(8,128)(2,1)S(1)}, u32[]{:S(2)}, u32[]{:S(2)}) collective-permute-start(bf16[32,2176]{1,0:T(8,128)(2,1)S(1)} %copy-done.8), channel_id=1, source_target_pairs={{0,1},{1,2},{2,3},{3,0},{4,5},{5,6},{6,7},{7,4},{8,9},{9,10},{10,1... | collective-permute-start | bytes 417800 | tf_op jit(solution)/shard_map/ppermute | solution.py:523
  24.2 4.8 %collective-permute-done.7.refs_9_ = bf16[32,2176]{1,0:T(8,128)(2,1)S(1)} collective-permute-done((bf16[32,2176]{1,0:T(8,128)(2,1)S(1)}, bf16[32,2176]{1,0:T(8,128)(2,1)S(1)}, u32[]{:S(2)}, u32[]{:S(2)}) %collective-permute-start.7) | collective-permute-done | bytes 139296 | tf_op jit(solution)/shard_map/ppermute | solution.py:523
  29.2 0.5 copy-done.11
  29.9 0.7 copy-done.7
  30.6 6.5 %attend_decode.1.refs_0_ = bf16[32,1024]{1,0:T(8,128)(2,1)} custom-call(s32[2]{0:T(128)} %pad_add_fusion.info_ref, s32[64]{0:T(128)} %assign_ref.3, s32[4,1024]{1,0:T(4,128)} %seg_ref.5, bf16[128,640]{1,0:T(8,128)(2,1)} %get-tuple-element.8.refs_0_, bf16[128,640]{1,0:T(8,128)(2,1)} %copy-done.3, bf16[128,640]{1,0:T(8,128)(2,1)} %copy-done.2, ...), custom_call_target="tpu_custom_call" | custom-call | flops 603979776 | bytes 3407872 | tf_op jit(solution)/shard_map/attend_decode/pallas_call | solution.py:399
  37.1 1.3 %collective-permute-start.12 = (bf16[32,1024]{1,0:T(8,128)(2,1)}, bf16[32,1024]{1,0:T(8,128)(2,1)S(1)}, u32[]{:S(2)}, u32[]{:S(2)}) collective-permute-start(bf16[32,1024]{1,0:T(8,128)(2,1)} %attend_decode.1.refs_0_), channel_id=1, source_target_pairs={{0,3},{1,0},{2,1},{3,2},{4,7},{5,4},{6,5},{7,6},{8,11},{9,8},{10,9... | collective-permute-start | bytes 196616 | tf_op jit(solution)/shard_map/ppermute | solution.py:523
  38.4 0.2 collective-permute-start.11
  38.6 1.2 %collective-permute-start.10 = (bf16[32,1024]{1,0:T(8,128)(2,1)}, bf16[32,1024]{1,0:T(8,128)(2,1)S(1)}, u32[]{:S(2)}, u32[]{:S(2)}) collective-permute-start(bf16[32,1024]{1,0:T(8,128)(2,1)} %attend_decode.1.refs_0_), channel_id=1, source_target_pairs={{0,1},{1,2},{2,3},{3,0},{4,5},{5,6},{6,7},{7,4},{8,9},{9,10},{10,1... | collective-permute-start | bytes 196616 | tf_op jit(solution)/shard_map/ppermute | solution.py:523
  39.8 15.3 %shard_map.113.refs_8_.refs_4_ = bf16[128,8192]{1,0:T(8,128)(2,1)} custom-call(s32[2]{0:T(128)} %pad_add_fusion.info_ref, s32[4,1024]{1,0:T(4,128)} %seg_ref.5, s32[4,1024]{1,0:T(4,128)} %seg_ref.5, bf16[8,1024,640]{2,1,0:T(8,128)(2,1)} %absorb_prefill.1.qa_hbm.refs_14_, bf16[128,640]{1,0:T(8,128)(2,1)} %get-tuple-element.8.refs_0_, ...), custom_call_target="tpu_custom_call" | custom-call | flops 5368709120 | bytes 10485760 | tf_op jit(solution)/shard_map/pallas_call | solution.py:274
  55.2 0.6 copy-done.12
  55.8 0.6 copy-done.14
  56.4 2.4 %select_rows.1.refs_0_ = bf16[32,1024]{1,0:T(8,128)(2,1)} custom-call(s32[2]{0:T(128)} %pad_add_fusion.info_ref, s32[64]{0:T(128)} %assign_ref.3, bf16[32,1024]{1,0:T(8,128)(2,1)} %attend_decode.1.refs_0_, bf16[32,1024]{1,0:T(8,128)(2,1)} %copy-done.14, bf16[32,1024]{1,0:T(8,128)(2,1)} %copy-done.13, bf16[32,1024]{1,0:T(8,128)(2,1)} %copy-done.12, ...), custom_call_target="tpu_custom_call" | custom-call | tf_op jit(solution)/shard_map/select_rows/pallas_call | solution.py:462
  58.8 0.4 collective-permute-start.19
  59.3 0.4 collective-permute-start.17
  59.7 3.3 %collective-permute-start.16 = (bf16[32,1024]{1,0:T(8,128)(2,1)}, bf16[32,1024]{1,0:T(8,128)(2,1)S(1)}, u32[]{:S(2)}, u32[]{:S(2)}) collective-permute-start(bf16[32,1024]{1,0:T(8,128)(2,1)} %select_rows.1.refs_0_), channel_id=1, source_target_pairs={{0,16},{4,20},{8,24},{12,28},{16,0},{20,4},{24,8},{28,12},{1,17},{... | collective-permute-start | bytes 196616 | tf_op jit(solution)/shard_map/ppermute | solution.py:523
  63.2 0.6 collective-permute-done.19.refs_7_
  63.8 0.7 collective-permute-start.14
  64.5 3.2 %collective-permute-start.13 = (bf16[32,1024]{1,0:T(8,128)(2,1)}, bf16[32,1024]{1,0:T(8,128)(2,1)S(1)}, u32[]{:S(2)}, u32[]{:S(2)}) collective-permute-start(bf16[32,1024]{1,0:T(8,128)(2,1)} %select_rows.1.refs_0_), channel_id=1, source_target_pairs={{0,4},{4,8},{8,12},{12,16},{16,20},{20,24},{24,28},{28,0},{1,5},{5... | collective-permute-start | bytes 196616 | tf_op jit(solution)/shard_map/ppermute | solution.py:523
  67.7 15.1 %shard_map.114 = bf16[128,8192]{1,0:T(8,128)(2,1)} custom-call(s32[2]{0:T(128)} %pad_add_fusion.info_ref, s32[4,1024]{1,0:T(4,128)} %seg_ref.5, s32[4,1024]{1,0:T(4,128)} %seg_ref.5, bf16[8,1024,640]{2,1,0:T(8,128)(2,1)} %absorb_prefill.1.qa_hbm.refs_14_, bf16[128,640]{1,0:T(8,128)(2,1)} %get-tuple-element.8.refs_0_, ...), custom_call_target="tpu_custom_call", output_to_operand_aliasing={{}: (12, {})} | custom-call | flops 5368709120 | bytes 10485760 | tf_op jit(solution)/shard_map/pallas_call | solution.py:274
  82.9 0.6 copy-done.17
  83.6 0.6 copy-done.21
  84.2 2.6 %assemble.1 = bf16[32,8192]{1,0:T(8,128)(2,1)} custom-call(s32[2]{0:T(128)} %pad_add_fusion.info_ref, bf16[32,1024]{1,0:T(8,128)(2,1)} %select_rows.1.refs_0_, bf16[32,1024]{1,0:T(8,128)(2,1)} %copy-done.21, bf16[32,1024]{1,0:T(8,128)(2,1)} %copy-done.20, bf16[32,1024]{1,0:T(8,128)(2,1)} %copy-done.19, bf16[32,1024]{1,0:T(8,128)(2,1)} %copy-done.18, ...), custom_call_target="tpu_custom_call" | custom-call | tf_op jit(solution)/shard_map/assemble/pallas_call | solution.py:495
  (60 shorter events, 0.7 us)
Async XLA Ops:
  3.9 14.3 %collective-permute-start.2 = (bf16[128,640]{1,0:T(8,128)(2,1)}, bf16[128,640]{1,0:T(8,128)(2,1)S(1)}, u32[]{:S(2)}, u32[]{:S(2)}) collective-permute-start(bf16[128,640]{1,0:T(8,128)(2,1)} %get-tuple-element.8.refs_0_), channel_id=1, source_target_pairs={{0,24},{4,28},{8,0},{12,4},{16,8},{20,12},{24,16},{28,20},{1,25},{... | collective-permute-start | bytes 491528 | tf_op jit(solution)/shard_map/ppermute | solution.py:511
  4.0 16.1 %collective-permute-start.1 = (bf16[128,640]{1,0:T(8,128)(2,1)}, bf16[128,640]{1,0:T(8,128)(2,1)S(1)}, u32[]{:S(2)}, u32[]{:S(2)}) collective-permute-start(bf16[128,640]{1,0:T(8,128)(2,1)} %get-tuple-element.8.refs_0_), channel_id=1, source_target_pairs={{0,16},{4,20},{8,24},{12,28},{16,0},{20,4},{24,8},{28,12},{1,17},{... | collective-permute-start | bytes 491528 | tf_op jit(solution)/shard_map/ppermute | solution.py:511
  7.2 14.0 %collective-permute-start = (bf16[128,640]{1,0:T(8,128)(2,1)}, bf16[128,640]{1,0:T(8,128)(2,1)S(1)}, u32[]{:S(2)}, u32[]{:S(2)}) collective-permute-start(bf16[128,640]{1,0:T(8,128)(2,1)} %get-tuple-element.8.refs_0_), channel_id=1, source_target_pairs={{0,8},{4,12},{8,16},{12,20},{16,24},{20,28},{24,0},{28,4},{1,9},{5... | collective-permute-start | bytes 491528 | tf_op jit(solution)/shard_map/ppermute | solution.py:511
  7.2 15.2 %collective-permute-start.9 = (bf16[32,2176]{1,0:T(8,128)(2,1)}, bf16[32,2176]{1,0:T(8,128)(2,1)S(1)}, u32[]{:S(2)}, u32[]{:S(2)}) collective-permute-start(bf16[32,2176]{1,0:T(8,128)(2,1)} %get-tuple-element.13.refs_8_), channel_id=1, source_target_pairs={{0,3},{1,0},{2,1},{3,2},{4,7},{5,4},{6,5},{7,6},{8,11},{9,8},{10,9... | collective-permute-start | bytes 417800 | tf_op jit(solution)/shard_map/ppermute | solution.py:523
  9.4 13.6 %collective-permute-start.8 = (bf16[32,2176]{1,0:T(8,128)(2,1)}, bf16[32,2176]{1,0:T(8,128)(2,1)S(1)}, u32[]{:S(2)}, u32[]{:S(2)}) collective-permute-start(bf16[32,2176]{1,0:T(8,128)(2,1)} %get-tuple-element.13.refs_8_), channel_id=1, source_target_pairs={{0,2},{1,3},{2,0},{3,1},{4,6},{5,7},{6,4},{7,5},{8,10},{9,11},{10,... | collective-permute-start | bytes 417800 | tf_op jit(solution)/shard_map/ppermute | solution.py:523
  9.6 8.6 %copy-start = (bf16[128,640]{1,0:T(8,128)(2,1)S(1)}, bf16[128,640]{1,0:T(8,128)(2,1)}, u32[]{:S(2)}) copy-start(bf16[128,640]{1,0:T(8,128)(2,1)} %get-tuple-element.8.refs_0_) | copy-start | bytes 491524
  9.6 13.3 %copy-start.8 = (bf16[32,2176]{1,0:T(8,128)(2,1)S(1)}, bf16[32,2176]{1,0:T(8,128)(2,1)}, u32[]{:S(2)}) copy-start(bf16[32,2176]{1,0:T(8,128)(2,1)} %get-tuple-element.13.refs_8_) | copy-start | bytes 417796
  18.2 10.9 %copy-start.1 = (bf16[128,640]{1,0:T(8,128)(2,1)}, bf16[128,640]{1,0:T(8,128)(2,1)S(1)}, u32[]{:S(2)}) copy-start(bf16[128,640]{1,0:T(8,128)(2,1)S(1)} %collective-permute-done.2.refs_3_) | copy-start | bytes 491524
  18.2 10.9 %collective-permute-start.3 = (bf16[128,640]{1,0:T(8,128)(2,1)S(1)}, bf16[128,640]{1,0:T(8,128)(2,1)S(1)}, u32[]{:S(2)}, u32[]{:S(2)}) collective-permute-start(bf16[128,640]{1,0:T(8,128)(2,1)S(1)} %copy-done), channel_id=1, source_target_pairs={{0,4},{4,0},{8,12},{12,8},{16,20},{20,16},{24,28},{28,24},{1,5},{5... | collective-permute-start | bytes 491528 | tf_op jit(solution)/shard_map/ppermute | solution.py:518
  20.1 9.1 %copy-start.2 = (bf16[128,640]{1,0:T(8,128)(2,1)}, bf16[128,640]{1,0:T(8,128)(2,1)S(1)}, u32[]{:S(2)}) copy-start(bf16[128,640]{1,0:T(8,128)(2,1)S(1)} %collective-permute-done.1.refs_2_) | copy-start | bytes 491524
  21.2 7.9 %copy-start.3 = (bf16[128,640]{1,0:T(8,128)(2,1)}, bf16[128,640]{1,0:T(8,128)(2,1)S(1)}, u32[]{:S(2)}) copy-start(bf16[128,640]{1,0:T(8,128)(2,1)S(1)} %collective-permute-done.refs_1_) | copy-start | bytes 491524
  21.2 7.9 %collective-permute-start.4 = (bf16[128,640]{1,0:T(8,128)(2,1)S(1)}, bf16[128,640]{1,0:T(8,128)(2,1)S(1)}, u32[]{:S(2)}, u32[]{:S(2)}) collective-permute-start(bf16[128,640]{1,0:T(8,128)(2,1)S(1)} %collective-permute-done.refs_1_), channel_id=1, source_target_pairs={{0,4},{4,0},{8,12},{12,8},{16,20},{20,16},{24,28},{28,24},{1,5},{5... | collective-permute-start | bytes 491528 | tf_op jit(solution)/shard_map/ppermute | solution.py:518
  22.4 6.7 %collective-permute-start.5 = (bf16[128,640]{1,0:T(8,128)(2,1)S(1)}, bf16[128,640]{1,0:T(8,128)(2,1)S(1)}, u32[]{:S(2)}, u32[]{:S(2)}) collective-permute-start(bf16[128,640]{1,0:T(8,128)(2,1)S(1)} %collective-permute-done.1.refs_2_), channel_id=1, source_target_pairs={{0,4},{4,0},{8,12},{12,8},{16,20},{20,16},{24,28},{28,24},{1,5},{5... | collective-permute-start | bytes 491528 | tf_op jit(solution)/shard_map/ppermute | solution.py:518
  22.5 6.7 %copy-start.9 = (bf16[32,2176]{1,0:T(8,128)(2,1)}, bf16[32,2176]{1,0:T(8,128)(2,1)S(1)}, u32[]{:S(2)}) copy-start(bf16[32,2176]{1,0:T(8,128)(2,1)S(1)} %collective-permute-done.9.refs_11_) | copy-start | bytes 417796
  22.5 6.7 %collective-permute-start.6 = (bf16[128,640]{1,0:T(8,128)(2,1)S(1)}, bf16[128,640]{1,0:T(8,128)(2,1)S(1)}, u32[]{:S(2)}, u32[]{:S(2)}) collective-permute-start(bf16[128,640]{1,0:T(8,128)(2,1)S(1)} %collective-permute-done.2.refs_3_), channel_id=1, source_target_pairs={{0,4},{4,0},{8,12},{12,8},{16,20},{20,16},{24,28},{28,24},{1,5},{5... | collective-permute-start | bytes 491528 | tf_op jit(solution)/shard_map/ppermute | solution.py:518
  23.0 6.2 %copy-start.10 = (bf16[32,2176]{1,0:T(8,128)(2,1)}, bf16[32,2176]{1,0:T(8,128)(2,1)S(1)}, u32[]{:S(2)}) copy-start(bf16[32,2176]{1,0:T(8,128)(2,1)S(1)} %collective-permute-done.8.refs_10_) | copy-start | bytes 417796
  23.0 6.1 %collective-permute-start.7 = (bf16[32,2176]{1,0:T(8,128)(2,1)S(1)}, bf16[32,2176]{1,0:T(8,128)(2,1)S(1)}, u32[]{:S(2)}, u32[]{:S(2)}) collective-permute-start(bf16[32,2176]{1,0:T(8,128)(2,1)S(1)} %copy-done.8), channel_id=1, source_target_pairs={{0,1},{1,2},{2,3},{3,0},{4,5},{5,6},{6,7},{7,4},{8,9},{9,10},{10,1... | collective-permute-start | bytes 417800 | tf_op jit(solution)/shard_map/ppermute | solution.py:523
  29.1 0.7 copy-start.4
  29.1 0.8 copy-start.5
  29.1 0.8 copy-start.6
  37.1 18.1 %collective-permute-start.12 = (bf16[32,1024]{1,0:T(8,128)(2,1)}, bf16[32,1024]{1,0:T(8,128)(2,1)S(1)}, u32[]{:S(2)}, u32[]{:S(2)}) collective-permute-start(bf16[32,1024]{1,0:T(8,128)(2,1)} %attend_decode.1.refs_0_), channel_id=1, source_target_pairs={{0,3},{1,0},{2,1},{3,2},{4,7},{5,4},{6,5},{7,6},{8,11},{9,8},{10,9... | collective-permute-start | bytes 196616 | tf_op jit(solution)/shard_map/ppermute | solution.py:523
  38.4 16.8 %collective-permute-start.11 = (bf16[32,1024]{1,0:T(8,128)(2,1)}, bf16[32,1024]{1,0:T(8,128)(2,1)S(1)}, u32[]{:S(2)}, u32[]{:S(2)}) collective-permute-start(bf16[32,1024]{1,0:T(8,128)(2,1)} %attend_decode.1.refs_0_), channel_id=1, source_target_pairs={{0,2},{1,3},{2,0},{3,1},{4,6},{5,7},{6,4},{7,5},{8,10},{9,11},{10,... | collective-permute-start | bytes 196616 | tf_op jit(solution)/shard_map/ppermute | solution.py:523
  38.6 16.6 %collective-permute-start.10 = (bf16[32,1024]{1,0:T(8,128)(2,1)}, bf16[32,1024]{1,0:T(8,128)(2,1)S(1)}, u32[]{:S(2)}, u32[]{:S(2)}) collective-permute-start(bf16[32,1024]{1,0:T(8,128)(2,1)} %attend_decode.1.refs_0_), channel_id=1, source_target_pairs={{0,1},{1,2},{2,3},{3,0},{4,5},{5,6},{6,7},{7,4},{8,9},{9,10},{10,1... | collective-permute-start | bytes 196616 | tf_op jit(solution)/shard_map/ppermute | solution.py:523
  58.8 4.9 %collective-permute-start.19 = (bf16[32,1024]{1,0:T(8,128)(2,1)}, bf16[32,1024]{1,0:T(8,128)(2,1)S(1)}, u32[]{:S(2)}, u32[]{:S(2)}) collective-permute-start(bf16[32,1024]{1,0:T(8,128)(2,1)} %select_rows.1.refs_0_), channel_id=1, source_target_pairs={{0,28},{4,0},{8,4},{12,8},{16,12},{20,16},{24,20},{28,24},{1,29},{... | collective-permute-start | bytes 196616 | tf_op jit(solution)/shard_map/ppermute | solution.py:523
  59.3 5.3 %collective-permute-start.18 = (bf16[32,1024]{1,0:T(8,128)(2,1)}, bf16[32,1024]{1,0:T(8,128)(2,1)S(1)}, u32[]{:S(2)}, u32[]{:S(2)}) collective-permute-start(bf16[32,1024]{1,0:T(8,128)(2,1)} %select_rows.1.refs_0_), channel_id=1, source_target_pairs={{0,24},{4,28},{8,0},{12,4},{16,8},{20,12},{24,16},{28,20},{1,25},{... | collective-permute-start | bytes 196616 | tf_op jit(solution)/shard_map/ppermute | solution.py:523
  59.3 23.6 %collective-permute-start.17 = (bf16[32,1024]{1,0:T(8,128)(2,1)}, bf16[32,1024]{1,0:T(8,128)(2,1)S(1)}, u32[]{:S(2)}, u32[]{:S(2)}) collective-permute-start(bf16[32,1024]{1,0:T(8,128)(2,1)} %select_rows.1.refs_0_), channel_id=1, source_target_pairs={{0,20},{4,24},{8,28},{12,0},{16,4},{20,8},{24,12},{28,16},{1,21},{... | collective-permute-start | bytes 196616 | tf_op jit(solution)/shard_map/ppermute | solution.py:523
  59.7 23.2 %collective-permute-start.16 = (bf16[32,1024]{1,0:T(8,128)(2,1)}, bf16[32,1024]{1,0:T(8,128)(2,1)S(1)}, u32[]{:S(2)}, u32[]{:S(2)}) collective-permute-start(bf16[32,1024]{1,0:T(8,128)(2,1)} %select_rows.1.refs_0_), channel_id=1, source_target_pairs={{0,16},{4,20},{8,24},{12,28},{16,0},{20,4},{24,8},{28,12},{1,17},{... | collective-permute-start | bytes 196616 | tf_op jit(solution)/shard_map/ppermute | solution.py:523
  63.1 19.8 %collective-permute-start.15 = (bf16[32,1024]{1,0:T(8,128)(2,1)}, bf16[32,1024]{1,0:T(8,128)(2,1)S(1)}, u32[]{:S(2)}, u32[]{:S(2)}) collective-permute-start(bf16[32,1024]{1,0:T(8,128)(2,1)} %select_rows.1.refs_0_), channel_id=1, source_target_pairs={{0,12},{4,16},{8,20},{12,24},{16,28},{20,0},{24,4},{28,8},{1,13},{... | collective-permute-start | bytes 196616 | tf_op jit(solution)/shard_map/ppermute | solution.py:523
  63.8 19.0 %copy-start.15 = (bf16[32,1024]{1,0:T(8,128)(2,1)}, bf16[32,1024]{1,0:T(8,128)(2,1)S(1)}, u32[]{:S(2)}) copy-start(bf16[32,1024]{1,0:T(8,128)(2,1)S(1)} %collective-permute-done.19.refs_7_) | copy-start | bytes 196612
  63.8 19.1 %collective-permute-start.14 = (bf16[32,1024]{1,0:T(8,128)(2,1)}, bf16[32,1024]{1,0:T(8,128)(2,1)S(1)}, u32[]{:S(2)}, u32[]{:S(2)}) collective-permute-start(bf16[32,1024]{1,0:T(8,128)(2,1)} %select_rows.1.refs_0_), channel_id=1, source_target_pairs={{0,8},{4,12},{8,16},{12,20},{16,24},{20,28},{24,0},{28,4},{1,9},{5... | collective-permute-start | bytes 196616 | tf_op jit(solution)/shard_map/ppermute | solution.py:523
  64.5 18.3 %copy-start.16 = (bf16[32,1024]{1,0:T(8,128)(2,1)}, bf16[32,1024]{1,0:T(8,128)(2,1)S(1)}, u32[]{:S(2)}) copy-start(bf16[32,1024]{1,0:T(8,128)(2,1)S(1)} %collective-permute-done.18.refs_6_) | copy-start | bytes 196612
  64.5 18.4 %collective-permute-start.13 = (bf16[32,1024]{1,0:T(8,128)(2,1)}, bf16[32,1024]{1,0:T(8,128)(2,1)S(1)}, u32[]{:S(2)}, u32[]{:S(2)}) collective-permute-start(bf16[32,1024]{1,0:T(8,128)(2,1)} %select_rows.1.refs_0_), channel_id=1, source_target_pairs={{0,4},{4,8},{8,12},{12,16},{16,20},{20,24},{24,28},{28,0},{1,5},{5... | collective-permute-start | bytes 196616 | tf_op jit(solution)/shard_map/ppermute | solution.py:523
  (10 other events, 6.4 us)
where the time goes:
time: 87.6 us; the launch traced here: 87 us
  Pallas kernels  53 us (61%)
  starting transfers between devices  21.6 us (25%)
  waiting for transfers between devices  6.65 us (8%)
  local copies, waits for them, and re-layouts  3.92 us (4%)
  between operations  1.09 us (1%)
    pallas_call x2, Pallas kernels, attend_prefill(): pl.pallas_call(functools.partial(prefill_kernel, count=count, part=part,...  30.4 us
    ppermute x13, starting transfers between devices, spread(): lax.ppermute(value, axis, [(i, (i + k) % count) for i in range(count)])  14.7 us
    pallas_call x1, Pallas kernels, absorb_prefill(): pl.pallas_call(functools.partial(absorb_kernel, group=group), in_specs=[A...  8.54 us
    pallas_call x1, Pallas kernels, attend_decode(): pl.pallas_call(functools.partial(decode_kernel, count=count, spans=spans,...  6.49 us
    ppermute x13, waiting for transfers between devices, spread(): lax.ppermute(value, axis, [(i, (i + k) % count) for i in range(count)])  5.5 us
    unnamed x44, local copies, waits for them, and re-layouts  3.92 us
    ppermute x4, starting transfers between devices, spread_near(): return pieces + [lax.ppermute(p, 'seq', swap) for p in pieces]  3.59 us
    ppermute x3, starting transfers between devices, spread_far(): lax.ppermute(value, 'seq', [(i, (i + 2 * k) % count) for i in range(count)])  3.38 us
  transfers between devices with their start and end apart: 20, of which 3 were waited for; matrix products, arithmetic and copies ran while one was open for 0% of the time, Pallas kernels for 45%

commit v1 on v0

--- a/solution.py
+++ b/solution.py
@@ -21,10 +21,11 @@
 TOK = 16
 PARTS = 2
 CHUNK = 512
-VMEM_LIMIT = 60 << 20
+MIB = 1 << 20
 
 NT = (((1,), (1,)), ((), ()))
-ANY = pl.BlockSpec(memory_space=pltpu.HBM)
+FAR = pl.BlockSpec(memory_space=pltpu.HBM)
+ANY = pl.BlockSpec(memory_space=pl.ANY)
 
 
 def normed(values):
@@ -82,13 +83,15 @@
             out_specs=tuple(full(s) for s in out_shape),
         ),
         out_shape=out_shape,
+        compiler_params=pltpu.CompilerParams(vmem_limit_bytes=60 * MIB),
         name="prepare",
     )(info, latent, rope, q_decode, new_latent, new_rope)
 
 
-def absorb_kernel(q_hbm, ak_hbm, o_hbm, q_buf, ak_buf, o_buf, q_sem, ak_sem, o_sem, *, group):
+def absorb_kernel(q_hbm, ak_hbm, o_hbm, token_ref, q_buf, ak_buf, o_buf, q_sem, ak_sem, o_sem, *, group):
     heads, _, tokens = q_buf.shape
     number = heads // group
+    token_ref[...] = jnp.zeros_like(token_ref)
 
     def copies(i):
         part = pl.ds(i * group, group)
@@ -128,9 +131,12 @@
     shape = (tokens // TOK, heads * TOK, WIDTH)
     return pl.pallas_call(
         functools.partial(absorb_kernel, group=group),
-        in_specs=[ANY, ANY],
-        out_specs=ANY,
-        out_shape=jax.ShapeDtypeStruct(shape, jnp.bfloat16),
+        in_specs=[FAR, FAR],
+        out_specs=(FAR, pl.BlockSpec(memory_space=pltpu.VMEM)),
+        out_shape=(
+            jax.ShapeDtypeStruct(shape, jnp.bfloat16),
+            jax.ShapeDtypeStruct((8, 128), jnp.int32),
+        ),
         scratch_shapes=[
             pltpu.VMEM(q.shape, jnp.bfloat16),
             pltpu.VMEM(absorb_key.shape, jnp.bfloat16),
@@ -144,7 +150,7 @@
             bytes_accessed=2 * heads * (tokens * (size + WIDTH) + NOPE * LAT),
             transcendentals=0,
         ),
-        compiler_params=pltpu.CompilerParams(vmem_limit_bytes=VMEM_LIMIT),
+        compiler_params=pltpu.CompilerParams(vmem_limit_bytes=61 * MIB),
         name="absorb_prefill",
     )(q, absorb_key)
 
@@ -169,18 +175,21 @@
 
 
 def prefill_kernel(
-    info_ref, segs_ref, seg_ref, qa_hbm, *refs, count, part, fast, slow, heads, chunk, aliased
+    info_ref, segs_ref, seg_ref, qa_hbm, keys_hbm, *refs, part, fast, slow, heads, chunk, aliased
 ):
-    pieces = refs[:count]
-    refs = refs[count + (1 if aliased else 0) :]
-    av_hbm, o_ref, kbuf, olat, av, qa_buf, ksem, qsem, vsem = refs
+    refs = refs[1 if aliased else 0 :]
+    av_hbm, o_ref, token_ref, kbuf, olat, av, qa_buf, ksem, qsem, vsem = refs
+    token_ref[...] = jnp.zeros_like(token_ref)
     blocks, rows, _ = qa_buf.shape
     tokens = olat.shape[1]
-    length = kbuf.shape[0]
+    held = kbuf.shape[0]
+    length = keys_hbm.shape[0]
     seq_idx = info_ref[0]
     span_idx = info_ref[1]
+    low = jnp.clip((seq_idx + 1) * tokens - held, 0, length - held)
+    low = pl.multiple_of(low, TOK)
+    keys_copy = pltpu.make_async_copy(keys_hbm.at[pl.ds(low, held)], kbuf, ksem)
     av_copy = pltpu.make_async_copy(av_hbm.at[pl.ds(part * heads, heads)], av, vsem)
-    copies = gather_copies(pieces, kbuf, ksem, seq_idx)
 
     def qa_copy(i):
         return pltpu.make_async_copy(
@@ -188,17 +197,10 @@
         )
 
     ahead = min(2, blocks)
-    near = fast // tokens + 1
-    used = []
-    for i in range(count):
-        gap = seq_idx - source_of(i, seq_idx, count)
-        used.append((gap >= 0) & (gap <= near) | (seq_idx < near))
-    for copy, use in zip(copies, used):
-        pl.when(use)(copy.start)
+    keys_copy.start()
     for i in range(ahead):
         qa_copy(i).start()
-    for copy, use in zip(copies, used):
-        pl.when(use)(copy.wait)
+    keys_copy.wait()
     seg = seg_ref[pl.ds(span_idx, 1), :]
     row = lax.broadcasted_iota(jnp.int32, (TOK, 1), 0)
 
@@ -224,9 +226,10 @@
             pos_k = begin + lax.broadcasted_iota(jnp.int32, (TOK, window), 1)
             keep = (pos_k >= start) & (pos_k <= base + row)
             bias = jnp.where(keep, 0.0, NEG)[None]
+            spot = pl.multiple_of(begin - low, TOK)
             for c in range(0, heads * TOK, chunk):
                 q = qa_buf[tb, pl.ds(c, chunk), :]
-                keys = kbuf[pl.ds(begin, window), :]
+                keys = kbuf[pl.ds(spot, window), :]
                 s = lax.dot_general(q, keys, NT, preferred_element_type=jnp.float32)
                 s = (s.reshape(chunk // TOK, TOK, window) + bias).reshape(chunk, window)
                 m = jnp.max(s, axis=1, keepdims=True)
@@ -234,7 +237,7 @@
                 den = jnp.sum(p, axis=1, keepdims=True)
                 o = jnp.dot(
                     p.astype(jnp.bfloat16),
-                    kbuf[pl.ds(begin, window), :LAT],
+                    kbuf[pl.ds(spot, window), :LAT],
                     preferred_element_type=jnp.float32,
                 )
                 o = (o * (1.0 / den)).astype(jnp.bfloat16)
@@ -261,20 +264,18 @@
         o_ref[:, h * VHEAD : (h + 1) * VHEAD] = r.astype(jnp.bfloat16)
 
 
-def attend_prefill(info, segment_ids, qa, pieces, absorb_value, part, parts, most, out=None):
+def attend_prefill(info, segment_ids, qa, keys, absorb_value, part, parts, most, out=None):
     blocks, rows, _ = qa.shape
     tokens = blocks * TOK
     heads = rows // TOK // parts
-    count = len(pieces)
-    length = count * tokens
+    length = keys.shape[0]
     fast = min(most, length)
     slow = min(most + 128, length)
     aliased = out is not None
-    args = [info, segment_ids, segment_ids, qa, *pieces, *([out] if aliased else []), absorb_value]
+    args = [info, segment_ids, segment_ids, qa, keys, *([out] if aliased else []), absorb_value]
     return pl.pallas_call(
         functools.partial(
             prefill_kernel,
-            count=count,
             part=part,
             fast=fast,
             slow=slow,
@@ -287,34 +288,42 @@
             grid=(1,),
             in_specs=[
                 pl.BlockSpec(segment_ids.shape, lambda i, *_: (0, 0)),
-                *([ANY] * (count + aliased + 2)),
+                *([FAR] * (aliased + 3)),
             ],
-            out_specs=pl.BlockSpec((tokens, heads * VHEAD), lambda i, *_: (0, part)),
+            out_specs=(
+                pl.BlockSpec((tokens, heads * VHEAD), lambda i, *_: (0, part)),
+                pl.BlockSpec((8, 128), lambda i, *_: (0, 0)),
+            ),
             scratch_shapes=[
-                pltpu.VMEM((length, WIDTH), jnp.bfloat16),
+                pltpu.VMEM((min(slow + tokens, length), WIDTH), jnp.bfloat16),
                 pltpu.VMEM((heads, tokens, LAT), jnp.bfloat16),
                 pltpu.VMEM((heads, LAT, VHEAD), jnp.bfloat16),
                 pltpu.VMEM((blocks, heads * TOK, WIDTH), jnp.bfloat16),
-                pltpu.SemaphoreType.DMA((count,)),
+                pltpu.SemaphoreType.DMA,
                 pltpu.SemaphoreType.DMA((blocks,)),
                 pltpu.SemaphoreType.DMA,
             ],
         ),
-        out_shape=jax.ShapeDtypeStruct((tokens, parts * heads * VHEAD), jnp.bfloat16),
-        input_output_aliases={4 + count: 0} if aliased else {},
+        out_shape=(
+            jax.ShapeDtypeStruct((tokens, parts * heads * VHEAD), jnp.bfloat16),
+            jax.ShapeDtypeStruct((8, 128), jnp.int32),
+        ),
+        input_output_aliases={5: 0} if aliased else {},
         cost_estimate=pl.CostEstimate(
             flops=2 * tokens * heads * (fast * (WIDTH + LAT) + LAT * VHEAD),
             bytes_accessed=2 * heads * (tokens * (WIDTH + VHEAD) + LAT * VHEAD),
             transcendentals=tokens * heads * fast,
         ),
-        compiler_params=pltpu.CompilerParams(vmem_limit_bytes=VMEM_LIMIT),
+        compiler_params=pltpu.CompilerParams(vmem_limit_bytes=61 * MIB),
     )(*args)
 
 
 def decode_kernel(info_ref, assign_ref, seg_ref, *refs, count, spans, docs, steps, group):
     pieces = refs[:count]
     packs = refs[count : count + spans]
-    ak_hbm, av_hbm, _, o_ref, kbuf, qa, pack_ref, ak_ref, av_ref, ksem, sems = refs[count + spans :]
+    ak_hbm, av_hbm, o_ref, keys_hbm, kbuf, qa, pack_ref, ak_ref, av_ref, ksem, sems = refs[
+        count + spans :
+    ]
     seq_idx = info_ref[0]
     span_idx = info_ref[1]
     near = steps * docs
@@ -360,6 +369,8 @@
         qa[pl.ds(h * near, near), LAT:] = jnp.concatenate([part, jnp.zeros_like(part)], axis=1)
     for copy in copies:
         copy.wait()
+    handed = pltpu.make_async_copy(kbuf, keys_hbm, sems.at[spans + 2])
+    handed.start()
     keys = kbuf[...]
     seg = seg_ref[pl.ds(span_idx, 1), :]
     old_bias = jnp.where(seg == lax.rem(row, docs), 0.0, NEG)[None]
@@ -385,9 +396,10 @@
         )
         r = jnp.dot(both, av_ref[h], preferred_element_type=jnp.float32)
         o_ref[:, h * VHEAD : (h + 1) * VHEAD] = (r[:near] + r[near:]).astype(jnp.bfloat16)
-
-
-def attend_decode(info, assignment, segment_ids, pieces, packs, absorb_key, absorb_value, after, steps):
+    handed.wait()
+
+
+def attend_decode(info, assignment, segment_ids, pieces, packs, absorb_key, absorb_value, steps):
     near, size = packs[0].shape
     docs = near // steps
     count, spans = len(pieces), len(packs)
@@ -405,9 +417,10 @@
             grid=(1,),
             in_specs=[
                 pl.BlockSpec(segment_ids.shape, lambda i, *_: (0, 0)),
-                *([ANY] * (count + spans + 3)),
+                *([ANY] * (count + spans)),
+                *([FAR] * 2),
             ],
-            out_specs=pl.BlockSpec((near, group * VHEAD), lambda i, *_: (0, 0)),
+            out_specs=(pl.BlockSpec((near, group * VHEAD), lambda i, *_: (0, 0)), FAR),
             scratch_shapes=[
                 pltpu.VMEM((length, WIDTH), jnp.bfloat16),
                 pltpu.VMEM((rows, WIDTH), jnp.bfloat16),
@@ -415,23 +428,26 @@
                 pltpu.VMEM((group, NOPE, LAT), jnp.bfloat16),
                 pltpu.VMEM((group, LAT, VHEAD), jnp.bfloat16),
                 pltpu.SemaphoreType.DMA((count,)),
-                pltpu.SemaphoreType.DMA((spans + 2,)),
+                pltpu.SemaphoreType.DMA((spans + 3,)),
             ],
         ),
-        out_shape=jax.ShapeDtypeStruct((near, group * VHEAD), jnp.bfloat16),
+        out_shape=(
+            jax.ShapeDtypeStruct((near, group * VHEAD), jnp.bfloat16),
+            jax.ShapeDtypeStruct((length, WIDTH), jnp.bfloat16),
+        ),
         cost_estimate=pl.CostEstimate(
             flops=2 * rows * length * (WIDTH + LAT),
             bytes_accessed=2 * (length * WIDTH + group * LAT * VHEAD * 2),
             transcendentals=rows * length,
         ),
-        compiler_params=pltpu.CompilerParams(vmem_limit_bytes=VMEM_LIMIT),
+        compiler_params=pltpu.CompilerParams(vmem_limit_bytes=55 * MIB),
         name="attend_decode",
-    )(info, assignment, segment_ids, *pieces, *packs, absorb_key, absorb_value, after)
+    )(info, assignment, segment_ids, *pieces, *packs, absorb_key, absorb_value)
 
 
 def select_kernel(info_ref, assign_ref, *refs, spans, docs, steps):
     parts = refs[:spans]
-    o_ref, value, sems = refs[spans + 1 :]
+    o_ref, value, sems = refs[spans:]
     span_idx = info_ref[1]
     near = steps * docs
     copies = [
@@ -456,7 +472,7 @@
     o_ref[...] = jnp.dot(pick, value[...], preferred_element_type=jnp.float32).astype(jnp.bfloat16)
 
 
-def select_rows(info, assignment, parts, after, steps):
+def select_rows(info, assignment, parts, steps):
     near, size = parts[0].shape
     spans = len(parts)
     return pl.pallas_call(
@@ -464,7 +480,7 @@
         grid_spec=pltpu.PrefetchScalarGridSpec(
             num_scalar_prefetch=2,
             grid=(1,),
-            in_specs=[ANY] * (spans + 1),
+            in_specs=[ANY] * spans,
             out_specs=pl.BlockSpec((near, size), lambda i, *_: (0, 0)),
             scratch_shapes=[
                 pltpu.VMEM((spans * near, size), jnp.bfloat16),
@@ -472,8 +488,9 @@
             ],
         ),
         out_shape=jax.ShapeDtypeStruct((near, size), jnp.bfloat16),
+        compiler_params=pltpu.CompilerParams(vmem_limit_bytes=8 * MIB),
         name="select_rows",
-    )(info, assignment, *parts, after)
+    )(info, assignment, *parts)
 
 
 def assemble_kernel(info_ref, *refs):
@@ -502,6 +519,7 @@
             scratch_shapes=[pltpu.SemaphoreType.DMA((len(parts),))],
         ),
         out_shape=jax.ShapeDtypeStruct(shape, jnp.bfloat16),
+        compiler_params=pltpu.CompilerParams(vmem_limit_bytes=8 * MIB),
         name="assemble",
     )(info, *parts)
 
@@ -549,18 +567,21 @@
     )
     pieces = spread_far(cache, count)
     packs = spread(pack, "span", spans)
-    qa = absorb_prefill(q_prefill[0].transpose(1, 2, 0), absorb_key)
-    far, qa = lax.optimization_barrier((pieces[1:], qa))
+    qa, token = absorb_prefill(q_prefill[0].transpose(1, 2, 0), absorb_key)
+    far, token = lax.optimization_barrier((pieces[1:], token))
     pieces = spread_near([cache, *far], count)
-    decoded = attend_decode(
-        info, assignment, segment_ids, pieces, packs, absorb_key, absorb_value, qa, steps
+    decoded, keys = attend_decode(
+        info, assignment, segment_ids, pieces, packs, absorb_key, absorb_value, steps
     )
     returned = spread(decoded, "span", spans)
-    out = attend_prefill(info, segment_ids, qa, pieces, absorb_value, 0, PARTS, most)
-    chosen = select_rows(info, assignment, returned, out, steps)
+    out, token = attend_prefill(info, segment_ids, qa, keys, absorb_value, 0, PARTS, most)
+    late, _ = lax.optimization_barrier((info, token))
+    chosen = select_rows(late, assignment, returned, steps)
     finals = spread(chosen, "seq", count)
     for part in range(1, PARTS):
-        out = attend_prefill(info, segment_ids, qa, pieces, absorb_value, part, PARTS, most, out)
+        out, _ = attend_prefill(
+            info, segment_ids, qa, keys, absorb_value, part, PARTS, most, out
+        )
     decode_out = assemble(info, finals)
     return (out[None], decode_out.reshape(steps, docs, heads * VHEAD))
 

time: 87.6 us -> 90.6 us (1.034)
  the two profiles are of different devices: /device:TPU:17 before, /device:TPU:0 now
where the time goes in v1:
time: 90.6 us; the launch traced here: 90 us
  Pallas kernels  48.6 us (54%)
  starting transfers between devices  28 us (31%)
  waiting for transfers between devices  10.5 us (12%)
  local copies, waits for them, and re-layouts  1.45 us (2%)
    pallas_call x2, Pallas kernels, attend_prefill(): pl.pallas_call(functools.partial(prefill_kernel, part=part, fast=fast, sl...  27.6 us
    ppermute x13, starting transfers between devices, spread(): lax.ppermute(value, axis, [(i, (i + k) % count) for i in range(count)])  20.4 us
    pallas_call x1, Pallas kernels, absorb_prefill(): pl.pallas_call(functools.partial(absorb_kernel, group=group), in_specs=[F...  9.12 us
    ppermute x3, starting transfers between devices, spread_far(): lax.ppermute(value, 'seq', [(i, (i + 2 * k) % count) for i in range(count)])  6.99 us
    ppermute x3, waiting for transfers between devices, spread_far(): lax.ppermute(value, 'seq', [(i, (i + 2 * k) % count) for i in range(count)])  6.59 us
    pallas_call x1, Pallas kernels, attend_decode(): pl.pallas_call(functools.partial(decode_kernel, count=count, spans=spans,...  6.51 us
    ppermute x13, waiting for transfers between devices, spread(): lax.ppermute(value, axis, [(i, (i + k) % count) for i in range(count)])  3.88 us
    pallas_call x1, Pallas kernels, prepare(): pl.pallas_call(functools.partial(prepare_kernel, group=group), grid_spec=...  2.55 us
  transfers between devices with their start and end apart: 20, of which 3 were waited for; matrix products, arithmetic and copies ran while one was open for 0% of the time, Pallas kernels for 41%

profile of v1, /device:TPU:0, one launch (start us, length us, event | category | flops | bytes accessed | tf_op | source)
XLA Modules:
  0.0 90.0 jit_solution(8629270571212070570)
XLA Ops:
  0.6 0.6 pad_add_fusion.info_ref
  1.2 2.6 %prepare.1 = (bf16[128,640]{1,0:T(8,128)(2,1)}, bf16[32,2176]{1,0:T(8,128)(2,1)}) custom-call(s32[2]{0:T(128)} %pad_add_fusion.info_ref, bf16[128,512]{1,0:T(8,128)(2,1)} %bitcast.14, bf16[64,128]{1,0:T(8,128)(2,1)} %bitcast.15, bf16[2,16,64,192]{3,2,1,0:T(8,128)(2,1)} %q_ref.1, bf16[2,16,512]{2,1,0:T(8,128)(2,1)} %nl_ref.1, bf16[2,16,64]{2,1,0:T(8,128)(2,1)} %nr_ref.1), custom_call_target="tpu_custom_call" | custom-call | tf_op jit(solution)/shard_map/prepare/pallas_call | solution.py:71
  3.7 3.1 %collective-permute-start = (bf16[128,640]{1,0:T(8,128)(2,1)}, bf16[128,640]{1,0:T(8,128)(2,1)S(1)}, u32[]{:S(2)}, u32[]{:S(2)}) collective-permute-start(bf16[128,640]{1,0:T(8,128)(2,1)} %get-tuple-element.13.refs_0_), channel_id=1, source_target_pairs={{0,8},{4,12},{8,16},{12,20},{16,24},{20,28},{24,0},{28,4},{1,9},{5... | collective-permute-start | bytes 491528 | tf_op jit(solution)/shard_map/ppermute | solution.py:529
  6.8 2.6 %collective-permute-start.1 = (bf16[128,640]{1,0:T(8,128)(2,1)}, bf16[128,640]{1,0:T(8,128)(2,1)S(1)}, u32[]{:S(2)}, u32[]{:S(2)}) collective-permute-start(bf16[128,640]{1,0:T(8,128)(2,1)} %get-tuple-element.13.refs_0_), channel_id=1, source_target_pairs={{0,16},{4,20},{8,24},{12,28},{16,0},{20,4},{24,8},{28,12},{1,17},{... | collective-permute-start | bytes 491528 | tf_op jit(solution)/shard_map/ppermute | solution.py:529
  9.4 1.3 %collective-permute-start.2 = (bf16[128,640]{1,0:T(8,128)(2,1)}, bf16[128,640]{1,0:T(8,128)(2,1)S(1)}, u32[]{:S(2)}, u32[]{:S(2)}) collective-permute-start(bf16[128,640]{1,0:T(8,128)(2,1)} %get-tuple-element.13.refs_0_), channel_id=1, source_target_pairs={{0,24},{4,28},{8,0},{12,4},{16,8},{20,12},{24,16},{28,20},{1,25},{... | collective-permute-start | bytes 491528 | tf_op jit(solution)/shard_map/ppermute | solution.py:529
  10.7 1.5 %collective-permute-start.7 = (bf16[32,2176]{1,0:T(8,128)(2,1)}, bf16[32,2176]{1,0:T(8,128)(2,1)S(1)}, u32[]{:S(2)}, u32[]{:S(2)}) collective-permute-start(bf16[32,2176]{1,0:T(8,128)(2,1)} %get-tuple-element.17.refs_8_), channel_id=1, source_target_pairs={{0,1},{1,2},{2,3},{3,0},{4,5},{5,6},{6,7},{7,4},{8,9},{9,10},{10,1... | collective-permute-start | bytes 417800 | tf_op jit(solution)/shard_map/ppermute | solution.py:541
  12.2 1.5 %collective-permute-start.8 = (bf16[32,2176]{1,0:T(8,128)(2,1)}, bf16[32,2176]{1,0:T(8,128)(2,1)S(1)}, u32[]{:S(2)}, u32[]{:S(2)}) collective-permute-start(bf16[32,2176]{1,0:T(8,128)(2,1)} %get-tuple-element.17.refs_8_), channel_id=1, source_target_pairs={{0,2},{1,3},{2,0},{3,1},{4,6},{5,7},{6,4},{7,5},{8,10},{9,11},{10,... | collective-permute-start | bytes 417800 | tf_op jit(solution)/shard_map/ppermute | solution.py:541
  13.7 0.4 collective-permute-done.refs_1_
  14.2 6.2 %collective-permute-done.1.refs_2_ = bf16[128,640]{1,0:T(8,128)(2,1)S(1)} collective-permute-done((bf16[128,640]{1,0:T(8,128)(2,1)}, bf16[128,640]{1,0:T(8,128)(2,1)S(1)}, u32[]{:S(2)}, u32[]{:S(2)}) %collective-permute-start.1) | collective-permute-done | bytes 163872 | tf_op jit(solution)/shard_map/ppermute | solution.py:529
  20.4 0.5 collective-permute-start.5
  20.9 0.1 collective-permute-start.6
  21.0 2.4 %collective-permute-start.9 = (bf16[32,2176]{1,0:T(8,128)(2,1)}, bf16[32,2176]{1,0:T(8,128)(2,1)S(1)}, u32[]{:S(2)}, u32[]{:S(2)}) collective-permute-start(bf16[32,2176]{1,0:T(8,128)(2,1)} %get-tuple-element.17.refs_8_), channel_id=1, source_target_pairs={{0,3},{1,0},{2,1},{3,2},{4,7},{5,4},{6,5},{7,6},{8,11},{9,8},{10,9... | collective-permute-start | bytes 417800 | tf_op jit(solution)/shard_map/ppermute | solution.py:541
  23.5 3.8 %collective-permute-done.9.refs_11_ = bf16[32,2176]{1,0:T(8,128)(2,1)S(1)} collective-permute-done((bf16[32,2176]{1,0:T(8,128)(2,1)}, bf16[32,2176]{1,0:T(8,128)(2,1)S(1)}, u32[]{:S(2)}, u32[]{:S(2)}) %collective-permute-start.9) | collective-permute-done | bytes 139296 | tf_op jit(solution)/shard_map/ppermute | solution.py:541
  27.4 0.5 copy-done.13
  28.0 0.1 copy-done.7
  28.0 0.1 copy-done.8
  28.1 0.7 copy-done.10
  28.8 6.5 %attend_decode.1 = (bf16[32,1024]{1,0:T(8,128)(2,1)}, bf16[1024,640]{1,0:T(8,128)(2,1)}) custom-call(s32[2]{0:T(128)} %pad_add_fusion.info_ref, s32[64]{0:T(128)} %assign_ref.3, s32[4,1024]{1,0:T(4,128)} %seg_ref.5, bf16[128,640]{1,0:T(8,128)(2,1)} %get-tuple-element.13.refs_0_, bf16[128,640]{1,0:T(8,128)(2,1)} %copy-done.4, bf16[128,640]{1,0:T(8,128)(2,1)} %copy-done.5, ...), custom_call_target="tpu_custom_call" | custom-call | flops 603979776 | bytes 3407872 | tf_op jit(solution)/shard_map/attend_decode/pallas_call | solution.py:411
  35.3 2.4 %collective-permute-start.10 = (bf16[32,1024]{1,0:T(8,128)(2,1)}, bf16[32,1024]{1,0:T(8,128)(2,1)S(1)}, u32[]{:S(2)}, u32[]{:S(2)}) collective-permute-start(bf16[32,1024]{1,0:T(8,128)(2,1)} %get-tuple-element.21.refs_0_), channel_id=1, source_target_pairs={{0,1},{1,2},{2,3},{3,0},{4,5},{5,6},{6,7},{7,4},{8,9},{9,10},{10,1... | collective-permute-start | bytes 196616 | tf_op jit(solution)/shard_map/ppermute | solution.py:541
  37.7 1.5 %collective-permute-start.11 = (bf16[32,1024]{1,0:T(8,128)(2,1)}, bf16[32,1024]{1,0:T(8,128)(2,1)S(1)}, u32[]{:S(2)}, u32[]{:S(2)}) collective-permute-start(bf16[32,1024]{1,0:T(8,128)(2,1)} %get-tuple-element.21.refs_0_), channel_id=1, source_target_pairs={{0,2},{1,3},{2,0},{3,1},{4,6},{5,7},{6,4},{7,5},{8,10},{9,11},{10,... | collective-permute-start | bytes 196616 | tf_op jit(solution)/shard_map/ppermute | solution.py:541
  39.2 0.5 collective-permute-start.12
  39.8 9.1 %absorb_prefill.1 = (bf16[8,1024,640]{2,1,0:T(8,128)(2,1)}, s32[8,128]{1,0:T(8,128)}) custom-call(bf16[64,192,128]{2,1,0:T(8,128)(2,1)} %bitcast.11, bf16[64,128,512]{2,1,0:T(8,128)(2,1)} %refs_12_.1), custom_call_target="tpu_custom_call" | custom-call | flops 1073741824 | bytes 22020096 | tf_op jit(solution)/shard_map/absorb_prefill/pallas_call | solution.py:132
  48.9 1.2 %select_rows.1.refs_0_ = bf16[32,1024]{1,0:T(8,128)(2,1)S(1)} custom-call(s32[2]{0:T(128)S(1)} %copy-done.1, s32[64]{0:T(128)S(1)} %copy-done.3, bf16[32,1024]{1,0:T(8,128)(2,1)S(1)} %copy-done, bf16[32,1024]{1,0:T(8,128)(2,1)S(1)} %collective-permute-done.10.refs_1_, bf16[32,1024]{1,0:T(8,128)(2,1)S(1)} %collective-permute-done.11.refs_2_, ...), custom_call_target="tpu_custom_call" | custom-call | tf_op jit(solution)/shard_map/select_rows/pallas_call | solution.py:478
  50.2 4.0 %collective-permute-start.14 = (bf16[32,1024]{1,0:T(8,128)(2,1)S(1)}, bf16[32,1024]{1,0:T(8,128)(2,1)S(1)}, u32[]{:S(2)}, u32[]{:S(2)}) collective-permute-start(bf16[32,1024]{1,0:T(8,128)(2,1)S(1)} %select_rows.1.refs_0_), channel_id=1, source_target_pairs={{0,8},{4,12},{8,16},{12,20},{16,24},{20,28},{24,0},{28,4},{1,9},{5... | collective-permute-start | bytes 196616 | tf_op jit(solution)/shard_map/ppermute | solution.py:541
  54.2 13.8 %shard_map.113 = (bf16[128,8192]{1,0:T(8,128)(2,1)}, s32[8,128]{1,0:T(8,128)}) custom-call(s32[2]{0:T(128)} %pad_add_fusion.info_ref, s32[4,1024]{1,0:T(4,128)} %seg_ref.5, s32[4,1024]{1,0:T(4,128)} %seg_ref.5, bf16[8,1024,640]{2,1,0:T(8,128)(2,1)} %get-tuple-element.12.qa_hbm, bf16[1024,640]{1,0:T(8,128)(2,1)} %get-tuple-element.18.keys_hbm, ...), custom_call_target="tpu_custom_call" | custom-call | flops 5368709120 | bytes 10485760 | tf_op jit(solution)/shard_map/pallas_call | solution.py:276
  67.9 1.7 %collective-permute-start.15 = (bf16[32,1024]{1,0:T(8,128)(2,1)S(1)}, bf16[32,1024]{1,0:T(8,128)(2,1)S(1)}, u32[]{:S(2)}, u32[]{:S(2)}) collective-permute-start(bf16[32,1024]{1,0:T(8,128)(2,1)S(1)} %select_rows.1.refs_0_), channel_id=1, source_target_pairs={{0,12},{4,16},{8,20},{12,24},{16,28},{20,0},{24,4},{28,8},{1,13},{... | collective-permute-start | bytes 196616 | tf_op jit(solution)/shard_map/ppermute | solution.py:541
  69.6 2.2 %collective-permute-start.16 = (bf16[32,1024]{1,0:T(8,128)(2,1)S(1)}, bf16[32,1024]{1,0:T(8,128)(2,1)S(1)}, u32[]{:S(2)}, u32[]{:S(2)}) collective-permute-start(bf16[32,1024]{1,0:T(8,128)(2,1)S(1)} %select_rows.1.refs_0_), channel_id=1, source_target_pairs={{0,16},{4,20},{8,24},{12,28},{16,0},{20,4},{24,8},{28,12},{1,17},{... | collective-permute-start | bytes 196616 | tf_op jit(solution)/shard_map/ppermute | solution.py:541
  71.8 0.3 collective-permute-start.17
  72.1 1.9 %collective-permute-start.18 = (bf16[32,1024]{1,0:T(8,128)(2,1)S(1)}, bf16[32,1024]{1,0:T(8,128)(2,1)S(1)}, u32[]{:S(2)}, u32[]{:S(2)}) collective-permute-start(bf16[32,1024]{1,0:T(8,128)(2,1)S(1)} %select_rows.1.refs_0_), channel_id=1, source_target_pairs={{0,24},{4,28},{8,0},{12,4},{16,8},{20,12},{24,16},{28,20},{1,25},{... | collective-permute-start | bytes 196616 | tf_op jit(solution)/shard_map/ppermute | solution.py:541
  73.9 0.5 collective-permute-start.19
  74.4 13.9 %shard_map.114 = (bf16[128,8192]{1,0:T(8,128)(2,1)}, s32[8,128]{1,0:T(8,128)}) custom-call(s32[2]{0:T(128)} %pad_add_fusion.info_ref, s32[4,1024]{1,0:T(4,128)} %seg_ref.5, s32[4,1024]{1,0:T(4,128)} %seg_ref.5, bf16[8,1024,640]{2,1,0:T(8,128)(2,1)} %get-tuple-element.12.qa_hbm, ...), custom_call_target="tpu_custom_call", output_to_operand_aliasing={{0}: (5, {})} | custom-call | flops 5368709120 | bytes 10485760 | tf_op jit(solution)/shard_map/pallas_call | solution.py:276
  88.4 1.6 %assemble.1 = bf16[32,8192]{1,0:T(8,128)(2,1)} custom-call(s32[2]{0:T(128)S(1)} %copy-done.2, bf16[32,1024]{1,0:T(8,128)(2,1)S(1)} %select_rows.1.refs_0_, bf16[32,1024]{1,0:T(8,128)(2,1)S(1)} %collective-permute-done.13.refs_1_, bf16[32,1024]{1,0:T(8,128)(2,1)S(1)} %collective-permute-done.14.refs_2_, bf16[32,1024]{1,0:T(8,128)(2,1)S(1)} %collective-permute-done.15.refs_3_, ...), custom_call_target="tpu_custom_call" | custom-call | tf_op jit(solution)/shard_map/assemble/pallas_call | solution.py:512
  (44 shorter events, 0.3 us)
Async XLA Ops:
  3.7 10.4 %collective-permute-start = (bf16[128,640]{1,0:T(8,128)(2,1)}, bf16[128,640]{1,0:T(8,128)(2,1)S(1)}, u32[]{:S(2)}, u32[]{:S(2)}) collective-permute-start(bf16[128,640]{1,0:T(8,128)(2,1)} %get-tuple-element.13.refs_0_), channel_id=1, source_target_pairs={{0,8},{4,12},{8,16},{12,20},{16,24},{20,28},{24,0},{28,4},{1,9},{5... | collective-permute-start | bytes 491528 | tf_op jit(solution)/shard_map/ppermute | solution.py:529
  6.8 13.5 %collective-permute-start.1 = (bf16[128,640]{1,0:T(8,128)(2,1)}, bf16[128,640]{1,0:T(8,128)(2,1)S(1)}, u32[]{:S(2)}, u32[]{:S(2)}) collective-permute-start(bf16[128,640]{1,0:T(8,128)(2,1)} %get-tuple-element.13.refs_0_), channel_id=1, source_target_pairs={{0,16},{4,20},{8,24},{12,28},{16,0},{20,4},{24,8},{28,12},{1,17},{... | collective-permute-start | bytes 491528 | tf_op jit(solution)/shard_map/ppermute | solution.py:529
  9.4 11.0 %collective-permute-start.2 = (bf16[128,640]{1,0:T(8,128)(2,1)}, bf16[128,640]{1,0:T(8,128)(2,1)S(1)}, u32[]{:S(2)}, u32[]{:S(2)}) collective-permute-start(bf16[128,640]{1,0:T(8,128)(2,1)} %get-tuple-element.13.refs_0_), channel_id=1, source_target_pairs={{0,24},{4,28},{8,0},{12,4},{16,8},{20,12},{24,16},{28,20},{1,25},{... | collective-permute-start | bytes 491528 | tf_op jit(solution)/shard_map/ppermute | solution.py:529
  10.7 10.2 %collective-permute-start.7 = (bf16[32,2176]{1,0:T(8,128)(2,1)}, bf16[32,2176]{1,0:T(8,128)(2,1)S(1)}, u32[]{:S(2)}, u32[]{:S(2)}) collective-permute-start(bf16[32,2176]{1,0:T(8,128)(2,1)} %get-tuple-element.17.refs_8_), channel_id=1, source_target_pairs={{0,1},{1,2},{2,3},{3,0},{4,5},{5,6},{6,7},{7,4},{8,9},{9,10},{10,1... | collective-permute-start | bytes 417800 | tf_op jit(solution)/shard_map/ppermute | solution.py:541
  12.2 8.8 %collective-permute-start.8 = (bf16[32,2176]{1,0:T(8,128)(2,1)}, bf16[32,2176]{1,0:T(8,128)(2,1)S(1)}, u32[]{:S(2)}, u32[]{:S(2)}) collective-permute-start(bf16[32,2176]{1,0:T(8,128)(2,1)} %get-tuple-element.17.refs_8_), channel_id=1, source_target_pairs={{0,2},{1,3},{2,0},{3,1},{4,6},{5,7},{6,4},{7,5},{8,10},{9,11},{10,... | collective-permute-start | bytes 417800 | tf_op jit(solution)/shard_map/ppermute | solution.py:541
  14.2 13.2 %copy-start.4 = (bf16[128,640]{1,0:T(8,128)(2,1)}, bf16[128,640]{1,0:T(8,128)(2,1)S(1)}, u32[]{:S(2)}) copy-start(bf16[128,640]{1,0:T(8,128)(2,1)S(1)} %collective-permute-done.refs_1_) | copy-start | bytes 491524
  14.2 13.1 %collective-permute-start.3 = (bf16[128,640]{1,0:T(8,128)(2,1)}, bf16[128,640]{1,0:T(8,128)(2,1)S(1)}, u32[]{:S(2)}, u32[]{:S(2)}) collective-permute-start(bf16[128,640]{1,0:T(8,128)(2,1)} %get-tuple-element.13.refs_0_), channel_id=1, source_target_pairs={{0,4},{4,0},{8,12},{12,8},{16,20},{20,16},{24,28},{28,24},{1,5},{5... | collective-permute-start | bytes 491528 | tf_op jit(solution)/shard_map/ppermute | solution.py:536
  20.3 7.0 %copy-start.5 = (bf16[128,640]{1,0:T(8,128)(2,1)}, bf16[128,640]{1,0:T(8,128)(2,1)S(1)}, u32[]{:S(2)}) copy-start(bf16[128,640]{1,0:T(8,128)(2,1)S(1)} %collective-permute-done.1.refs_2_) | copy-start | bytes 491524
  20.3 7.0 %copy-start.6 = (bf16[128,640]{1,0:T(8,128)(2,1)}, bf16[128,640]{1,0:T(8,128)(2,1)S(1)}, u32[]{:S(2)}) copy-start(bf16[128,640]{1,0:T(8,128)(2,1)S(1)} %collective-permute-done.2.refs_3_) | copy-start | bytes 491524
  20.3 7.0 %collective-permute-start.4 = (bf16[128,640]{1,0:T(8,128)(2,1)S(1)}, bf16[128,640]{1,0:T(8,128)(2,1)S(1)}, u32[]{:S(2)}, u32[]{:S(2)}) collective-permute-start(bf16[128,640]{1,0:T(8,128)(2,1)S(1)} %collective-permute-done.refs_1_), channel_id=1, source_target_pairs={{0,4},{4,0},{8,12},{12,8},{16,20},{20,16},{24,28},{28,24},{1,5},{5... | collective-permute-start | bytes 491528 | tf_op jit(solution)/shard_map/ppermute | solution.py:536
  20.4 6.9 %collective-permute-start.5 = (bf16[128,640]{1,0:T(8,128)(2,1)S(1)}, bf16[128,640]{1,0:T(8,128)(2,1)S(1)}, u32[]{:S(2)}, u32[]{:S(2)}) collective-permute-start(bf16[128,640]{1,0:T(8,128)(2,1)S(1)} %collective-permute-done.1.refs_2_), channel_id=1, source_target_pairs={{0,4},{4,0},{8,12},{12,8},{16,20},{20,16},{24,28},{28,24},{1,5},{5... | collective-permute-start | bytes 491528 | tf_op jit(solution)/shard_map/ppermute | solution.py:536
  20.9 6.5 %copy-start.11 = (bf16[32,2176]{1,0:T(8,128)(2,1)}, bf16[32,2176]{1,0:T(8,128)(2,1)S(1)}, u32[]{:S(2)}) copy-start(bf16[32,2176]{1,0:T(8,128)(2,1)S(1)} %collective-permute-done.7.refs_9_) | copy-start | bytes 417796
  20.9 6.4 %collective-permute-start.6 = (bf16[128,640]{1,0:T(8,128)(2,1)S(1)}, bf16[128,640]{1,0:T(8,128)(2,1)S(1)}, u32[]{:S(2)}, u32[]{:S(2)}) collective-permute-start(bf16[128,640]{1,0:T(8,128)(2,1)S(1)} %collective-permute-done.2.refs_3_), channel_id=1, source_target_pairs={{0,4},{4,0},{8,12},{12,8},{16,20},{20,16},{24,28},{28,24},{1,5},{5... | collective-permute-start | bytes 491528 | tf_op jit(solution)/shard_map/ppermute | solution.py:536
  21.0 6.4 %copy-start.12 = (bf16[32,2176]{1,0:T(8,128)(2,1)}, bf16[32,2176]{1,0:T(8,128)(2,1)S(1)}, u32[]{:S(2)}) copy-start(bf16[32,2176]{1,0:T(8,128)(2,1)S(1)} %collective-permute-done.8.refs_10_) | copy-start | bytes 417796
  21.0 6.3 %collective-permute-start.9 = (bf16[32,2176]{1,0:T(8,128)(2,1)}, bf16[32,2176]{1,0:T(8,128)(2,1)S(1)}, u32[]{:S(2)}, u32[]{:S(2)}) collective-permute-start(bf16[32,2176]{1,0:T(8,128)(2,1)} %get-tuple-element.17.refs_8_), channel_id=1, source_target_pairs={{0,3},{1,0},{2,1},{3,2},{4,7},{5,4},{6,5},{7,6},{8,11},{9,8},{10,9... | collective-permute-start | bytes 417800 | tf_op jit(solution)/shard_map/ppermute | solution.py:541
  27.3 0.7 copy-start.7
  27.3 0.8 copy-start.8
  27.3 0.8 copy-start.9
  35.3 13.6 %collective-permute-start.10 = (bf16[32,1024]{1,0:T(8,128)(2,1)}, bf16[32,1024]{1,0:T(8,128)(2,1)S(1)}, u32[]{:S(2)}, u32[]{:S(2)}) collective-permute-start(bf16[32,1024]{1,0:T(8,128)(2,1)} %get-tuple-element.21.refs_0_), channel_id=1, source_target_pairs={{0,1},{1,2},{2,3},{3,0},{4,5},{5,6},{6,7},{7,4},{8,9},{9,10},{10,1... | collective-permute-start | bytes 196616 | tf_op jit(solution)/shard_map/ppermute | solution.py:541
  37.7 11.2 %collective-permute-start.11 = (bf16[32,1024]{1,0:T(8,128)(2,1)}, bf16[32,1024]{1,0:T(8,128)(2,1)S(1)}, u32[]{:S(2)}, u32[]{:S(2)}) collective-permute-start(bf16[32,1024]{1,0:T(8,128)(2,1)} %get-tuple-element.21.refs_0_), channel_id=1, source_target_pairs={{0,2},{1,3},{2,0},{3,1},{4,6},{5,7},{6,4},{7,5},{8,10},{9,11},{10,... | collective-permute-start | bytes 196616 | tf_op jit(solution)/shard_map/ppermute | solution.py:541
  39.2 9.7 %collective-permute-start.12 = (bf16[32,1024]{1,0:T(8,128)(2,1)}, bf16[32,1024]{1,0:T(8,128)(2,1)S(1)}, u32[]{:S(2)}, u32[]{:S(2)}) collective-permute-start(bf16[32,1024]{1,0:T(8,128)(2,1)} %get-tuple-element.21.refs_0_), channel_id=1, source_target_pairs={{0,3},{1,0},{2,1},{3,2},{4,7},{5,4},{6,5},{7,6},{8,11},{9,8},{10,9... | collective-permute-start | bytes 196616 | tf_op jit(solution)/shard_map/ppermute | solution.py:541
  39.8 9.2 %copy-start = (bf16[32,1024]{1,0:T(8,128)(2,1)S(1)}, bf16[32,1024]{1,0:T(8,128)(2,1)}, u32[]{:S(2)}) copy-start(bf16[32,1024]{1,0:T(8,128)(2,1)} %get-tuple-element.21.refs_0_) | copy-start | bytes 196612
  39.8 9.2 %copy-start.1 = (s32[2]{0:T(128)S(1)}, s32[2]{0:T(128)}, u32[]{:S(2)}) copy-start(s32[2]{0:T(128)} %pad_add_fusion.info_ref) | copy-start | bytes 28
  39.8 9.2 %copy-start.3 = (s32[64]{0:T(128)S(1)}, s32[64]{0:T(128)}, u32[]{:S(2)}) copy-start(s32[64]{0:T(128)} %assign_ref.3) | copy-start | bytes 772
  50.1 21.9 %collective-permute-start.13 = (bf16[32,1024]{1,0:T(8,128)(2,1)S(1)}, bf16[32,1024]{1,0:T(8,128)(2,1)S(1)}, u32[]{:S(2)}, u32[]{:S(2)}) collective-permute-start(bf16[32,1024]{1,0:T(8,128)(2,1)S(1)} %select_rows.1.refs_0_), channel_id=1, source_target_pairs={{0,4},{4,8},{8,12},{12,16},{16,20},{20,24},{24,28},{28,0},{1,5},{5... | collective-permute-start | bytes 196616 | tf_op jit(solution)/shard_map/ppermute | solution.py:541
  50.2 23.7 %collective-permute-start.14 = (bf16[32,1024]{1,0:T(8,128)(2,1)S(1)}, bf16[32,1024]{1,0:T(8,128)(2,1)S(1)}, u32[]{:S(2)}, u32[]{:S(2)}) collective-permute-start(bf16[32,1024]{1,0:T(8,128)(2,1)S(1)} %select_rows.1.refs_0_), channel_id=1, source_target_pairs={{0,8},{4,12},{8,16},{12,20},{16,24},{20,28},{24,0},{28,4},{1,9},{5... | collective-permute-start | bytes 196616 | tf_op jit(solution)/shard_map/ppermute | solution.py:541
  67.9 20.4 %collective-permute-start.15 = (bf16[32,1024]{1,0:T(8,128)(2,1)S(1)}, bf16[32,1024]{1,0:T(8,128)(2,1)S(1)}, u32[]{:S(2)}, u32[]{:S(2)}) collective-permute-start(bf16[32,1024]{1,0:T(8,128)(2,1)S(1)} %select_rows.1.refs_0_), channel_id=1, source_target_pairs={{0,12},{4,16},{8,20},{12,24},{16,28},{20,0},{24,4},{28,8},{1,13},{... | collective-permute-start | bytes 196616 | tf_op jit(solution)/shard_map/ppermute | solution.py:541
  69.6 18.7 %collective-permute-start.16 = (bf16[32,1024]{1,0:T(8,128)(2,1)S(1)}, bf16[32,1024]{1,0:T(8,128)(2,1)S(1)}, u32[]{:S(2)}, u32[]{:S(2)}) collective-permute-start(bf16[32,1024]{1,0:T(8,128)(2,1)S(1)} %select_rows.1.refs_0_), channel_id=1, source_target_pairs={{0,16},{4,20},{8,24},{12,28},{16,0},{20,4},{24,8},{28,12},{1,17},{... | collective-permute-start | bytes 196616 | tf_op jit(solution)/shard_map/ppermute | solution.py:541
  71.8 16.6 %collective-permute-start.17 = (bf16[32,1024]{1,0:T(8,128)(2,1)S(1)}, bf16[32,1024]{1,0:T(8,128)(2,1)S(1)}, u32[]{:S(2)}, u32[]{:S(2)}) collective-permute-start(bf16[32,1024]{1,0:T(8,128)(2,1)S(1)} %select_rows.1.refs_0_), channel_id=1, source_target_pairs={{0,20},{4,24},{8,28},{12,0},{16,4},{20,8},{24,12},{28,16},{1,21},{... | collective-permute-start | bytes 196616 | tf_op jit(solution)/shard_map/ppermute | solution.py:541
  72.1 16.3 %collective-permute-start.18 = (bf16[32,1024]{1,0:T(8,128)(2,1)S(1)}, bf16[32,1024]{1,0:T(8,128)(2,1)S(1)}, u32[]{:S(2)}, u32[]{:S(2)}) collective-permute-start(bf16[32,1024]{1,0:T(8,128)(2,1)S(1)} %select_rows.1.refs_0_), channel_id=1, source_target_pairs={{0,24},{4,28},{8,0},{12,4},{16,8},{20,12},{24,16},{28,20},{1,25},{... | collective-permute-start | bytes 196616 | tf_op jit(solution)/shard_map/ppermute | solution.py:541
  73.9 14.4 %collective-permute-start.19 = (bf16[32,1024]{1,0:T(8,128)(2,1)S(1)}, bf16[32,1024]{1,0:T(8,128)(2,1)S(1)}, u32[]{:S(2)}, u32[]{:S(2)}) collective-permute-start(bf16[32,1024]{1,0:T(8,128)(2,1)S(1)} %select_rows.1.refs_0_), channel_id=1, source_target_pairs={{0,28},{4,0},{8,4},{12,8},{16,12},{20,16},{24,20},{28,24},{1,29},{... | collective-permute-start | bytes 196616 | tf_op jit(solution)/shard_map/ppermute | solution.py:541
  74.4 14.0 %copy-start.2 = (s32[2]{0:T(128)S(1)}, s32[2]{0:T(128)}, u32[]{:S(2)}) copy-start(s32[2]{0:T(128)} %pad_add_fusion.info_ref) | copy-start | bytes 28
  (2 other events, 1.3 us)

commit v2 on v1

--- a/solution.py
+++ b/solution.py
@@ -20,7 +20,8 @@
 SCALE2 = (NOPE + ROPE) ** (-0.5) * math.log2(math.e)
 TOK = 16
 PARTS = 2
-CHUNK = 512
+GROUP = 2
+OUTS = 4
 MIB = 1 << 20
 
 NT = (((1,), (1,)), ((), ()))
@@ -88,10 +89,9 @@
     )(info, latent, rope, q_decode, new_latent, new_rope)
 
 
-def absorb_kernel(q_hbm, ak_hbm, o_hbm, token_ref, q_buf, ak_buf, o_buf, q_sem, ak_sem, o_sem, *, group):
+def absorb_kernel(q_hbm, ak_hbm, o_hbm, q_buf, ak_buf, o_buf, q_sem, ak_sem, o_sem, *, group):
     heads, _, tokens = q_buf.shape
     number = heads // group
-    token_ref[...] = jnp.zeros_like(token_ref)
 
     def copies(i):
         part = pl.ds(i * group, group)
@@ -132,11 +132,8 @@
     return pl.pallas_call(
         functools.partial(absorb_kernel, group=group),
         in_specs=[FAR, FAR],
-        out_specs=(FAR, pl.BlockSpec(memory_space=pltpu.VMEM)),
-        out_shape=(
-            jax.ShapeDtypeStruct(shape, jnp.bfloat16),
-            jax.ShapeDtypeStruct((8, 128), jnp.int32),
-        ),
+        out_specs=FAR,
+        out_shape=jax.ShapeDtypeStruct(shape, jnp.bfloat16),
         scratch_shapes=[
             pltpu.VMEM(q.shape, jnp.bfloat16),
             pltpu.VMEM(absorb_key.shape, jnp.bfloat16),
@@ -161,10 +158,6 @@
     return lax.rem(origin - 2 * (i % half) + count, count)
 
 
-def direct_source(i, seq_idx, count):
-    return lax.rem(seq_idx - i + count, count)
-
-
 def gather_copies(pieces, kbuf, sems, seq_idx):
     rows = pieces[0].shape[0]
     copies = []
@@ -175,11 +168,10 @@
 
 
 def prefill_kernel(
-    info_ref, segs_ref, seg_ref, qa_hbm, keys_hbm, *refs, part, fast, slow, heads, chunk, aliased
+    info_ref, segs_ref, seg_hbm, qa_hbm, keys_hbm, *refs, part, fast, slow, heads, aliased
 ):
     refs = refs[1 if aliased else 0 :]
-    av_hbm, o_ref, token_ref, kbuf, olat, av, qa_buf, ksem, qsem, vsem = refs
-    token_ref[...] = jnp.zeros_like(token_ref)
+    av_hbm, o_hbm, kbuf, olat, av, qa_buf, seg_buf, o_buf, ksem, qsem, vsem, ssem, osem = refs
     blocks, rows, _ = qa_buf.shape
     tokens = olat.shape[1]
     held = kbuf.shape[0]
@@ -196,29 +188,25 @@
             qa_hbm.at[i, pl.ds(part * rows, rows)], qa_buf.at[i], qsem.at[i]
         )
 
-    ahead = min(2, blocks)
+    ahead = min(2 * GROUP, blocks)
+    seg_copy = pltpu.make_async_copy(seg_hbm, seg_buf, ssem)
+    seg_copy.start()
     keys_copy.start()
     for i in range(ahead):
         qa_copy(i).start()
+    seg_copy.wait()
     keys_copy.wait()
-    seg = seg_ref[pl.ds(span_idx, 1), :]
+    seg = seg_buf[pl.ds(span_idx, 1), :]
     row = lax.broadcasted_iota(jnp.int32, (TOK, 1), 0)
 
-    @pl.loop(0, blocks)
-    def _(tb):
-        base = seq_idx * tokens + tb * TOK
-        qa_copy(tb).wait()
-
-        @pl.when(tb + ahead < blocks)
-        def _():
-            qa_copy(tb + ahead).start()
-
-        @pl.when(tb == blocks // 2)
-        def _():
-            av_copy.start()
-
-        def attend(window, begin, chunk):
-            begin = pl.multiple_of(begin, TOK)
+    def base_of(tb):
+        return seq_idx * tokens + tb * TOK
+
+    def attend(window, tbs):
+        staged = []
+        for tb in tbs:
+            base = base_of(tb)
+            begin = jnp.clip(base + TOK - window, 0, length - window)
             seg_q = jnp.zeros((TOK, 1), jnp.int32)
             for i in range(TOK):
                 seg_q = jnp.where(row == i, segs_ref[span_idx, base + i], seg_q)
@@ -226,42 +214,68 @@
             pos_k = begin + lax.broadcasted_iota(jnp.int32, (TOK, window), 1)
             keep = (pos_k >= start) & (pos_k <= base + row)
             bias = jnp.where(keep, 0.0, NEG)[None]
-            spot = pl.multiple_of(begin - low, TOK)
-            for c in range(0, heads * TOK, chunk):
-                q = qa_buf[tb, pl.ds(c, chunk), :]
-                keys = kbuf[pl.ds(spot, window), :]
-                s = lax.dot_general(q, keys, NT, preferred_element_type=jnp.float32)
-                s = (s.reshape(chunk // TOK, TOK, window) + bias).reshape(chunk, window)
-                m = jnp.max(s, axis=1, keepdims=True)
-                p = jnp.exp2((s - m) * SCALE2)
-                den = jnp.sum(p, axis=1, keepdims=True)
-                o = jnp.dot(
-                    p.astype(jnp.bfloat16),
-                    kbuf[pl.ds(spot, window), :LAT],
-                    preferred_element_type=jnp.float32,
-                )
-                o = (o * (1.0 / den)).astype(jnp.bfloat16)
-                place = pl.ds(pl.multiple_of(tb * TOK, TOK), TOK)
-                olat[pl.ds(c // TOK, chunk // TOK), place, :] = o.reshape(chunk // TOK, TOK, LAT)
-
-        fast_begin = jnp.clip(base + TOK - fast, 0, length - fast)
-        slow_begin = jnp.clip(base + TOK - slow, 0, length - slow)
-
-        ahead_seg = segs_ref[span_idx, jnp.maximum(fast_begin - 1, 0)]
-        reaches = (fast_begin > 0) & (ahead_seg == segs_ref[span_idx, base])
-
-        @pl.when(jnp.logical_not(reaches))
+            spot = pl.ds(pl.multiple_of(begin - low, TOK), window)
+            s = lax.dot_general(qa_buf[tb], kbuf[spot, :], NT, preferred_element_type=jnp.float32)
+            staged.append((tb, spot, bias, s))
+        for tb, spot, bias, s in staged:
+            s = (s.reshape(heads, TOK, window) + bias).reshape(rows, window)
+            m = jnp.max(s, axis=1, keepdims=True)
+            p = jnp.exp2((s - m) * SCALE2)
+            den = jnp.sum(p, axis=1, keepdims=True)
+            o = jnp.dot(
+                p.astype(jnp.bfloat16), kbuf[spot, :LAT], preferred_element_type=jnp.float32
+            )
+            o = (o * (1.0 / den)).astype(jnp.bfloat16)
+            place = pl.ds(pl.multiple_of(tb * TOK, TOK), TOK)
+            olat[:, place, :] = o.reshape(heads, TOK, LAT)
+
+    def reaches(tb):
+        begin = jnp.clip(base_of(tb) + TOK - fast, 0, length - fast)
+        ahead_seg = segs_ref[span_idx, jnp.maximum(begin - 1, 0)]
+        return (begin > 0) & (ahead_seg == segs_ref[span_idx, base_of(tb)])
+
+    @pl.loop(0, blocks // GROUP)
+    def _(step):
+        tbs = [step * GROUP + k for k in range(GROUP)]
+        for tb in tbs:
+            qa_copy(tb).wait()
+
+            @pl.when(tb + ahead < blocks)
+            def _():
+                qa_copy(tb + ahead).start()
+
+        @pl.when(step == blocks // GROUP // 2)
         def _():
-            attend(fast, fast_begin, chunk)
-
-        @pl.when(reaches)
+            av_copy.start()
+
+        far = [reaches(tb) for tb in tbs]
+        any_far = functools.reduce(jnp.logical_or, far)
+
+        @pl.when(jnp.logical_not(any_far))
         def _():
-            attend(slow, slow_begin, 128)
+            attend(fast, tbs)
+
+        @pl.when(any_far)
+        def _():
+            @pl.loop(0, GROUP)
+            def _(k):
+                attend(slow, [step * GROUP + k])
 
     av_copy.wait()
-    for h in range(heads):
-        r = jnp.dot(olat[h], av[h], preferred_element_type=jnp.float32)
-        o_ref[:, h * VHEAD : (h + 1) * VHEAD] = r.astype(jnp.bfloat16)
+    batch = heads // OUTS
+    results = []
+    for i in range(OUTS):
+        for h in range(i * batch, (i + 1) * batch):
+            r = jnp.dot(olat[h], av[h], preferred_element_type=jnp.float32)
+            o_buf[:, h * VHEAD : (h + 1) * VHEAD] = r.astype(jnp.bfloat16)
+        source = pl.ds(i * batch * VHEAD, batch * VHEAD)
+        target = pl.ds((part * heads + i * batch) * VHEAD, batch * VHEAD)
+        results.append(
+            pltpu.make_async_copy(o_buf.at[:, source], o_hbm.at[:, target], osem.at[i])
+        )
+        results[-1].start()
+    for result in results:
+        result.wait()
 
 
 def attend_prefill(info, segment_ids, qa, keys, absorb_value, part, parts, most, out=None):
@@ -280,34 +294,30 @@
             fast=fast,
             slow=slow,
             heads=heads,
-            chunk=CHUNK,
             aliased=aliased,
         ),
         grid_spec=pltpu.PrefetchScalarGridSpec(
             num_scalar_prefetch=2,
             grid=(1,),
             in_specs=[
-                pl.BlockSpec(segment_ids.shape, lambda i, *_: (0, 0)),
-                *([FAR] * (aliased + 3)),
+                *([FAR] * (aliased + 4)),
             ],
-            out_specs=(
-                pl.BlockSpec((tokens, heads * VHEAD), lambda i, *_: (0, part)),
-                pl.BlockSpec((8, 128), lambda i, *_: (0, 0)),
-            ),
+            out_specs=FAR,
             scratch_shapes=[
                 pltpu.VMEM((min(slow + tokens, length), WIDTH), jnp.bfloat16),
                 pltpu.VMEM((heads, tokens, LAT), jnp.bfloat16),
                 pltpu.VMEM((heads, LAT, VHEAD), jnp.bfloat16),
                 pltpu.VMEM((blocks, heads * TOK, WIDTH), jnp.bfloat16),
+                pltpu.VMEM(segment_ids.shape, jnp.int32),
+                pltpu.VMEM((tokens, heads * VHEAD), jnp.bfloat16),
                 pltpu.SemaphoreType.DMA,
                 pltpu.SemaphoreType.DMA((blocks,)),
                 pltpu.SemaphoreType.DMA,
+                pltpu.SemaphoreType.DMA,
+                pltpu.SemaphoreType.DMA((OUTS,)),
             ],
         ),
-        out_shape=(
-            jax.ShapeDtypeStruct((tokens, parts * heads * VHEAD), jnp.bfloat16),
-            jax.ShapeDtypeStruct((8, 128), jnp.int32),
-        ),
+        out_shape=jax.ShapeDtypeStruct((tokens, parts * heads * VHEAD), jnp.bfloat16),
         input_output_aliases={5: 0} if aliased else {},
         cost_estimate=pl.CostEstimate(
             flops=2 * tokens * heads * (fast * (WIDTH + LAT) + LAT * VHEAD),
@@ -318,10 +328,10 @@
     )(*args)
 
 
-def decode_kernel(info_ref, assign_ref, seg_ref, *refs, count, spans, docs, steps, group):
+def decode_kernel(info_ref, assign_ref, seg_hbm, *refs, count, spans, docs, steps, group):
     pieces = refs[:count]
     packs = refs[count : count + spans]
-    ak_hbm, av_hbm, o_ref, keys_hbm, kbuf, qa, pack_ref, ak_ref, av_ref, ksem, sems = refs[
+    ak_hbm, av_hbm, o_ref, keys_hbm, kbuf, qa, pack_ref, ak_ref, av_ref, seg_ref, ksem, sems = refs[
         count + spans :
     ]
     seq_idx = info_ref[0]
@@ -335,6 +345,7 @@
         for i, pack in enumerate(packs)
     ]
     early.append(pltpu.make_async_copy(ak_hbm.at[own], ak_ref, sems.at[spans]))
+    early.append(pltpu.make_async_copy(seg_hbm, seg_ref, sems.at[spans + 3]))
     late = pltpu.make_async_copy(av_hbm.at[own], av_ref, sems.at[spans + 1])
     for copy in (*early, *copies, late):
         copy.start()
@@ -416,7 +427,7 @@
             num_scalar_prefetch=2,
             grid=(1,),
             in_specs=[
-                pl.BlockSpec(segment_ids.shape, lambda i, *_: (0, 0)),
+                FAR,
                 *([ANY] * (count + spans)),
                 *([FAR] * 2),
             ],
@@ -427,8 +438,9 @@
                 pltpu.VMEM((spans * near, size), jnp.bfloat16),
                 pltpu.VMEM((group, NOPE, LAT), jnp.bfloat16),
                 pltpu.VMEM((group, LAT, VHEAD), jnp.bfloat16),
+                pltpu.VMEM(segment_ids.shape, jnp.int32),
                 pltpu.SemaphoreType.DMA((count,)),
-                pltpu.SemaphoreType.DMA((spans + 3,)),
+                pltpu.SemaphoreType.DMA((spans + 4,)),
             ],
         ),
         out_shape=(
@@ -495,11 +507,23 @@
 
 def assemble_kernel(info_ref, *refs):
     parts, o_ref, sems = refs[:-2], refs[-2], refs[-1]
-    _, size = parts[0].shape
+    near = parts[0].shape[0] // 2
+    size = parts[0].shape[1]
+    seq_idx = info_ref[0]
+    core = lax.rem(seq_idx, 2)
     copies = []
     for i, part in enumerate(parts):
-        start = pl.multiple_of(direct_source(i, info_ref[0], len(parts)) * size, 128)
-        copies.append(pltpu.make_async_copy(part, o_ref.at[:, pl.ds(start, size)], sems.at[i]))
+        source = lax.rem(seq_idx - 2 * i + 2 * len(parts), 2 * len(parts))
+        for k in range(2):
+            owner = source if k == 0 else source + 1 - 2 * core
+            start = pl.multiple_of(owner * size, 128)
+            copies.append(
+                pltpu.make_async_copy(
+                    part.at[pl.ds(k * near, near)],
+                    o_ref.at[:, pl.ds(start, size)],
+                    sems.at[2 * i + k],
+                )
+            )
     for copy in copies:
         copy.start()
     for copy in copies:
@@ -508,7 +532,8 @@
 
 def assemble(info, parts):
     near, size = parts[0].shape
-    shape = (near, len(parts) * size)
+    number = 2 * len(parts)
+    shape = (near // 2, number * size)
     return pl.pallas_call(
         assemble_kernel,
         grid_spec=pltpu.PrefetchScalarGridSpec(
@@ -516,7 +541,7 @@
             grid=(1,),
             in_specs=[ANY] * len(parts),
             out_specs=pl.BlockSpec(shape, lambda i, info: (0, 0)),
-            scratch_shapes=[pltpu.SemaphoreType.DMA((len(parts),))],
+            scratch_shapes=[pltpu.SemaphoreType.DMA((number,))],
         ),
         out_shape=jax.ShapeDtypeStruct(shape, jnp.bfloat16),
         compiler_params=pltpu.CompilerParams(vmem_limit_bytes=8 * MIB),
@@ -567,21 +592,19 @@
     )
     pieces = spread_far(cache, count)
     packs = spread(pack, "span", spans)
-    qa, token = absorb_prefill(q_prefill[0].transpose(1, 2, 0), absorb_key)
-    far, token = lax.optimization_barrier((pieces[1:], token))
-    pieces = spread_near([cache, *far], count)
+    qa = absorb_prefill(q_prefill[0].transpose(1, 2, 0), absorb_key)
+    pieces = spread_near(pieces, count)
     decoded, keys = attend_decode(
         info, assignment, segment_ids, pieces, packs, absorb_key, absorb_value, steps
     )
     returned = spread(decoded, "span", spans)
-    out, token = attend_prefill(info, segment_ids, qa, keys, absorb_value, 0, PARTS, most)
-    late, _ = lax.optimization_barrier((info, token))
-    chosen = select_rows(late, assignment, returned, steps)
-    finals = spread(chosen, "seq", count)
+    out = attend_prefill(info, segment_ids, qa, keys, absorb_value, 0, PARTS, most)
+    chosen = select_rows(info, assignment, returned, steps)
+    swapped = lax.ppermute(chosen, "seq", [(i, i ^ 1) for i in range(count)])
+    both = jnp.concatenate([chosen, swapped], axis=0)
+    finals = spread_far(both, count)
     for part in range(1, PARTS):
-        out, _ = attend_prefill(
-            info, segment_ids, qa, keys, absorb_value, part, PARTS, most, out
-        )
+        out = attend_prefill(info, segment_ids, qa, keys, absorb_value, part, PARTS, most, out)
     decode_out = assemble(info, finals)
     return (out[None], decode_out.reshape(steps, docs, heads * VHEAD))
 

time: 90.6 us -> 80.2 us (0.89)
  Pallas kernels: 48.6 us -> 42.7 us
  starting transfers between devices: 28 us -> 24.3 us
    ppermute x13 -> x6, starting transfers between devices: 20.4 us -> 9.88 us  [spread(): lax.ppermute(value, axis, [(i, (i + k) % count) for i in range(count)])]
    ppermute x3 -> x6, starting transfers between devices: 6.99 us -> 13.4 us  [spread_far(): lax.ppermute(value, 'seq', [(i, (i + 2 * k) % count) for i in range(count)])]
    pallas_call x2, Pallas kernels: 27.6 us -> 23.1 us  [attend_prefill(): pl.pallas_call(functools.partial(prefill_kernel, part=part, fast=fast, sl...]
    ppermute x3 -> x6, waiting for transfers between devices: 6.59 us -> 2.93 us  [spread_far(): lax.ppermute(value, 'seq', [(i, (i + 2 * k) % count) for i in range(count)])]
    ppermute x13 -> x6, waiting for transfers between devices: 3.88 us -> 6.66 us  [spread(): lax.ppermute(value, axis, [(i, (i + k) % count) for i in range(count)])]
  transfers between devices with their start and end apart: 20 -> 17, of which waited for: 3 -> 3; matrix products, arithmetic and copies ran while one was open for 0% -> 0% of each run, Pallas kernels for 41% -> 40%
where the time goes in v2:
time: 80.2 us; the launch traced here: 79.7 us
  Pallas kernels  42.7 us (53%)
  starting transfers between devices  24.3 us (30%)
  waiting for transfers between devices  9.6 us (12%)
  local copies, waits for them, and re-layouts  1.46 us (2%)
  between operations  1.06 us (1%)
    pallas_call x2, Pallas kernels, attend_prefill(): pl.pallas_call(functools.partial(prefill_kernel, part=part, fast=fast, sl...  23.1 us
    ppermute x6, starting transfers between devices, spread_far(): lax.ppermute(value, 'seq', [(i, (i + 2 * k) % count) for i in range(count)])  13.4 us
    ppermute x6, starting transfers between devices, spread(): lax.ppermute(value, axis, [(i, (i + k) % count) for i in range(count)])  9.88 us
    pallas_call x1, Pallas kernels, absorb_prefill(): pl.pallas_call(functools.partial(absorb_kernel, group=group), in_specs=[F...  8.53 us
    ppermute x6, waiting for transfers between devices, spread(): lax.ppermute(value, axis, [(i, (i + k) % count) for i in range(count)])  6.66 us
    pallas_call x1, Pallas kernels, attend_decode(): pl.pallas_call(functools.partial(decode_kernel, count=count, spans=spans,...  5.8 us
    ppermute x6, waiting for transfers between devices, spread_far(): lax.ppermute(value, 'seq', [(i, (i + 2 * k) % count) for i in range(count)])  2.93 us
    pallas_call x1, Pallas kernels, prepare(): pl.pallas_call(functools.partial(prepare_kernel, group=group), grid_spec=...  2.54 us
  transfers between devices with their start and end apart: 17, of which 3 were waited for; matrix products, arithmetic and copies ran while one was open for 0% of the time, Pallas kernels for 40%

profile of v2, /device:TPU:0, one launch (start us, length us, event | category | flops | bytes accessed | tf_op | source)
XLA Modules:
  0.0 79.7 jit_solution(3255882380551186978)
XLA Ops:
  0.6 0.6 pad_add_fusion.info_ref
  1.2 2.5 %prepare.1 = (bf16[128,640]{1,0:T(8,128)(2,1)}, bf16[32,2176]{1,0:T(8,128)(2,1)}) custom-call(s32[2]{0:T(128)} %pad_add_fusion.info_ref, bf16[128,512]{1,0:T(8,128)(2,1)} %bitcast.14, bf16[64,128]{1,0:T(8,128)(2,1)} %bitcast.15, bf16[2,16,64,192]{3,2,1,0:T(8,128)(2,1)} %q_ref.1, bf16[2,16,512]{2,1,0:T(8,128)(2,1)} %nl_ref.1, bf16[2,16,64]{2,1,0:T(8,128)(2,1)} %nr_ref.1), custom_call_target="tpu_custom_call" | custom-call | tf_op jit(solution)/shard_map/prepare/pallas_call | solution.py:72
  3.7 3.1 %collective-permute-start = (bf16[128,640]{1,0:T(8,128)(2,1)}, bf16[128,640]{1,0:T(8,128)(2,1)S(1)}, u32[]{:S(2)}, u32[]{:S(2)}) collective-permute-start(bf16[128,640]{1,0:T(8,128)(2,1)} %get-tuple-element.6.refs_0_), channel_id=1, source_target_pairs={{0,8},{4,12},{8,16},{12,20},{16,24},{20,28},{24,0},{28,4},{1,9},{5... | collective-permute-start | bytes 491528 | tf_op jit(solution)/shard_map/ppermute | solution.py:554
  6.8 2.6 %collective-permute-start.1 = (bf16[128,640]{1,0:T(8,128)(2,1)}, bf16[128,640]{1,0:T(8,128)(2,1)S(1)}, u32[]{:S(2)}, u32[]{:S(2)}) collective-permute-start(bf16[128,640]{1,0:T(8,128)(2,1)} %get-tuple-element.6.refs_0_), channel_id=1, source_target_pairs={{0,16},{4,20},{8,24},{12,28},{16,0},{20,4},{24,8},{28,12},{1,17},{... | collective-permute-start | bytes 491528 | tf_op jit(solution)/shard_map/ppermute | solution.py:554
  9.4 1.3 %collective-permute-start.2 = (bf16[128,640]{1,0:T(8,128)(2,1)}, bf16[128,640]{1,0:T(8,128)(2,1)S(1)}, u32[]{:S(2)}, u32[]{:S(2)}) collective-permute-start(bf16[128,640]{1,0:T(8,128)(2,1)} %get-tuple-element.6.refs_0_), channel_id=1, source_target_pairs={{0,24},{4,28},{8,0},{12,4},{16,8},{20,12},{24,16},{28,20},{1,25},{... | collective-permute-start | bytes 491528 | tf_op jit(solution)/shard_map/ppermute | solution.py:554
  10.7 1.5 %collective-permute-start.7 = (bf16[32,2176]{1,0:T(8,128)(2,1)}, bf16[32,2176]{1,0:T(8,128)(2,1)S(1)}, u32[]{:S(2)}, u32[]{:S(2)}) collective-permute-start(bf16[32,2176]{1,0:T(8,128)(2,1)} %get-tuple-element.7.refs_8_), channel_id=1, source_target_pairs={{0,1},{1,2},{2,3},{3,0},{4,5},{5,6},{6,7},{7,4},{8,9},{9,10},{10,1... | collective-permute-start | bytes 417800 | tf_op jit(solution)/shard_map/ppermute | solution.py:566
  12.2 1.5 %collective-permute-start.8 = (bf16[32,2176]{1,0:T(8,128)(2,1)}, bf16[32,2176]{1,0:T(8,128)(2,1)S(1)}, u32[]{:S(2)}, u32[]{:S(2)}) collective-permute-start(bf16[32,2176]{1,0:T(8,128)(2,1)} %get-tuple-element.7.refs_8_), channel_id=1, source_target_pairs={{0,2},{1,3},{2,0},{3,1},{4,6},{5,7},{6,4},{7,5},{8,10},{9,11},{10,... | collective-permute-start | bytes 417800 | tf_op jit(solution)/shard_map/ppermute | solution.py:566
  13.7 3.2 %collective-permute-done.7.refs_9_ = bf16[32,2176]{1,0:T(8,128)(2,1)S(1)} collective-permute-done((bf16[32,2176]{1,0:T(8,128)(2,1)}, bf16[32,2176]{1,0:T(8,128)(2,1)S(1)}, u32[]{:S(2)}, u32[]{:S(2)}) %collective-permute-start.7) | collective-permute-done | bytes 139296 | tf_op jit(solution)/shard_map/ppermute | solution.py:566
  16.9 0.0 copy-start.4
  16.9 0.5 collective-permute-start.4
  17.4 2.9 %collective-permute-done.1.refs_2_ = bf16[128,640]{1,0:T(8,128)(2,1)S(1)} collective-permute-done((bf16[128,640]{1,0:T(8,128)(2,1)}, bf16[128,640]{1,0:T(8,128)(2,1)S(1)}, u32[]{:S(2)}, u32[]{:S(2)}) %collective-permute-start.1) | collective-permute-done | bytes 163872 | tf_op jit(solution)/shard_map/ppermute | solution.py:554
  20.4 0.5 collective-permute-start.6
  20.9 2.4 %collective-permute-start.9 = (bf16[32,2176]{1,0:T(8,128)(2,1)}, bf16[32,2176]{1,0:T(8,128)(2,1)S(1)}, u32[]{:S(2)}, u32[]{:S(2)}) collective-permute-start(bf16[32,2176]{1,0:T(8,128)(2,1)} %get-tuple-element.7.refs_8_), channel_id=1, source_target_pairs={{0,3},{1,0},{2,1},{3,2},{4,7},{5,4},{6,5},{7,6},{8,11},{9,8},{10,9... | collective-permute-start | bytes 417800 | tf_op jit(solution)/shard_map/ppermute | solution.py:566
  23.3 3.5 %collective-permute-done.9.refs_11_ = bf16[32,2176]{1,0:T(8,128)(2,1)S(1)} collective-permute-done((bf16[32,2176]{1,0:T(8,128)(2,1)}, bf16[32,2176]{1,0:T(8,128)(2,1)S(1)}, u32[]{:S(2)}, u32[]{:S(2)}) %collective-permute-start.9) | collective-permute-done | bytes 139296 | tf_op jit(solution)/shard_map/ppermute | solution.py:566
  26.9 0.6 copy-done.13
  27.5 0.1 copy-done.7
  27.5 0.0 copy-done.8
  27.6 0.1 copy-done.9
  27.6 0.7 copy-done.10
  28.3 5.8 %attend_decode.1 = (bf16[32,1024]{1,0:T(8,128)(2,1)}, bf16[1024,640]{1,0:T(8,128)(2,1)}) custom-call(s32[2]{0:T(128)} %pad_add_fusion.info_ref, s32[64]{0:T(128)} %assign_ref.3, s32[4,1024]{1,0:T(4,128)} %seg_hbm.5, bf16[128,640]{1,0:T(8,128)(2,1)} %get-tuple-element.6.refs_0_, bf16[128,640]{1,0:T(8,128)(2,1)} %copy-done.4, bf16[128,640]{1,0:T(8,128)(2,1)} %copy-done.5, ...), custom_call_target="tpu_custom_call" | custom-call | flops 603979776 | bytes 3407872 | tf_op jit(solution)/shard_map/attend_decode/pallas_call | solution.py:422
  34.1 2.4 %collective-permute-start.10 = (bf16[32,1024]{1,0:T(8,128)(2,1)}, bf16[32,1024]{1,0:T(8,128)(2,1)S(1)}, u32[]{:S(2)}, u32[]{:S(2)}) collective-permute-start(bf16[32,1024]{1,0:T(8,128)(2,1)} %get-tuple-element.9.refs_0_), channel_id=1, source_target_pairs={{0,1},{1,2},{2,3},{3,0},{4,5},{5,6},{6,7},{7,4},{8,9},{9,10},{10,1... | collective-permute-start | bytes 196616 | tf_op jit(solution)/shard_map/ppermute | solution.py:566
  36.5 1.5 %collective-permute-start.11 = (bf16[32,1024]{1,0:T(8,128)(2,1)}, bf16[32,1024]{1,0:T(8,128)(2,1)S(1)}, u32[]{:S(2)}, u32[]{:S(2)}) collective-permute-start(bf16[32,1024]{1,0:T(8,128)(2,1)} %get-tuple-element.9.refs_0_), channel_id=1, source_target_pairs={{0,2},{1,3},{2,0},{3,1},{4,6},{5,7},{6,4},{7,5},{8,10},{9,11},{10,... | collective-permute-start | bytes 196616 | tf_op jit(solution)/shard_map/ppermute | solution.py:566
  38.0 0.5 collective-permute-start.12
  38.6 8.5 %absorb_prefill.1.qa_hbm = bf16[8,1024,640]{2,1,0:T(8,128)(2,1)} custom-call(bf16[64,192,128]{2,1,0:T(8,128)(2,1)} %bitcast.12, bf16[64,128,512]{2,1,0:T(8,128)(2,1)} %refs_12_.1), custom_call_target="tpu_custom_call" | custom-call | flops 1073741824 | bytes 22020096 | tf_op jit(solution)/shard_map/absorb_prefill/pallas_call | solution.py:132
  47.2 1.2 %select_rows.1 = bf16[32,1024]{1,0:T(8,128)(2,1)S(1)} custom-call(s32[2]{0:T(128)S(1)} %copy-done.1, s32[64]{0:T(128)S(1)} %copy-done.3, bf16[32,1024]{1,0:T(8,128)(2,1)S(1)} %copy-done, bf16[32,1024]{1,0:T(8,128)(2,1)S(1)} %collective-permute-done.10.refs_1_, bf16[32,1024]{1,0:T(8,128)(2,1)S(1)} %collective-permute-done.11.refs_2_, ...), custom_call_target="tpu_custom_call" | custom-call | tf_op jit(solution)/shard_map/select_rows/pallas_call | solution.py:490
  48.3 0.1 collective-permute-start.13
  48.4 11.5 %shard_map.113.refs_0_ = bf16[128,8192]{1,0:T(8,128)(2,1)} custom-call(s32[2]{0:T(128)} %pad_add_fusion.info_ref, s32[4,1024]{1,0:T(4,128)} %seg_hbm.5, s32[4,1024]{1,0:T(4,128)} %seg_hbm.5, bf16[8,1024,640]{2,1,0:T(8,128)(2,1)} %absorb_prefill.1.qa_hbm, bf16[1024,640]{1,0:T(8,128)(2,1)} %get-tuple-element.8.keys_hbm, bf16[64,512,128]{2,1,0:T(8,128)(2,1)} %refs_1_.1), custom_call_target="tpu_custom_call" | custom-call | flops 5368709120 | bytes 10485760 | tf_op jit(solution)/shard_map/pallas_call | solution.py:290
  60.0 3.9 %collective-permute-start.14 = (bf16[64,1024]{1,0:T(8,128)(2,1)S(1)}, bf16[64,1024]{1,0:T(8,128)(2,1)S(1)}, u32[]{:S(2)}, u32[]{:S(2)}) collective-permute-start(bf16[64,1024]{1,0:T(8,128)(2,1)S(1)} %pad_maximum_fusion.refs_0_), channel_id=1, source_target_pairs={{0,8},{4,12},{8,16},{12,20},{16,24},{20,28},{24,0},{28,4},{1,9},{5... | collective-permute-start | bytes 393224 | tf_op jit(solution)/shard_map/ppermute | solution.py:554
  63.9 1.8 %collective-permute-start.15 = (bf16[64,1024]{1,0:T(8,128)(2,1)S(1)}, bf16[64,1024]{1,0:T(8,128)(2,1)S(1)}, u32[]{:S(2)}, u32[]{:S(2)}) collective-permute-start(bf16[64,1024]{1,0:T(8,128)(2,1)S(1)} %pad_maximum_fusion.refs_0_), channel_id=1, source_target_pairs={{0,16},{4,20},{8,24},{12,28},{16,0},{20,4},{24,8},{28,12},{1,17},{... | collective-permute-start | bytes 393224 | tf_op jit(solution)/shard_map/ppermute | solution.py:554
  65.8 0.6 collective-permute-start.16
  66.4 11.5 %shard_map.114 = bf16[128,8192]{1,0:T(8,128)(2,1)} custom-call(s32[2]{0:T(128)} %pad_add_fusion.info_ref, s32[4,1024]{1,0:T(4,128)} %seg_hbm.5, s32[4,1024]{1,0:T(4,128)} %seg_hbm.5, bf16[8,1024,640]{2,1,0:T(8,128)(2,1)} %absorb_prefill.1.qa_hbm, bf16[1024,640]{1,0:T(8,128)(2,1)} %get-tuple-element.8.keys_hbm, ...), custom_call_target="tpu_custom_call", output_to_operand_aliasing={{}: (5, {})} | custom-call | flops 5368709120 | bytes 10485760 | tf_op jit(solution)/shard_map/pallas_call | solution.py:290
  77.9 1.6 %assemble.1 = bf16[32,8192]{1,0:T(8,128)(2,1)} custom-call(s32[2]{0:T(128)S(1)} %copy-done.2, bf16[64,1024]{1,0:T(8,128)(2,1)S(1)} %pad_maximum_fusion.refs_0_, bf16[64,1024]{1,0:T(8,128)(2,1)S(1)} %collective-permute-done.14.refs_1_, bf16[64,1024]{1,0:T(8,128)(2,1)S(1)} %collective-permute-done.15.refs_2_, bf16[64,1024]{1,0:T(8,128)(2,1)S(1)} %collective-permute-done.16.refs_3_), custom_call_target="tpu_custom_call" | custom-call | tf_op jit(solution)/shard_map/assemble/pallas_call | solution.py:537
  (39 shorter events, 0.1 us)
Async XLA Ops:
  3.7 13.2 %collective-permute-start = (bf16[128,640]{1,0:T(8,128)(2,1)}, bf16[128,640]{1,0:T(8,128)(2,1)S(1)}, u32[]{:S(2)}, u32[]{:S(2)}) collective-permute-start(bf16[128,640]{1,0:T(8,128)(2,1)} %get-tuple-element.6.refs_0_), channel_id=1, source_target_pairs={{0,8},{4,12},{8,16},{12,20},{16,24},{20,28},{24,0},{28,4},{1,9},{5... | collective-permute-start | bytes 491528 | tf_op jit(solution)/shard_map/ppermute | solution.py:554
  6.8 13.5 %collective-permute-start.1 = (bf16[128,640]{1,0:T(8,128)(2,1)}, bf16[128,640]{1,0:T(8,128)(2,1)S(1)}, u32[]{:S(2)}, u32[]{:S(2)}) collective-permute-start(bf16[128,640]{1,0:T(8,128)(2,1)} %get-tuple-element.6.refs_0_), channel_id=1, source_target_pairs={{0,16},{4,20},{8,24},{12,28},{16,0},{20,4},{24,8},{28,12},{1,17},{... | collective-permute-start | bytes 491528 | tf_op jit(solution)/shard_map/ppermute | solution.py:554
  9.4 11.0 %collective-permute-start.2 = (bf16[128,640]{1,0:T(8,128)(2,1)}, bf16[128,640]{1,0:T(8,128)(2,1)S(1)}, u32[]{:S(2)}, u32[]{:S(2)}) collective-permute-start(bf16[128,640]{1,0:T(8,128)(2,1)} %get-tuple-element.6.refs_0_), channel_id=1, source_target_pairs={{0,24},{4,28},{8,0},{12,4},{16,8},{20,12},{24,16},{28,20},{1,25},{... | collective-permute-start | bytes 491528 | tf_op jit(solution)/shard_map/ppermute | solution.py:554
  10.7 6.2 %collective-permute-start.7 = (bf16[32,2176]{1,0:T(8,128)(2,1)}, bf16[32,2176]{1,0:T(8,128)(2,1)S(1)}, u32[]{:S(2)}, u32[]{:S(2)}) collective-permute-start(bf16[32,2176]{1,0:T(8,128)(2,1)} %get-tuple-element.7.refs_8_), channel_id=1, source_target_pairs={{0,1},{1,2},{2,3},{3,0},{4,5},{5,6},{6,7},{7,4},{8,9},{9,10},{10,1... | collective-permute-start | bytes 417800 | tf_op jit(solution)/shard_map/ppermute | solution.py:566
  12.2 8.6 %collective-permute-start.8 = (bf16[32,2176]{1,0:T(8,128)(2,1)}, bf16[32,2176]{1,0:T(8,128)(2,1)S(1)}, u32[]{:S(2)}, u32[]{:S(2)}) collective-permute-start(bf16[32,2176]{1,0:T(8,128)(2,1)} %get-tuple-element.7.refs_8_), channel_id=1, source_target_pairs={{0,2},{1,3},{2,0},{3,1},{4,6},{5,7},{6,4},{7,5},{8,10},{9,11},{10,... | collective-permute-start | bytes 417800 | tf_op jit(solution)/shard_map/ppermute | solution.py:566
  16.9 10.0 %copy-start.11 = (bf16[32,2176]{1,0:T(8,128)(2,1)}, bf16[32,2176]{1,0:T(8,128)(2,1)S(1)}, u32[]{:S(2)}) copy-start(bf16[32,2176]{1,0:T(8,128)(2,1)S(1)} %collective-permute-done.7.refs_9_) | copy-start | bytes 417796
  16.9 9.9 %collective-permute-start.3 = (bf16[128,640]{1,0:T(8,128)(2,1)}, bf16[128,640]{1,0:T(8,128)(2,1)S(1)}, u32[]{:S(2)}, u32[]{:S(2)}) collective-permute-start(bf16[128,640]{1,0:T(8,128)(2,1)} %get-tuple-element.6.refs_0_), channel_id=1, source_target_pairs={{0,4},{4,0},{8,12},{12,8},{16,20},{20,16},{24,28},{28,24},{1,5},{5... | collective-permute-start | bytes 491528 | tf_op jit(solution)/shard_map/ppermute | solution.py:561
  16.9 10.0 %copy-start.4 = (bf16[128,640]{1,0:T(8,128)(2,1)}, bf16[128,640]{1,0:T(8,128)(2,1)S(1)}, u32[]{:S(2)}) copy-start(bf16[128,640]{1,0:T(8,128)(2,1)S(1)} %collective-permute-done.refs_1_) | copy-start | bytes 491524
  16.9 9.9 %collective-permute-start.4 = (bf16[128,640]{1,0:T(8,128)(2,1)S(1)}, bf16[128,640]{1,0:T(8,128)(2,1)S(1)}, u32[]{:S(2)}, u32[]{:S(2)}) collective-permute-start(bf16[128,640]{1,0:T(8,128)(2,1)S(1)} %collective-permute-done.refs_1_), channel_id=1, source_target_pairs={{0,4},{4,0},{8,12},{12,8},{16,20},{20,16},{24,28},{28,24},{1,5},{5... | collective-permute-start | bytes 491528 | tf_op jit(solution)/shard_map/ppermute | solution.py:561
  20.3 6.5 %copy-start.5 = (bf16[128,640]{1,0:T(8,128)(2,1)}, bf16[128,640]{1,0:T(8,128)(2,1)S(1)}, u32[]{:S(2)}) copy-start(bf16[128,640]{1,0:T(8,128)(2,1)S(1)} %collective-permute-done.1.refs_2_) | copy-start | bytes 491524
  20.3 6.5 %collective-permute-start.5 = (bf16[128,640]{1,0:T(8,128)(2,1)S(1)}, bf16[128,640]{1,0:T(8,128)(2,1)S(1)}, u32[]{:S(2)}, u32[]{:S(2)}) collective-permute-start(bf16[128,640]{1,0:T(8,128)(2,1)S(1)} %collective-permute-done.1.refs_2_), channel_id=1, source_target_pairs={{0,4},{4,0},{8,12},{12,8},{16,20},{20,16},{24,28},{28,24},{1,5},{5... | collective-permute-start | bytes 491528 | tf_op jit(solution)/shard_map/ppermute | solution.py:561
  20.3 6.5 %copy-start.6 = (bf16[128,640]{1,0:T(8,128)(2,1)}, bf16[128,640]{1,0:T(8,128)(2,1)S(1)}, u32[]{:S(2)}) copy-start(bf16[128,640]{1,0:T(8,128)(2,1)S(1)} %collective-permute-done.2.refs_3_) | copy-start | bytes 491524
  20.4 6.5 %collective-permute-start.6 = (bf16[128,640]{1,0:T(8,128)(2,1)S(1)}, bf16[128,640]{1,0:T(8,128)(2,1)S(1)}, u32[]{:S(2)}, u32[]{:S(2)}) collective-permute-start(bf16[128,640]{1,0:T(8,128)(2,1)S(1)} %collective-permute-done.2.refs_3_), channel_id=1, source_target_pairs={{0,4},{4,0},{8,12},{12,8},{16,20},{20,16},{24,28},{28,24},{1,5},{5... | collective-permute-start | bytes 491528 | tf_op jit(solution)/shard_map/ppermute | solution.py:561
  20.9 6.0 %copy-start.12 = (bf16[32,2176]{1,0:T(8,128)(2,1)}, bf16[32,2176]{1,0:T(8,128)(2,1)S(1)}, u32[]{:S(2)}) copy-start(bf16[32,2176]{1,0:T(8,128)(2,1)S(1)} %collective-permute-done.8.refs_10_) | copy-start | bytes 417796
  20.9 5.9 %collective-permute-start.9 = (bf16[32,2176]{1,0:T(8,128)(2,1)}, bf16[32,2176]{1,0:T(8,128)(2,1)S(1)}, u32[]{:S(2)}, u32[]{:S(2)}) collective-permute-start(bf16[32,2176]{1,0:T(8,128)(2,1)} %get-tuple-element.7.refs_8_), channel_id=1, source_target_pairs={{0,3},{1,0},{2,1},{3,2},{4,7},{5,4},{6,5},{7,6},{8,11},{9,8},{10,9... | collective-permute-start | bytes 417800 | tf_op jit(solution)/shard_map/ppermute | solution.py:566
  26.8 0.7 copy-start.13
  26.8 0.7 copy-start.7
  26.8 0.8 copy-start.8
  26.8 0.8 %copy-start.9 = (bf16[128,640]{1,0:T(8,128)(2,1)}, bf16[128,640]{1,0:T(8,128)(2,1)S(1)}, u32[]{:S(2)}) copy-start(bf16[128,640]{1,0:T(8,128)(2,1)S(1)} %collective-permute-done.5.refs_6_) | copy-start | bytes 491524
  27.6 0.7 copy-start.10
  34.1 13.0 %collective-permute-start.10 = (bf16[32,1024]{1,0:T(8,128)(2,1)}, bf16[32,1024]{1,0:T(8,128)(2,1)S(1)}, u32[]{:S(2)}, u32[]{:S(2)}) collective-permute-start(bf16[32,1024]{1,0:T(8,128)(2,1)} %get-tuple-element.9.refs_0_), channel_id=1, source_target_pairs={{0,1},{1,2},{2,3},{3,0},{4,5},{5,6},{6,7},{7,4},{8,9},{9,10},{10,1... | collective-permute-start | bytes 196616 | tf_op jit(solution)/shard_map/ppermute | solution.py:566
  36.5 10.6 %collective-permute-start.11 = (bf16[32,1024]{1,0:T(8,128)(2,1)}, bf16[32,1024]{1,0:T(8,128)(2,1)S(1)}, u32[]{:S(2)}, u32[]{:S(2)}) collective-permute-start(bf16[32,1024]{1,0:T(8,128)(2,1)} %get-tuple-element.9.refs_0_), channel_id=1, source_target_pairs={{0,2},{1,3},{2,0},{3,1},{4,6},{5,7},{6,4},{7,5},{8,10},{9,11},{10,... | collective-permute-start | bytes 196616 | tf_op jit(solution)/shard_map/ppermute | solution.py:566
  38.0 9.1 %collective-permute-start.12 = (bf16[32,1024]{1,0:T(8,128)(2,1)}, bf16[32,1024]{1,0:T(8,128)(2,1)S(1)}, u32[]{:S(2)}, u32[]{:S(2)}) collective-permute-start(bf16[32,1024]{1,0:T(8,128)(2,1)} %get-tuple-element.9.refs_0_), channel_id=1, source_target_pairs={{0,3},{1,0},{2,1},{3,2},{4,7},{5,4},{6,5},{7,6},{8,11},{9,8},{10,9... | collective-permute-start | bytes 196616 | tf_op jit(solution)/shard_map/ppermute | solution.py:566
  38.5 8.6 %copy-start = (bf16[32,1024]{1,0:T(8,128)(2,1)S(1)}, bf16[32,1024]{1,0:T(8,128)(2,1)}, u32[]{:S(2)}) copy-start(bf16[32,1024]{1,0:T(8,128)(2,1)} %get-tuple-element.9.refs_0_) | copy-start | bytes 196612
  38.5 8.6 %copy-start.1 = (s32[2]{0:T(128)S(1)}, s32[2]{0:T(128)}, u32[]{:S(2)}) copy-start(s32[2]{0:T(128)} %pad_add_fusion.info_ref) | copy-start | bytes 28
  38.6 8.6 %copy-start.3 = (s32[64]{0:T(128)S(1)}, s32[64]{0:T(128)}, u32[]{:S(2)}) copy-start(s32[64]{0:T(128)} %assign_ref.3) | copy-start | bytes 772
  48.3 11.6 %collective-permute-start.13 = (bf16[32,1024]{1,0:T(8,128)(2,1)S(1)}, bf16[32,1024]{1,0:T(8,128)(2,1)S(1)}, u32[]{:S(2)}, u32[]{:S(2)}) collective-permute-start(bf16[32,1024]{1,0:T(8,128)(2,1)S(1)} %select_rows.1), channel_id=1, source_target_pairs={{0,4},{4,0},{8,12},{12,8},{16,20},{20,16},{24,28},{28,24},{1,5},{5... | collective-permute-start | bytes 196616 | tf_op jit(solution)/shard_map/ppermute | solution.py:603
  60.0 18.0 %copy-start.2 = (s32[2]{0:T(128)S(1)}, s32[2]{0:T(128)}, u32[]{:S(2)}) copy-start(s32[2]{0:T(128)} %pad_add_fusion.info_ref) | copy-start | bytes 28
  60.0 17.9 %collective-permute-start.14 = (bf16[64,1024]{1,0:T(8,128)(2,1)S(1)}, bf16[64,1024]{1,0:T(8,128)(2,1)S(1)}, u32[]{:S(2)}, u32[]{:S(2)}) collective-permute-start(bf16[64,1024]{1,0:T(8,128)(2,1)S(1)} %pad_maximum_fusion.refs_0_), channel_id=1, source_target_pairs={{0,8},{4,12},{8,16},{12,20},{16,24},{20,28},{24,0},{28,4},{1,9},{5... | collective-permute-start | bytes 393224 | tf_op jit(solution)/shard_map/ppermute | solution.py:554
  63.9 14.0 %collective-permute-start.15 = (bf16[64,1024]{1,0:T(8,128)(2,1)S(1)}, bf16[64,1024]{1,0:T(8,128)(2,1)S(1)}, u32[]{:S(2)}, u32[]{:S(2)}) collective-permute-start(bf16[64,1024]{1,0:T(8,128)(2,1)S(1)} %pad_maximum_fusion.refs_0_), channel_id=1, source_target_pairs={{0,16},{4,20},{8,24},{12,28},{16,0},{20,4},{24,8},{28,12},{1,17},{... | collective-permute-start | bytes 393224 | tf_op jit(solution)/shard_map/ppermute | solution.py:554
  65.8 12.2 %collective-permute-start.16 = (bf16[64,1024]{1,0:T(8,128)(2,1)S(1)}, bf16[64,1024]{1,0:T(8,128)(2,1)S(1)}, u32[]{:S(2)}, u32[]{:S(2)}) collective-permute-start(bf16[64,1024]{1,0:T(8,128)(2,1)S(1)} %pad_maximum_fusion.refs_0_), channel_id=1, source_target_pairs={{0,24},{4,28},{8,0},{12,4},{16,8},{20,12},{24,16},{28,20},{1,25},{... | collective-permute-start | bytes 393224 | tf_op jit(solution)/shard_map/ppermute | solution.py:554

commit v3 on v2

--- a/solution.py
+++ b/solution.py
@@ -35,58 +35,60 @@
     return (values * lax.rsqrt(mean + EPS)).astype(jnp.bfloat16)
 
 
-def prepare_kernel(info_ref, lat_ref, rope_ref, q_ref, nl_ref, nr_ref, cache_ref, pack_ref, *, group):
+def prepare_kernel(lat_ref, rope_ref, q_hbm, nl_ref, nr_ref, cache_ref, pack_ref, q_ref, sem, *, group):
     steps, docs, block, _ = q_ref.shape
+    seq_idx = lax.axis_index("seq")
+    ratio = block // group
+    begin = pl.multiple_of(seq_idx // ratio * block, block)
+    copy = pltpu.make_async_copy(q_hbm.at[:, :, pl.ds(begin, block)], q_ref, sem)
+    copy.start()
     cache_ref[:, :LAT] = normed(lat_ref[...])
     rope = jnp.transpose(rope_ref[...].astype(jnp.float32))
     rope = rope.astype(jnp.bfloat16)
     cache_ref[:, LAT:] = jnp.concatenate([rope, jnp.zeros_like(rope)], axis=1)
     wide = group * NOPE
+    base = wide + LAT
+    for t in range(steps):
+        row = pl.ds(t * docs, docs)
+        pack_ref[row, wide : wide + LAT] = normed(nl_ref[t])
+        rope = nr_ref[t]
+        pack_ref[row, base + group * ROPE :] = jnp.concatenate([rope, jnp.zeros_like(rope)], axis=1)
+    copy.wait()
     for t in range(steps):
         row = pl.ds(t * docs, docs)
         q = jnp.swapaxes(q_ref[t].astype(jnp.float32), 0, 1)
         part = q[:group]
-        for k in range(1, block // group):
-            chosen = lax.rem(info_ref[0], block // group) == k
+        for k in range(1, ratio):
+            chosen = lax.rem(seq_idx, ratio) == k
             part = jnp.where(chosen, q[k * group : (k + 1) * group], part)
         part = part.astype(jnp.bfloat16)
-        pack_ref[row, wide : wide + LAT] = normed(nl_ref[t])
-        base = wide + LAT
         for h in range(group):
             pack_ref[row, h * NOPE : (h + 1) * NOPE] = part[h, :, :NOPE]
             pack_ref[row, base + h * ROPE : base + (h + 1) * ROPE] = part[h, :, NOPE:]
-        rope = nr_ref[t]
-        pack_ref[row, base + group * ROPE :] = jnp.concatenate([rope, jnp.zeros_like(rope)], axis=1)
-
-
-def prepare(info, latent, rope, q_decode, new_latent, new_rope, group):
+
+
+def prepare(latent, rope, q_decode, new_latent, new_rope, group):
     tokens = latent.shape[0]
     steps, docs, _, size = q_decode.shape
     block = max(group, 8)
-    ratio = block // group
-    full = lambda x: pl.BlockSpec(x.shape, lambda i, info: (0,) * x.ndim)
+    full = lambda x: pl.BlockSpec(x.shape, lambda i: (0,) * len(x.shape))
     out_shape = (
         jax.ShapeDtypeStruct((tokens, WIDTH), jnp.bfloat16),
         jax.ShapeDtypeStruct((steps * docs, group * size + WIDTH), jnp.bfloat16),
     )
     return pl.pallas_call(
         functools.partial(prepare_kernel, group=group),
-        grid_spec=pltpu.PrefetchScalarGridSpec(
-            num_scalar_prefetch=1,
-            grid=(1,),
-            in_specs=[
-                full(latent),
-                full(rope),
-                pl.BlockSpec((steps, docs, block, size), lambda i, info: (0, 0, info[0] // ratio, 0)),
-                full(new_latent),
-                full(new_rope),
-            ],
-            out_specs=tuple(full(s) for s in out_shape),
-        ),
+        grid=(1,),
+        in_specs=[full(latent), full(rope), FAR, full(new_latent), full(new_rope)],
+        out_specs=tuple(full(s) for s in out_shape),
         out_shape=out_shape,
+        scratch_shapes=[
+            pltpu.VMEM((steps, docs, block, size), jnp.bfloat16),
+            pltpu.SemaphoreType.DMA,
+        ],
         compiler_params=pltpu.CompilerParams(vmem_limit_bytes=60 * MIB),
         name="prepare",
-    )(info, latent, rope, q_decode, new_latent, new_rope)
+    )(latent, rope, q_decode, new_latent, new_rope)
 
 
 def absorb_kernel(q_hbm, ak_hbm, o_hbm, q_buf, ak_buf, o_buf, q_sem, ak_sem, o_sem, *, group):
@@ -168,7 +170,7 @@
 
 
 def prefill_kernel(
-    info_ref, segs_ref, seg_hbm, qa_hbm, keys_hbm, *refs, part, fast, slow, heads, aliased
+    segs_ref, seg_hbm, qa_hbm, keys_hbm, *refs, part, fast, slow, heads, aliased
 ):
     refs = refs[1 if aliased else 0 :]
     av_hbm, o_hbm, kbuf, olat, av, qa_buf, seg_buf, o_buf, ksem, qsem, vsem, ssem, osem = refs
@@ -176,8 +178,8 @@
     tokens = olat.shape[1]
     held = kbuf.shape[0]
     length = keys_hbm.shape[0]
-    seq_idx = info_ref[0]
-    span_idx = info_ref[1]
+    seq_idx = lax.axis_index("seq")
+    span_idx = lax.axis_index("span")
     low = jnp.clip((seq_idx + 1) * tokens - held, 0, length - held)
     low = pl.multiple_of(low, TOK)
     keys_copy = pltpu.make_async_copy(keys_hbm.at[pl.ds(low, held)], kbuf, ksem)
@@ -278,7 +280,7 @@
         result.wait()
 
 
-def attend_prefill(info, segment_ids, qa, keys, absorb_value, part, parts, most, out=None):
+def attend_prefill(segment_ids, qa, keys, absorb_value, part, parts, most, out=None):
     blocks, rows, _ = qa.shape
     tokens = blocks * TOK
     heads = rows // TOK // parts
@@ -286,7 +288,7 @@
     fast = min(most, length)
     slow = min(most + 128, length)
     aliased = out is not None
-    args = [info, segment_ids, segment_ids, qa, keys, *([out] if aliased else []), absorb_value]
+    args = [segment_ids, segment_ids, qa, keys, *([out] if aliased else []), absorb_value]
     return pl.pallas_call(
         functools.partial(
             prefill_kernel,
@@ -297,7 +299,7 @@
             aliased=aliased,
         ),
         grid_spec=pltpu.PrefetchScalarGridSpec(
-            num_scalar_prefetch=2,
+            num_scalar_prefetch=1,
             grid=(1,),
             in_specs=[
                 *([FAR] * (aliased + 4)),
@@ -318,7 +320,7 @@
             ],
         ),
         out_shape=jax.ShapeDtypeStruct((tokens, parts * heads * VHEAD), jnp.bfloat16),
-        input_output_aliases={5: 0} if aliased else {},
+        input_output_aliases={4: 0} if aliased else {},
         cost_estimate=pl.CostEstimate(
             flops=2 * tokens * heads * (fast * (WIDTH + LAT) + LAT * VHEAD),
             bytes_accessed=2 * heads * (tokens * (WIDTH + VHEAD) + LAT * VHEAD),
@@ -328,14 +330,14 @@
     )(*args)
 
 
-def decode_kernel(info_ref, assign_ref, seg_hbm, *refs, count, spans, docs, steps, group):
+def decode_kernel(assign_ref, seg_hbm, *refs, count, spans, docs, steps, group):
     pieces = refs[:count]
     packs = refs[count : count + spans]
     ak_hbm, av_hbm, o_ref, keys_hbm, kbuf, qa, pack_ref, ak_ref, av_ref, seg_ref, ksem, sems = refs[
         count + spans :
     ]
-    seq_idx = info_ref[0]
-    span_idx = info_ref[1]
+    seq_idx = lax.axis_index("seq")
+    span_idx = lax.axis_index("span")
     near = steps * docs
     rows = near * group
     copies = gather_copies(pieces, kbuf, ksem, seq_idx)
@@ -410,7 +412,7 @@
     handed.wait()
 
 
-def attend_decode(info, assignment, segment_ids, pieces, packs, absorb_key, absorb_value, steps):
+def attend_decode(assignment, segment_ids, pieces, packs, absorb_key, absorb_value, steps):
     near, size = packs[0].shape
     docs = near // steps
     count, spans = len(pieces), len(packs)
@@ -424,7 +426,7 @@
             decode_kernel, count=count, spans=spans, docs=docs, steps=steps, group=group
         ),
         grid_spec=pltpu.PrefetchScalarGridSpec(
-            num_scalar_prefetch=2,
+            num_scalar_prefetch=1,
             grid=(1,),
             in_specs=[
                 FAR,
@@ -452,15 +454,15 @@
             bytes_accessed=2 * (length * WIDTH + group * LAT * VHEAD * 2),
             transcendentals=rows * length,
         ),
-        compiler_params=pltpu.CompilerParams(vmem_limit_bytes=55 * MIB),
+        compiler_params=pltpu.CompilerParams(vmem_limit_bytes=52 * MIB),
         name="attend_decode",
-    )(info, assignment, segment_ids, *pieces, *packs, absorb_key, absorb_value)
-
-
-def select_kernel(info_ref, assign_ref, *refs, spans, docs, steps):
+    )(assignment, segment_ids, *pieces, *packs, absorb_key, absorb_value)
+
+
+def select_kernel(assign_ref, *refs, spans, docs, steps):
     parts = refs[:spans]
     o_ref, value, sems = refs[spans:]
-    span_idx = info_ref[1]
+    span_idx = lax.axis_index("span")
     near = steps * docs
     copies = [
         pltpu.make_async_copy(part, value.at[pl.ds(i * near, near)], sems.at[i])
@@ -484,13 +486,13 @@
     o_ref[...] = jnp.dot(pick, value[...], preferred_element_type=jnp.float32).astype(jnp.bfloat16)
 
 
-def select_rows(info, assignment, parts, steps):
+def select_rows(assignment, parts, steps):
     near, size = parts[0].shape
     spans = len(parts)
     return pl.pallas_call(
         functools.partial(select_kernel, spans=spans, docs=near // steps, steps=steps),
         grid_spec=pltpu.PrefetchScalarGridSpec(
-            num_scalar_prefetch=2,
+            num_scalar_prefetch=1,
             grid=(1,),
             in_specs=[ANY] * spans,
             out_specs=pl.BlockSpec((near, size), lambda i, *_: (0, 0)),
@@ -502,14 +504,14 @@
         out_shape=jax.ShapeDtypeStruct((near, size), jnp.bfloat16),
         compiler_params=pltpu.CompilerParams(vmem_limit_bytes=8 * MIB),
         name="select_rows",
-    )(info, assignment, *parts)
-
-
-def assemble_kernel(info_ref, *refs):
+    )(assignment, *parts)
+
+
+def assemble_kernel(*refs):
     parts, o_ref, sems = refs[:-2], refs[-2], refs[-1]
     near = parts[0].shape[0] // 2
     size = parts[0].shape[1]
-    seq_idx = info_ref[0]
+    seq_idx = lax.axis_index("seq")
     core = lax.rem(seq_idx, 2)
     copies = []
     for i, part in enumerate(parts):
@@ -530,23 +532,23 @@
         copy.wait()
 
 
-def assemble(info, parts):
+def assemble(parts):
     near, size = parts[0].shape
     number = 2 * len(parts)
     shape = (near // 2, number * size)
     return pl.pallas_call(
         assemble_kernel,
         grid_spec=pltpu.PrefetchScalarGridSpec(
-            num_scalar_prefetch=1,
+            num_scalar_prefetch=0,
             grid=(1,),
             in_specs=[ANY] * len(parts),
-            out_specs=pl.BlockSpec(shape, lambda i, info: (0, 0)),
+            out_specs=pl.BlockSpec(shape, lambda i: (0, 0)),
             scratch_shapes=[pltpu.SemaphoreType.DMA((number,))],
         ),
         out_shape=jax.ShapeDtypeStruct(shape, jnp.bfloat16),
         compiler_params=pltpu.CompilerParams(vmem_limit_bytes=8 * MIB),
         name="assemble",
-    )(info, *parts)
+    )(*parts)
 
 
 def spread_far(value, count):
@@ -585,27 +587,24 @@
     spans = lax.axis_size("span")
     group = heads // count
     most = segment_ids.shape[1] // 2
-    info = jnp.stack([lax.axis_index("seq"), lax.axis_index("span")]).astype(jnp.int32)
-
-    cache, pack = prepare(
-        info, kv_latent[0], key_rope[0].T, q_decode, new_latent, new_rope, group
-    )
+
+    cache, pack = prepare(kv_latent[0], key_rope[0].T, q_decode, new_latent, new_rope, group)
     pieces = spread_far(cache, count)
     packs = spread(pack, "span", spans)
     qa = absorb_prefill(q_prefill[0].transpose(1, 2, 0), absorb_key)
     pieces = spread_near(pieces, count)
     decoded, keys = attend_decode(
-        info, assignment, segment_ids, pieces, packs, absorb_key, absorb_value, steps
+        assignment, segment_ids, pieces, packs, absorb_key, absorb_value, steps
     )
     returned = spread(decoded, "span", spans)
-    out = attend_prefill(info, segment_ids, qa, keys, absorb_value, 0, PARTS, most)
-    chosen = select_rows(info, assignment, returned, steps)
+    out = attend_prefill(segment_ids, qa, keys, absorb_value, 0, PARTS, most)
+    chosen = select_rows(assignment, returned, steps)
     swapped = lax.ppermute(chosen, "seq", [(i, i ^ 1) for i in range(count)])
     both = jnp.concatenate([chosen, swapped], axis=0)
     finals = spread_far(both, count)
     for part in range(1, PARTS):
-        out = attend_prefill(info, segment_ids, qa, keys, absorb_value, part, PARTS, most, out)
-    decode_out = assemble(info, finals)
+        out = attend_prefill(segment_ids, qa, keys, absorb_value, part, PARTS, most, out)
+    decode_out = assemble(finals)
     return (out[None], decode_out.reshape(steps, docs, heads * VHEAD))
 
 

time: 80.2 us -> 81.2 us (1.012)
  local copies, waits for them, and re-layouts: 1.46 us -> 3.19 us
    unnamed x28 -> x10, local copies, waits for them, and re-layouts: 1.46 us -> 3.19 us
  transfers between devices with their start and end apart: 17 -> 17, of which waited for: 3 -> 3; matrix products, arithmetic and copies ran while one was open for 0% -> 0% of each run, Pallas kernels for 40% -> 39%
where the time goes in v3:
time: 81.2 us; the launch traced here: 80.6 us
  Pallas kernels  42.4 us (52%)
  starting transfers between devices  24.4 us (30%)
  waiting for transfers between devices  9.59 us (12%)
  local copies, waits for them, and re-layouts  3.19 us (4%)
  between operations  0.95 us (1%)
    pallas_call x2, Pallas kernels, attend_prefill(): pl.pallas_call(functools.partial(prefill_kernel, part=part, fast=fast, sl...  23 us
    ppermute x6, starting transfers between devices, spread_far(): lax.ppermute(value, 'seq', [(i, (i + 2 * k) % count) for i in range(count)])  13.5 us
    ppermute x6, starting transfers between devices, spread(): lax.ppermute(value, axis, [(i, (i + k) % count) for i in range(count)])  9.88 us
    pallas_call x1, Pallas kernels, absorb_prefill(): pl.pallas_call(functools.partial(absorb_kernel, group=group), in_specs=[F...  8.49 us
    ppermute x6, waiting for transfers between devices, spread(): lax.ppermute(value, axis, [(i, (i + k) % count) for i in range(count)])  6.64 us
    pallas_call x1, Pallas kernels, attend_decode(): pl.pallas_call(functools.partial(decode_kernel, count=count, spans=spans,...  6.02 us
    unnamed x10, local copies, waits for them, and re-layouts  3.19 us
    ppermute x6, waiting for transfers between devices, spread_far(): lax.ppermute(value, 'seq', [(i, (i + 2 * k) % count) for i in range(count)])  2.94 us
  transfers between devices with their start and end apart: 17, of which 3 were waited for; matrix products, arithmetic and copies ran while one was open for 0% of the time, Pallas kernels for 39%

profile of v3, /device:TPU:0, one launch (start us, length us, event | category | flops | bytes accessed | tf_op | source)
XLA Modules:
  0.0 80.6 jit_solution(11060228342922059992)
XLA Ops:
  0.6 2.6 %prepare.1 = (bf16[128,640]{1,0:T(8,128)(2,1)}, bf16[32,2176]{1,0:T(8,128)(2,1)}) custom-call(bf16[128,512]{1,0:T(8,128)(2,1)} %bitcast.12, bf16[64,128]{1,0:T(8,128)(2,1)} %bitcast.13, bf16[2,16,64,192]{3,2,1,0:T(8,128)(2,1)} %q_hbm.1, bf16[2,16,512]{2,1,0:T(8,128)(2,1)} %nl_ref.1, bf16[2,16,64]{2,1,0:T(8,128)(2,1)} %nr_ref.1), custom_call_target="tpu_custom_call" | custom-call | tf_op jit(solution)/shard_map/prepare/pallas_call | solution.py:79
  3.3 3.1 %collective-permute-start = (bf16[128,640]{1,0:T(8,128)(2,1)}, bf16[128,640]{1,0:T(8,128)(2,1)S(1)}, u32[]{:S(2)}, u32[]{:S(2)}) collective-permute-start(bf16[128,640]{1,0:T(8,128)(2,1)} %get-tuple-element.6.refs_0_), channel_id=1, source_target_pairs={{0,8},{4,12},{8,16},{12,20},{16,24},{20,28},{24,0},{28,4},{1,9},{5... | collective-permute-start | bytes 491528 | tf_op jit(solution)/shard_map/ppermute | solution.py:556
  6.4 2.6 %collective-permute-start.1 = (bf16[128,640]{1,0:T(8,128)(2,1)}, bf16[128,640]{1,0:T(8,128)(2,1)S(1)}, u32[]{:S(2)}, u32[]{:S(2)}) collective-permute-start(bf16[128,640]{1,0:T(8,128)(2,1)} %get-tuple-element.6.refs_0_), channel_id=1, source_target_pairs={{0,16},{4,20},{8,24},{12,28},{16,0},{20,4},{24,8},{28,12},{1,17},{... | collective-permute-start | bytes 491528 | tf_op jit(solution)/shard_map/ppermute | solution.py:556
  9.0 1.3 %collective-permute-start.2 = (bf16[128,640]{1,0:T(8,128)(2,1)}, bf16[128,640]{1,0:T(8,128)(2,1)S(1)}, u32[]{:S(2)}, u32[]{:S(2)}) collective-permute-start(bf16[128,640]{1,0:T(8,128)(2,1)} %get-tuple-element.6.refs_0_), channel_id=1, source_target_pairs={{0,24},{4,28},{8,0},{12,4},{16,8},{20,12},{24,16},{28,20},{1,25},{... | collective-permute-start | bytes 491528 | tf_op jit(solution)/shard_map/ppermute | solution.py:556
  10.3 1.5 %collective-permute-start.7 = (bf16[32,2176]{1,0:T(8,128)(2,1)}, bf16[32,2176]{1,0:T(8,128)(2,1)S(1)}, u32[]{:S(2)}, u32[]{:S(2)}) collective-permute-start(bf16[32,2176]{1,0:T(8,128)(2,1)} %get-tuple-element.7.refs_8_), channel_id=1, source_target_pairs={{0,1},{1,2},{2,3},{3,0},{4,5},{5,6},{6,7},{7,4},{8,9},{9,10},{10,1... | collective-permute-start | bytes 417800 | tf_op jit(solution)/shard_map/ppermute | solution.py:568
  11.8 1.5 %collective-permute-start.8 = (bf16[32,2176]{1,0:T(8,128)(2,1)}, bf16[32,2176]{1,0:T(8,128)(2,1)S(1)}, u32[]{:S(2)}, u32[]{:S(2)}) collective-permute-start(bf16[32,2176]{1,0:T(8,128)(2,1)} %get-tuple-element.7.refs_8_), channel_id=1, source_target_pairs={{0,2},{1,3},{2,0},{3,1},{4,6},{5,7},{6,4},{7,5},{8,10},{9,11},{10,... | collective-permute-start | bytes 417800 | tf_op jit(solution)/shard_map/ppermute | solution.py:568
  13.3 3.2 %collective-permute-done.7.refs_9_ = bf16[32,2176]{1,0:T(8,128)(2,1)S(1)} collective-permute-done((bf16[32,2176]{1,0:T(8,128)(2,1)}, bf16[32,2176]{1,0:T(8,128)(2,1)S(1)}, u32[]{:S(2)}, u32[]{:S(2)}) %collective-permute-start.7) | collective-permute-done | bytes 139296 | tf_op jit(solution)/shard_map/ppermute | solution.py:568
  16.5 0.0 collective-permute-done.refs_1_
  16.5 0.5 collective-permute-start.4
  17.0 2.9 %collective-permute-done.1.refs_2_ = bf16[128,640]{1,0:T(8,128)(2,1)S(1)} collective-permute-done((bf16[128,640]{1,0:T(8,128)(2,1)}, bf16[128,640]{1,0:T(8,128)(2,1)S(1)}, u32[]{:S(2)}, u32[]{:S(2)}) %collective-permute-start.1) | collective-permute-done | bytes 163872 | tf_op jit(solution)/shard_map/ppermute | solution.py:556
  19.9 0.5 collective-permute-start.6
  20.5 2.4 %collective-permute-start.9 = (bf16[32,2176]{1,0:T(8,128)(2,1)}, bf16[32,2176]{1,0:T(8,128)(2,1)S(1)}, u32[]{:S(2)}, u32[]{:S(2)}) collective-permute-start(bf16[32,2176]{1,0:T(8,128)(2,1)} %get-tuple-element.7.refs_8_), channel_id=1, source_target_pairs={{0,3},{1,0},{2,1},{3,2},{4,7},{5,4},{6,5},{7,6},{8,11},{9,8},{10,9... | collective-permute-start | bytes 417800 | tf_op jit(solution)/shard_map/ppermute | solution.py:568
  22.9 3.5 %collective-permute-done.9.refs_11_ = bf16[32,2176]{1,0:T(8,128)(2,1)S(1)} collective-permute-done((bf16[32,2176]{1,0:T(8,128)(2,1)}, bf16[32,2176]{1,0:T(8,128)(2,1)S(1)}, u32[]{:S(2)}, u32[]{:S(2)}) %collective-permute-start.9) | collective-permute-done | bytes 139296 | tf_op jit(solution)/shard_map/ppermute | solution.py:568
  26.4 0.0 collective-permute-done.6.refs_7_
  26.4 0.0 copy-start
  26.4 0.7 copy-done
  27.1 0.9 %copy-done.1 = bf16[128,640]{1,0:T(8,128)(2,1)S(1)} copy-done((bf16[128,640]{1,0:T(8,128)(2,1)S(1)}, bf16[128,640]{1,0:T(8,128)(2,1)}, u32[]{:S(2)}) %copy-start.1) | copy-done | bytes 163864
  28.0 0.9 %copy-done.2 = bf16[32,2176]{1,0:T(8,128)(2,1)S(1)} copy-done((bf16[32,2176]{1,0:T(8,128)(2,1)S(1)}, bf16[32,2176]{1,0:T(8,128)(2,1)}, u32[]{:S(2)}) %copy-start.2) | copy-done | bytes 139288
  28.9 0.7 copy-done.3
  29.6 6.0 %attend_decode.1 = (bf16[32,1024]{1,0:T(8,128)(2,1)S(1)}, bf16[1024,640]{1,0:T(8,128)(2,1)}) custom-call(s32[64]{0:T(128)S(1)} %copy-done.3, s32[4,1024]{1,0:T(4,128)S(1)} %copy-done, bf16[128,640]{1,0:T(8,128)(2,1)S(1)} %copy-done.1, bf16[128,640]{1,0:T(8,128)(2,1)S(1)} %collective-permute-done.refs_1_, ...), custom_call_target="tpu_custom_call" | custom-call | flops 603979776 | bytes 3407872 | tf_op jit(solution)/shard_map/attend_decode/pallas_call | solution.py:424
  35.6 2.4 %collective-permute-start.10 = (bf16[32,1024]{1,0:T(8,128)(2,1)S(1)}, bf16[32,1024]{1,0:T(8,128)(2,1)S(1)}, u32[]{:S(2)}, u32[]{:S(2)}) collective-permute-start(bf16[32,1024]{1,0:T(8,128)(2,1)S(1)} %get-tuple-element.9.refs_0_), channel_id=1, source_target_pairs={{0,1},{1,2},{2,3},{3,0},{4,5},{5,6},{6,7},{7,4},{8,9},{9,10},{10,1... | collective-permute-start | bytes 196616 | tf_op jit(solution)/shard_map/ppermute | solution.py:568
  38.0 1.5 %collective-permute-start.11 = (bf16[32,1024]{1,0:T(8,128)(2,1)S(1)}, bf16[32,1024]{1,0:T(8,128)(2,1)S(1)}, u32[]{:S(2)}, u32[]{:S(2)}) collective-permute-start(bf16[32,1024]{1,0:T(8,128)(2,1)S(1)} %get-tuple-element.9.refs_0_), channel_id=1, source_target_pairs={{0,2},{1,3},{2,0},{3,1},{4,6},{5,7},{6,4},{7,5},{8,10},{9,11},{10,... | collective-permute-start | bytes 196616 | tf_op jit(solution)/shard_map/ppermute | solution.py:568
  39.5 0.5 collective-permute-start.12
  40.1 8.5 %absorb_prefill.1.qa_hbm = bf16[8,1024,640]{2,1,0:T(8,128)(2,1)} custom-call(bf16[64,192,128]{2,1,0:T(8,128)(2,1)} %bitcast.10, bf16[64,128,512]{2,1,0:T(8,128)(2,1)} %refs_12_.1), custom_call_target="tpu_custom_call" | custom-call | flops 1073741824 | bytes 22020096 | tf_op jit(solution)/shard_map/absorb_prefill/pallas_call | solution.py:134
  48.6 1.2 %select_rows.1 = bf16[32,1024]{1,0:T(8,128)(2,1)S(1)} custom-call(s32[64]{0:T(128)S(1)} %copy-done.4, bf16[32,1024]{1,0:T(8,128)(2,1)S(1)} %get-tuple-element.9.refs_0_, bf16[32,1024]{1,0:T(8,128)(2,1)S(1)} %collective-permute-done.10.refs_1_, bf16[32,1024]{1,0:T(8,128)(2,1)S(1)} %collective-permute-done.11.refs_2_, ...), custom_call_target="tpu_custom_call" | custom-call | tf_op jit(solution)/shard_map/select_rows/pallas_call | solution.py:492
  49.8 0.1 collective-permute-start.13
  49.8 11.5 %shard_map.113.refs_0_ = bf16[128,8192]{1,0:T(8,128)(2,1)} custom-call(s32[4,1024]{1,0:T(4,128)} %seg_hbm.5, s32[4,1024]{1,0:T(4,128)} %seg_hbm.5, bf16[8,1024,640]{2,1,0:T(8,128)(2,1)} %absorb_prefill.1.qa_hbm, bf16[1024,640]{1,0:T(8,128)(2,1)} %get-tuple-element.8.keys_hbm, bf16[64,512,128]{2,1,0:T(8,128)(2,1)} %refs_1_.1), custom_call_target="tpu_custom_call" | custom-call | flops 5368709120 | bytes 10485760 | tf_op jit(solution)/shard_map/pallas_call | solution.py:292
  61.4 4.0 %collective-permute-start.14 = (bf16[64,1024]{1,0:T(8,128)(2,1)S(1)}, bf16[64,1024]{1,0:T(8,128)(2,1)S(1)}, u32[]{:S(2)}, u32[]{:S(2)}) collective-permute-start(bf16[64,1024]{1,0:T(8,128)(2,1)S(1)} %pad_maximum_fusion.refs_0_), channel_id=1, source_target_pairs={{0,8},{4,12},{8,16},{12,20},{16,24},{20,28},{24,0},{28,4},{1,9},{5... | collective-permute-start | bytes 393224 | tf_op jit(solution)/shard_map/ppermute | solution.py:556
  65.4 1.8 %collective-permute-start.15 = (bf16[64,1024]{1,0:T(8,128)(2,1)S(1)}, bf16[64,1024]{1,0:T(8,128)(2,1)S(1)}, u32[]{:S(2)}, u32[]{:S(2)}) collective-permute-start(bf16[64,1024]{1,0:T(8,128)(2,1)S(1)} %pad_maximum_fusion.refs_0_), channel_id=1, source_target_pairs={{0,16},{4,20},{8,24},{12,28},{16,0},{20,4},{24,8},{28,12},{1,17},{... | collective-permute-start | bytes 393224 | tf_op jit(solution)/shard_map/ppermute | solution.py:556
  67.2 0.7 collective-permute-start.16
  67.8 11.5 %shard_map.114 = bf16[128,8192]{1,0:T(8,128)(2,1)} custom-call(s32[4,1024]{1,0:T(4,128)} %seg_hbm.5, s32[4,1024]{1,0:T(4,128)} %seg_hbm.5, bf16[8,1024,640]{2,1,0:T(8,128)(2,1)} %absorb_prefill.1.qa_hbm, bf16[1024,640]{1,0:T(8,128)(2,1)} %get-tuple-element.8.keys_hbm, bf16[128,8192]{1,0:T(8,128)(2,1)} %shard_map.113.refs_0_, ...), custom_call_target="tpu_custom_call", output_to_operand_aliasing={{}: (4, {})} | custom-call | flops 5368709120 | bytes 10485760 | tf_op jit(solution)/shard_map/pallas_call | solution.py:292
  79.4 1.1 %assemble.1 = bf16[32,8192]{1,0:T(8,128)(2,1)} custom-call(bf16[64,1024]{1,0:T(8,128)(2,1)S(1)} %pad_maximum_fusion.refs_0_, bf16[64,1024]{1,0:T(8,128)(2,1)S(1)} %collective-permute-done.14.refs_1_, bf16[64,1024]{1,0:T(8,128)(2,1)S(1)} %collective-permute-done.15.refs_2_, bf16[64,1024]{1,0:T(8,128)(2,1)S(1)} %collective-permute-done.16.refs_3_), custom_call_target="tpu_custom_call" | custom-call | tf_op jit(solution)/shard_map/assemble/pallas_call | solution.py:539
  (20 shorter events, 0.1 us)
Async XLA Ops:
  3.3 13.2 %collective-permute-start = (bf16[128,640]{1,0:T(8,128)(2,1)}, bf16[128,640]{1,0:T(8,128)(2,1)S(1)}, u32[]{:S(2)}, u32[]{:S(2)}) collective-permute-start(bf16[128,640]{1,0:T(8,128)(2,1)} %get-tuple-element.6.refs_0_), channel_id=1, source_target_pairs={{0,8},{4,12},{8,16},{12,20},{16,24},{20,28},{24,0},{28,4},{1,9},{5... | collective-permute-start | bytes 491528 | tf_op jit(solution)/shard_map/ppermute | solution.py:556
  6.4 13.5 %collective-permute-start.1 = (bf16[128,640]{1,0:T(8,128)(2,1)}, bf16[128,640]{1,0:T(8,128)(2,1)S(1)}, u32[]{:S(2)}, u32[]{:S(2)}) collective-permute-start(bf16[128,640]{1,0:T(8,128)(2,1)} %get-tuple-element.6.refs_0_), channel_id=1, source_target_pairs={{0,16},{4,20},{8,24},{12,28},{16,0},{20,4},{24,8},{28,12},{1,17},{... | collective-permute-start | bytes 491528 | tf_op jit(solution)/shard_map/ppermute | solution.py:556
  9.0 11.0 %collective-permute-start.2 = (bf16[128,640]{1,0:T(8,128)(2,1)}, bf16[128,640]{1,0:T(8,128)(2,1)S(1)}, u32[]{:S(2)}, u32[]{:S(2)}) collective-permute-start(bf16[128,640]{1,0:T(8,128)(2,1)} %get-tuple-element.6.refs_0_), channel_id=1, source_target_pairs={{0,24},{4,28},{8,0},{12,4},{16,8},{20,12},{24,16},{28,20},{1,25},{... | collective-permute-start | bytes 491528 | tf_op jit(solution)/shard_map/ppermute | solution.py:556
  10.3 6.2 %collective-permute-start.7 = (bf16[32,2176]{1,0:T(8,128)(2,1)}, bf16[32,2176]{1,0:T(8,128)(2,1)S(1)}, u32[]{:S(2)}, u32[]{:S(2)}) collective-permute-start(bf16[32,2176]{1,0:T(8,128)(2,1)} %get-tuple-element.7.refs_8_), channel_id=1, source_target_pairs={{0,1},{1,2},{2,3},{3,0},{4,5},{5,6},{6,7},{7,4},{8,9},{9,10},{10,1... | collective-permute-start | bytes 417800 | tf_op jit(solution)/shard_map/ppermute | solution.py:568
  11.8 8.6 %collective-permute-start.8 = (bf16[32,2176]{1,0:T(8,128)(2,1)}, bf16[32,2176]{1,0:T(8,128)(2,1)S(1)}, u32[]{:S(2)}, u32[]{:S(2)}) collective-permute-start(bf16[32,2176]{1,0:T(8,128)(2,1)} %get-tuple-element.7.refs_8_), channel_id=1, source_target_pairs={{0,2},{1,3},{2,0},{3,1},{4,6},{5,7},{6,4},{7,5},{8,10},{9,11},{10,... | collective-permute-start | bytes 417800 | tf_op jit(solution)/shard_map/ppermute | solution.py:568
  16.5 9.9 %collective-permute-start.3 = (bf16[128,640]{1,0:T(8,128)(2,1)}, bf16[128,640]{1,0:T(8,128)(2,1)S(1)}, u32[]{:S(2)}, u32[]{:S(2)}) collective-permute-start(bf16[128,640]{1,0:T(8,128)(2,1)} %get-tuple-element.6.refs_0_), channel_id=1, source_target_pairs={{0,4},{4,0},{8,12},{12,8},{16,20},{20,16},{24,28},{28,24},{1,5},{5... | collective-permute-start | bytes 491528 | tf_op jit(solution)/shard_map/ppermute | solution.py:563
  16.5 9.9 %collective-permute-start.4 = (bf16[128,640]{1,0:T(8,128)(2,1)S(1)}, bf16[128,640]{1,0:T(8,128)(2,1)S(1)}, u32[]{:S(2)}, u32[]{:S(2)}) collective-permute-start(bf16[128,640]{1,0:T(8,128)(2,1)S(1)} %collective-permute-done.refs_1_), channel_id=1, source_target_pairs={{0,4},{4,0},{8,12},{12,8},{16,20},{20,16},{24,28},{28,24},{1,5},{5... | collective-permute-start | bytes 491528 | tf_op jit(solution)/shard_map/ppermute | solution.py:563
  19.9 6.4 %collective-permute-start.5 = (bf16[128,640]{1,0:T(8,128)(2,1)S(1)}, bf16[128,640]{1,0:T(8,128)(2,1)S(1)}, u32[]{:S(2)}, u32[]{:S(2)}) collective-permute-start(bf16[128,640]{1,0:T(8,128)(2,1)S(1)} %collective-permute-done.1.refs_2_), channel_id=1, source_target_pairs={{0,4},{4,0},{8,12},{12,8},{16,20},{20,16},{24,28},{28,24},{1,5},{5... | collective-permute-start | bytes 491528 | tf_op jit(solution)/shard_map/ppermute | solution.py:563
  19.9 6.4 %collective-permute-start.6 = (bf16[128,640]{1,0:T(8,128)(2,1)S(1)}, bf16[128,640]{1,0:T(8,128)(2,1)S(1)}, u32[]{:S(2)}, u32[]{:S(2)}) collective-permute-start(bf16[128,640]{1,0:T(8,128)(2,1)S(1)} %collective-permute-done.2.refs_3_), channel_id=1, source_target_pairs={{0,4},{4,0},{8,12},{12,8},{16,20},{20,16},{24,28},{28,24},{1,5},{5... | collective-permute-start | bytes 491528 | tf_op jit(solution)/shard_map/ppermute | solution.py:563
  20.5 5.9 %collective-permute-start.9 = (bf16[32,2176]{1,0:T(8,128)(2,1)}, bf16[32,2176]{1,0:T(8,128)(2,1)S(1)}, u32[]{:S(2)}, u32[]{:S(2)}) collective-permute-start(bf16[32,2176]{1,0:T(8,128)(2,1)} %get-tuple-element.7.refs_8_), channel_id=1, source_target_pairs={{0,3},{1,0},{2,1},{3,2},{4,7},{5,4},{6,5},{7,6},{8,11},{9,8},{10,9... | collective-permute-start | bytes 417800 | tf_op jit(solution)/shard_map/ppermute | solution.py:568
  26.4 0.7 copy-start
  27.1 0.9 %copy-start.1 = (bf16[128,640]{1,0:T(8,128)(2,1)S(1)}, bf16[128,640]{1,0:T(8,128)(2,1)}, u32[]{:S(2)}) copy-start(bf16[128,640]{1,0:T(8,128)(2,1)} %get-tuple-element.6.refs_0_) | copy-start | bytes 491524
  28.0 0.9 %copy-start.2 = (bf16[32,2176]{1,0:T(8,128)(2,1)S(1)}, bf16[32,2176]{1,0:T(8,128)(2,1)}, u32[]{:S(2)}) copy-start(bf16[32,2176]{1,0:T(8,128)(2,1)} %get-tuple-element.7.refs_8_) | copy-start | bytes 417796
  28.9 0.7 copy-start.3
  35.6 12.9 %collective-permute-start.10 = (bf16[32,1024]{1,0:T(8,128)(2,1)S(1)}, bf16[32,1024]{1,0:T(8,128)(2,1)S(1)}, u32[]{:S(2)}, u32[]{:S(2)}) collective-permute-start(bf16[32,1024]{1,0:T(8,128)(2,1)S(1)} %get-tuple-element.9.refs_0_), channel_id=1, source_target_pairs={{0,1},{1,2},{2,3},{3,0},{4,5},{5,6},{6,7},{7,4},{8,9},{9,10},{10,1... | collective-permute-start | bytes 196616 | tf_op jit(solution)/shard_map/ppermute | solution.py:568
  38.0 10.6 %collective-permute-start.11 = (bf16[32,1024]{1,0:T(8,128)(2,1)S(1)}, bf16[32,1024]{1,0:T(8,128)(2,1)S(1)}, u32[]{:S(2)}, u32[]{:S(2)}) collective-permute-start(bf16[32,1024]{1,0:T(8,128)(2,1)S(1)} %get-tuple-element.9.refs_0_), channel_id=1, source_target_pairs={{0,2},{1,3},{2,0},{3,1},{4,6},{5,7},{6,4},{7,5},{8,10},{9,11},{10,... | collective-permute-start | bytes 196616 | tf_op jit(solution)/shard_map/ppermute | solution.py:568
  39.5 9.1 %collective-permute-start.12 = (bf16[32,1024]{1,0:T(8,128)(2,1)S(1)}, bf16[32,1024]{1,0:T(8,128)(2,1)S(1)}, u32[]{:S(2)}, u32[]{:S(2)}) collective-permute-start(bf16[32,1024]{1,0:T(8,128)(2,1)S(1)} %get-tuple-element.9.refs_0_), channel_id=1, source_target_pairs={{0,3},{1,0},{2,1},{3,2},{4,7},{5,4},{6,5},{7,6},{8,11},{9,8},{10,9... | collective-permute-start | bytes 196616 | tf_op jit(solution)/shard_map/ppermute | solution.py:568
  40.1 8.5 %copy-start.4 = (s32[64]{0:T(128)S(1)}, s32[64]{0:T(128)}, u32[]{:S(2)}) copy-start(s32[64]{0:T(128)} %assign_ref.3) | copy-start | bytes 772
  49.8 11.6 %collective-permute-start.13 = (bf16[32,1024]{1,0:T(8,128)(2,1)S(1)}, bf16[32,1024]{1,0:T(8,128)(2,1)S(1)}, u32[]{:S(2)}, u32[]{:S(2)}) collective-permute-start(bf16[32,1024]{1,0:T(8,128)(2,1)S(1)} %select_rows.1), channel_id=1, source_target_pairs={{0,4},{4,0},{8,12},{12,8},{16,20},{20,16},{24,28},{28,24},{1,5},{5... | collective-permute-start | bytes 196616 | tf_op jit(solution)/shard_map/ppermute | solution.py:602
  61.4 17.9 %collective-permute-start.14 = (bf16[64,1024]{1,0:T(8,128)(2,1)S(1)}, bf16[64,1024]{1,0:T(8,128)(2,1)S(1)}, u32[]{:S(2)}, u32[]{:S(2)}) collective-permute-start(bf16[64,1024]{1,0:T(8,128)(2,1)S(1)} %pad_maximum_fusion.refs_0_), channel_id=1, source_target_pairs={{0,8},{4,12},{8,16},{12,20},{16,24},{20,28},{24,0},{28,4},{1,9},{5... | collective-permute-start | bytes 393224 | tf_op jit(solution)/shard_map/ppermute | solution.py:556
  65.4 14.0 %collective-permute-start.15 = (bf16[64,1024]{1,0:T(8,128)(2,1)S(1)}, bf16[64,1024]{1,0:T(8,128)(2,1)S(1)}, u32[]{:S(2)}, u32[]{:S(2)}) collective-permute-start(bf16[64,1024]{1,0:T(8,128)(2,1)S(1)} %pad_maximum_fusion.refs_0_), channel_id=1, source_target_pairs={{0,16},{4,20},{8,24},{12,28},{16,0},{20,4},{24,8},{28,12},{1,17},{... | collective-permute-start | bytes 393224 | tf_op jit(solution)/shard_map/ppermute | solution.py:556
  67.2 12.2 %collective-permute-start.16 = (bf16[64,1024]{1,0:T(8,128)(2,1)S(1)}, bf16[64,1024]{1,0:T(8,128)(2,1)S(1)}, u32[]{:S(2)}, u32[]{:S(2)}) collective-permute-start(bf16[64,1024]{1,0:T(8,128)(2,1)S(1)} %pad_maximum_fusion.refs_0_), channel_id=1, source_target_pairs={{0,24},{4,28},{8,0},{12,4},{16,8},{20,12},{24,16},{28,20},{1,25},{... | collective-permute-start | bytes 393224 | tf_op jit(solution)/shard_map/ppermute | solution.py:556

commit v4 on v3

--- a/solution.py
+++ b/solution.py
@@ -346,10 +346,10 @@
         pltpu.make_async_copy(pack, pack_ref.at[pl.ds(i * near, near)], sems.at[i])
         for i, pack in enumerate(packs)
     ]
-    early.append(pltpu.make_async_copy(ak_hbm.at[own], ak_ref, sems.at[spans]))
+    middle = pltpu.make_async_copy(ak_hbm.at[own], ak_ref, sems.at[spans])
     early.append(pltpu.make_async_copy(seg_hbm, seg_ref, sems.at[spans + 3]))
     late = pltpu.make_async_copy(av_hbm.at[own], av_ref, sems.at[spans + 1])
-    for copy in (*early, *copies, late):
+    for copy in (*early, middle, *copies):
         copy.start()
     row = lax.broadcasted_iota(jnp.int32, (near, 1), 0)
     want = jnp.zeros((near, 1), jnp.int32)
@@ -365,6 +365,7 @@
     wide = group * NOPE
     for copy in early:
         copy.wait()
+    late.start()
     pack = pack_ref[...]
     nope = jnp.dot(pick, pack[:, :wide], preferred_element_type=jnp.float32).astype(jnp.bfloat16)
     rope = jnp.dot(
@@ -373,6 +374,7 @@
     fresh = jnp.concatenate(
         [pack[:, wide : wide + LAT], pack[:, wide + LAT + group * ROPE :]], axis=1
     )
+    middle.wait()
     for h in range(group):
         lat = jnp.dot(
             nope[:, h * NOPE : (h + 1) * NOPE], ak_ref[h], preferred_element_type=jnp.float32

time: 81.2 us -> 81.3 us (level)
  no operation moved by 1% of the time
where the time goes in v4:
time: 81.3 us; the launch traced here: 80.7 us
  Pallas kernels  42.5 us (52%)
  starting transfers between devices  24.4 us (30%)
  waiting for transfers between devices  9.59 us (12%)
  local copies, waits for them, and re-layouts  3.19 us (4%)
  between operations  0.95 us (1%)
    pallas_call x2, Pallas kernels, attend_prefill(): pl.pallas_call(functools.partial(prefill_kernel, part=part, fast=fast, sl...  23 us
    ppermute x6, starting transfers between devices, spread_far(): lax.ppermute(value, 'seq', [(i, (i + 2 * k) % count) for i in range(count)])  13.5 us
    ppermute x6, starting transfers between devices, spread(): lax.ppermute(value, axis, [(i, (i + k) % count) for i in range(count)])  9.88 us
    pallas_call x1, Pallas kernels, absorb_prefill(): pl.pallas_call(functools.partial(absorb_kernel, group=group), in_specs=[F...  8.49 us
    ppermute x6, waiting for transfers between devices, spread(): lax.ppermute(value, axis, [(i, (i + k) % count) for i in range(count)])  6.64 us
    pallas_call x1, Pallas kernels, attend_decode(): pl.pallas_call(functools.partial(decode_kernel, count=count, spans=spans,...  6.08 us
    unnamed x10, local copies, waits for them, and re-layouts  3.19 us
    ppermute x6, waiting for transfers between devices, spread_far(): lax.ppermute(value, 'seq', [(i, (i + 2 * k) % count) for i in range(count)])  2.94 us
  transfers between devices with their start and end apart: 17, of which 3 were waited for; matrix products, arithmetic and copies ran while one was open for 0% of the time, Pallas kernels for 39%

profile of v4, /device:TPU:0, one launch (start us, length us, event | category | flops | bytes accessed | tf_op | source)
XLA Modules:
  0.0 80.7 jit_solution(15495153615280049261)
XLA Ops:
  0.6 2.6 %prepare.1 = (bf16[128,640]{1,0:T(8,128)(2,1)}, bf16[32,2176]{1,0:T(8,128)(2,1)}) custom-call(bf16[128,512]{1,0:T(8,128)(2,1)} %bitcast.12, bf16[64,128]{1,0:T(8,128)(2,1)} %bitcast.13, bf16[2,16,64,192]{3,2,1,0:T(8,128)(2,1)} %q_hbm.1, bf16[2,16,512]{2,1,0:T(8,128)(2,1)} %nl_ref.1, bf16[2,16,64]{2,1,0:T(8,128)(2,1)} %nr_ref.1), custom_call_target="tpu_custom_call" | custom-call | tf_op jit(solution)/shard_map/prepare/pallas_call | solution.py:79
  3.3 3.1 %collective-permute-start = (bf16[128,640]{1,0:T(8,128)(2,1)}, bf16[128,640]{1,0:T(8,128)(2,1)S(1)}, u32[]{:S(2)}, u32[]{:S(2)}) collective-permute-start(bf16[128,640]{1,0:T(8,128)(2,1)} %get-tuple-element.6.refs_0_), channel_id=1, source_target_pairs={{0,8},{4,12},{8,16},{12,20},{16,24},{20,28},{24,0},{28,4},{1,9},{5... | collective-permute-start | bytes 491528 | tf_op jit(solution)/shard_map/ppermute | solution.py:558
  6.4 2.6 %collective-permute-start.1 = (bf16[128,640]{1,0:T(8,128)(2,1)}, bf16[128,640]{1,0:T(8,128)(2,1)S(1)}, u32[]{:S(2)}, u32[]{:S(2)}) collective-permute-start(bf16[128,640]{1,0:T(8,128)(2,1)} %get-tuple-element.6.refs_0_), channel_id=1, source_target_pairs={{0,16},{4,20},{8,24},{12,28},{16,0},{20,4},{24,8},{28,12},{1,17},{... | collective-permute-start | bytes 491528 | tf_op jit(solution)/shard_map/ppermute | solution.py:558
  9.0 1.3 %collective-permute-start.2 = (bf16[128,640]{1,0:T(8,128)(2,1)}, bf16[128,640]{1,0:T(8,128)(2,1)S(1)}, u32[]{:S(2)}, u32[]{:S(2)}) collective-permute-start(bf16[128,640]{1,0:T(8,128)(2,1)} %get-tuple-element.6.refs_0_), channel_id=1, source_target_pairs={{0,24},{4,28},{8,0},{12,4},{16,8},{20,12},{24,16},{28,20},{1,25},{... | collective-permute-start | bytes 491528 | tf_op jit(solution)/shard_map/ppermute | solution.py:558
  10.3 1.5 %collective-permute-start.7 = (bf16[32,2176]{1,0:T(8,128)(2,1)}, bf16[32,2176]{1,0:T(8,128)(2,1)S(1)}, u32[]{:S(2)}, u32[]{:S(2)}) collective-permute-start(bf16[32,2176]{1,0:T(8,128)(2,1)} %get-tuple-element.7.refs_8_), channel_id=1, source_target_pairs={{0,1},{1,2},{2,3},{3,0},{4,5},{5,6},{6,7},{7,4},{8,9},{9,10},{10,1... | collective-permute-start | bytes 417800 | tf_op jit(solution)/shard_map/ppermute | solution.py:570
  11.8 1.5 %collective-permute-start.8 = (bf16[32,2176]{1,0:T(8,128)(2,1)}, bf16[32,2176]{1,0:T(8,128)(2,1)S(1)}, u32[]{:S(2)}, u32[]{:S(2)}) collective-permute-start(bf16[32,2176]{1,0:T(8,128)(2,1)} %get-tuple-element.7.refs_8_), channel_id=1, source_target_pairs={{0,2},{1,3},{2,0},{3,1},{4,6},{5,7},{6,4},{7,5},{8,10},{9,11},{10,... | collective-permute-start | bytes 417800 | tf_op jit(solution)/shard_map/ppermute | solution.py:570
  13.3 3.2 %collective-permute-done.7.refs_9_ = bf16[32,2176]{1,0:T(8,128)(2,1)S(1)} collective-permute-done((bf16[32,2176]{1,0:T(8,128)(2,1)}, bf16[32,2176]{1,0:T(8,128)(2,1)S(1)}, u32[]{:S(2)}, u32[]{:S(2)}) %collective-permute-start.7) | collective-permute-done | bytes 139296 | tf_op jit(solution)/shard_map/ppermute | solution.py:570
  16.5 0.0 collective-permute-done.refs_1_
  16.5 0.5 collective-permute-start.4
  17.0 2.9 %collective-permute-done.1.refs_2_ = bf16[128,640]{1,0:T(8,128)(2,1)S(1)} collective-permute-done((bf16[128,640]{1,0:T(8,128)(2,1)}, bf16[128,640]{1,0:T(8,128)(2,1)S(1)}, u32[]{:S(2)}, u32[]{:S(2)}) %collective-permute-start.1) | collective-permute-done | bytes 163872 | tf_op jit(solution)/shard_map/ppermute | solution.py:558
  19.9 0.5 collective-permute-start.6
  20.5 2.4 %collective-permute-start.9 = (bf16[32,2176]{1,0:T(8,128)(2,1)}, bf16[32,2176]{1,0:T(8,128)(2,1)S(1)}, u32[]{:S(2)}, u32[]{:S(2)}) collective-permute-start(bf16[32,2176]{1,0:T(8,128)(2,1)} %get-tuple-element.7.refs_8_), channel_id=1, source_target_pairs={{0,3},{1,0},{2,1},{3,2},{4,7},{5,4},{6,5},{7,6},{8,11},{9,8},{10,9... | collective-permute-start | bytes 417800 | tf_op jit(solution)/shard_map/ppermute | solution.py:570
  22.9 3.5 %collective-permute-done.9.refs_11_ = bf16[32,2176]{1,0:T(8,128)(2,1)S(1)} collective-permute-done((bf16[32,2176]{1,0:T(8,128)(2,1)}, bf16[32,2176]{1,0:T(8,128)(2,1)S(1)}, u32[]{:S(2)}, u32[]{:S(2)}) %collective-permute-start.9) | collective-permute-done | bytes 139296 | tf_op jit(solution)/shard_map/ppermute | solution.py:570
  26.4 0.0 collective-permute-done.6.refs_7_
  26.4 0.0 copy-start
  26.4 0.7 copy-done
  27.1 0.9 %copy-done.1 = bf16[128,640]{1,0:T(8,128)(2,1)S(1)} copy-done((bf16[128,640]{1,0:T(8,128)(2,1)S(1)}, bf16[128,640]{1,0:T(8,128)(2,1)}, u32[]{:S(2)}) %copy-start.1) | copy-done | bytes 163864
  28.0 0.9 %copy-done.2 = bf16[32,2176]{1,0:T(8,128)(2,1)S(1)} copy-done((bf16[32,2176]{1,0:T(8,128)(2,1)S(1)}, bf16[32,2176]{1,0:T(8,128)(2,1)}, u32[]{:S(2)}) %copy-start.2) | copy-done | bytes 139288
  28.9 0.7 copy-done.3
  29.6 6.1 %attend_decode.1 = (bf16[32,1024]{1,0:T(8,128)(2,1)S(1)}, bf16[1024,640]{1,0:T(8,128)(2,1)}) custom-call(s32[64]{0:T(128)S(1)} %copy-done.3, s32[4,1024]{1,0:T(4,128)S(1)} %copy-done, bf16[128,640]{1,0:T(8,128)(2,1)S(1)} %copy-done.1, bf16[128,640]{1,0:T(8,128)(2,1)S(1)} %collective-permute-done.refs_1_, ...), custom_call_target="tpu_custom_call" | custom-call | flops 603979776 | bytes 3407872 | tf_op jit(solution)/shard_map/attend_decode/pallas_call | solution.py:426
  35.7 2.4 %collective-permute-start.10 = (bf16[32,1024]{1,0:T(8,128)(2,1)S(1)}, bf16[32,1024]{1,0:T(8,128)(2,1)S(1)}, u32[]{:S(2)}, u32[]{:S(2)}) collective-permute-start(bf16[32,1024]{1,0:T(8,128)(2,1)S(1)} %get-tuple-element.9.refs_0_), channel_id=1, source_target_pairs={{0,1},{1,2},{2,3},{3,0},{4,5},{5,6},{6,7},{7,4},{8,9},{9,10},{10,1... | collective-permute-start | bytes 196616 | tf_op jit(solution)/shard_map/ppermute | solution.py:570
  38.0 1.5 %collective-permute-start.11 = (bf16[32,1024]{1,0:T(8,128)(2,1)S(1)}, bf16[32,1024]{1,0:T(8,128)(2,1)S(1)}, u32[]{:S(2)}, u32[]{:S(2)}) collective-permute-start(bf16[32,1024]{1,0:T(8,128)(2,1)S(1)} %get-tuple-element.9.refs_0_), channel_id=1, source_target_pairs={{0,2},{1,3},{2,0},{3,1},{4,6},{5,7},{6,4},{7,5},{8,10},{9,11},{10,... | collective-permute-start | bytes 196616 | tf_op jit(solution)/shard_map/ppermute | solution.py:570
  39.6 0.5 collective-permute-start.12
  40.1 8.5 %absorb_prefill.1.qa_hbm = bf16[8,1024,640]{2,1,0:T(8,128)(2,1)} custom-call(bf16[64,192,128]{2,1,0:T(8,128)(2,1)} %bitcast.10, bf16[64,128,512]{2,1,0:T(8,128)(2,1)} %refs_12_.1), custom_call_target="tpu_custom_call" | custom-call | flops 1073741824 | bytes 22020096 | tf_op jit(solution)/shard_map/absorb_prefill/pallas_call | solution.py:134
  48.6 1.2 %select_rows.1 = bf16[32,1024]{1,0:T(8,128)(2,1)S(1)} custom-call(s32[64]{0:T(128)S(1)} %copy-done.4, bf16[32,1024]{1,0:T(8,128)(2,1)S(1)} %get-tuple-element.9.refs_0_, bf16[32,1024]{1,0:T(8,128)(2,1)S(1)} %collective-permute-done.10.refs_1_, bf16[32,1024]{1,0:T(8,128)(2,1)S(1)} %collective-permute-done.11.refs_2_, ...), custom_call_target="tpu_custom_call" | custom-call | tf_op jit(solution)/shard_map/select_rows/pallas_call | solution.py:494
  49.8 0.1 collective-permute-start.13
  49.9 11.5 %shard_map.113.refs_0_ = bf16[128,8192]{1,0:T(8,128)(2,1)} custom-call(s32[4,1024]{1,0:T(4,128)} %seg_hbm.5, s32[4,1024]{1,0:T(4,128)} %seg_hbm.5, bf16[8,1024,640]{2,1,0:T(8,128)(2,1)} %absorb_prefill.1.qa_hbm, bf16[1024,640]{1,0:T(8,128)(2,1)} %get-tuple-element.8.keys_hbm, bf16[64,512,128]{2,1,0:T(8,128)(2,1)} %refs_1_.1), custom_call_target="tpu_custom_call" | custom-call | flops 5368709120 | bytes 10485760 | tf_op jit(solution)/shard_map/pallas_call | solution.py:292
  61.5 4.0 %collective-permute-start.14 = (bf16[64,1024]{1,0:T(8,128)(2,1)S(1)}, bf16[64,1024]{1,0:T(8,128)(2,1)S(1)}, u32[]{:S(2)}, u32[]{:S(2)}) collective-permute-start(bf16[64,1024]{1,0:T(8,128)(2,1)S(1)} %pad_maximum_fusion.refs_0_), channel_id=1, source_target_pairs={{0,8},{4,12},{8,16},{12,20},{16,24},{20,28},{24,0},{28,4},{1,9},{5... | collective-permute-start | bytes 393224 | tf_op jit(solution)/shard_map/ppermute | solution.py:558
  65.4 1.8 %collective-permute-start.15 = (bf16[64,1024]{1,0:T(8,128)(2,1)S(1)}, bf16[64,1024]{1,0:T(8,128)(2,1)S(1)}, u32[]{:S(2)}, u32[]{:S(2)}) collective-permute-start(bf16[64,1024]{1,0:T(8,128)(2,1)S(1)} %pad_maximum_fusion.refs_0_), channel_id=1, source_target_pairs={{0,16},{4,20},{8,24},{12,28},{16,0},{20,4},{24,8},{28,12},{1,17},{... | collective-permute-start | bytes 393224 | tf_op jit(solution)/shard_map/ppermute | solution.py:558
  67.2 0.7 collective-permute-start.16
  67.9 11.5 %shard_map.114 = bf16[128,8192]{1,0:T(8,128)(2,1)} custom-call(s32[4,1024]{1,0:T(4,128)} %seg_hbm.5, s32[4,1024]{1,0:T(4,128)} %seg_hbm.5, bf16[8,1024,640]{2,1,0:T(8,128)(2,1)} %absorb_prefill.1.qa_hbm, bf16[1024,640]{1,0:T(8,128)(2,1)} %get-tuple-element.8.keys_hbm, bf16[128,8192]{1,0:T(8,128)(2,1)} %shard_map.113.refs_0_, ...), custom_call_target="tpu_custom_call", output_to_operand_aliasing={{}: (4, {})} | custom-call | flops 5368709120 | bytes 10485760 | tf_op jit(solution)/shard_map/pallas_call | solution.py:292
  79.4 1.1 %assemble.1 = bf16[32,8192]{1,0:T(8,128)(2,1)} custom-call(bf16[64,1024]{1,0:T(8,128)(2,1)S(1)} %pad_maximum_fusion.refs_0_, bf16[64,1024]{1,0:T(8,128)(2,1)S(1)} %collective-permute-done.14.refs_1_, bf16[64,1024]{1,0:T(8,128)(2,1)S(1)} %collective-permute-done.15.refs_2_, bf16[64,1024]{1,0:T(8,128)(2,1)S(1)} %collective-permute-done.16.refs_3_), custom_call_target="tpu_custom_call" | custom-call | tf_op jit(solution)/shard_map/assemble/pallas_call | solution.py:541
  (20 shorter events, 0.1 us)
Async XLA Ops:
  3.3 13.2 %collective-permute-start = (bf16[128,640]{1,0:T(8,128)(2,1)}, bf16[128,640]{1,0:T(8,128)(2,1)S(1)}, u32[]{:S(2)}, u32[]{:S(2)}) collective-permute-start(bf16[128,640]{1,0:T(8,128)(2,1)} %get-tuple-element.6.refs_0_), channel_id=1, source_target_pairs={{0,8},{4,12},{8,16},{12,20},{16,24},{20,28},{24,0},{28,4},{1,9},{5... | collective-permute-start | bytes 491528 | tf_op jit(solution)/shard_map/ppermute | solution.py:558
  6.4 13.5 %collective-permute-start.1 = (bf16[128,640]{1,0:T(8,128)(2,1)}, bf16[128,640]{1,0:T(8,128)(2,1)S(1)}, u32[]{:S(2)}, u32[]{:S(2)}) collective-permute-start(bf16[128,640]{1,0:T(8,128)(2,1)} %get-tuple-element.6.refs_0_), channel_id=1, source_target_pairs={{0,16},{4,20},{8,24},{12,28},{16,0},{20,4},{24,8},{28,12},{1,17},{... | collective-permute-start | bytes 491528 | tf_op jit(solution)/shard_map/ppermute | solution.py:558
  9.0 11.0 %collective-permute-start.2 = (bf16[128,640]{1,0:T(8,128)(2,1)}, bf16[128,640]{1,0:T(8,128)(2,1)S(1)}, u32[]{:S(2)}, u32[]{:S(2)}) collective-permute-start(bf16[128,640]{1,0:T(8,128)(2,1)} %get-tuple-element.6.refs_0_), channel_id=1, source_target_pairs={{0,24},{4,28},{8,0},{12,4},{16,8},{20,12},{24,16},{28,20},{1,25},{... | collective-permute-start | bytes 491528 | tf_op jit(solution)/shard_map/ppermute | solution.py:558
  10.3 6.2 %collective-permute-start.7 = (bf16[32,2176]{1,0:T(8,128)(2,1)}, bf16[32,2176]{1,0:T(8,128)(2,1)S(1)}, u32[]{:S(2)}, u32[]{:S(2)}) collective-permute-start(bf16[32,2176]{1,0:T(8,128)(2,1)} %get-tuple-element.7.refs_8_), channel_id=1, source_target_pairs={{0,1},{1,2},{2,3},{3,0},{4,5},{5,6},{6,7},{7,4},{8,9},{9,10},{10,1... | collective-permute-start | bytes 417800 | tf_op jit(solution)/shard_map/ppermute | solution.py:570
  11.8 8.6 %collective-permute-start.8 = (bf16[32,2176]{1,0:T(8,128)(2,1)}, bf16[32,2176]{1,0:T(8,128)(2,1)S(1)}, u32[]{:S(2)}, u32[]{:S(2)}) collective-permute-start(bf16[32,2176]{1,0:T(8,128)(2,1)} %get-tuple-element.7.refs_8_), channel_id=1, source_target_pairs={{0,2},{1,3},{2,0},{3,1},{4,6},{5,7},{6,4},{7,5},{8,10},{9,11},{10,... | collective-permute-start | bytes 417800 | tf_op jit(solution)/shard_map/ppermute | solution.py:570
  16.5 9.9 %collective-permute-start.3 = (bf16[128,640]{1,0:T(8,128)(2,1)}, bf16[128,640]{1,0:T(8,128)(2,1)S(1)}, u32[]{:S(2)}, u32[]{:S(2)}) collective-permute-start(bf16[128,640]{1,0:T(8,128)(2,1)} %get-tuple-element.6.refs_0_), channel_id=1, source_target_pairs={{0,4},{4,0},{8,12},{12,8},{16,20},{20,16},{24,28},{28,24},{1,5},{5... | collective-permute-start | bytes 491528 | tf_op jit(solution)/shard_map/ppermute | solution.py:565
  16.5 9.9 %collective-permute-start.4 = (bf16[128,640]{1,0:T(8,128)(2,1)S(1)}, bf16[128,640]{1,0:T(8,128)(2,1)S(1)}, u32[]{:S(2)}, u32[]{:S(2)}) collective-permute-start(bf16[128,640]{1,0:T(8,128)(2,1)S(1)} %collective-permute-done.refs_1_), channel_id=1, source_target_pairs={{0,4},{4,0},{8,12},{12,8},{16,20},{20,16},{24,28},{28,24},{1,5},{5... | collective-permute-start | bytes 491528 | tf_op jit(solution)/shard_map/ppermute | solution.py:565
  19.9 6.4 %collective-permute-start.5 = (bf16[128,640]{1,0:T(8,128)(2,1)S(1)}, bf16[128,640]{1,0:T(8,128)(2,1)S(1)}, u32[]{:S(2)}, u32[]{:S(2)}) collective-permute-start(bf16[128,640]{1,0:T(8,128)(2,1)S(1)} %collective-permute-done.1.refs_2_), channel_id=1, source_target_pairs={{0,4},{4,0},{8,12},{12,8},{16,20},{20,16},{24,28},{28,24},{1,5},{5... | collective-permute-start | bytes 491528 | tf_op jit(solution)/shard_map/ppermute | solution.py:565
  19.9 6.4 %collective-permute-start.6 = (bf16[128,640]{1,0:T(8,128)(2,1)S(1)}, bf16[128,640]{1,0:T(8,128)(2,1)S(1)}, u32[]{:S(2)}, u32[]{:S(2)}) collective-permute-start(bf16[128,640]{1,0:T(8,128)(2,1)S(1)} %collective-permute-done.2.refs_3_), channel_id=1, source_target_pairs={{0,4},{4,0},{8,12},{12,8},{16,20},{20,16},{24,28},{28,24},{1,5},{5... | collective-permute-start | bytes 491528 | tf_op jit(solution)/shard_map/ppermute | solution.py:565
  20.5 5.9 %collective-permute-start.9 = (bf16[32,2176]{1,0:T(8,128)(2,1)}, bf16[32,2176]{1,0:T(8,128)(2,1)S(1)}, u32[]{:S(2)}, u32[]{:S(2)}) collective-permute-start(bf16[32,2176]{1,0:T(8,128)(2,1)} %get-tuple-element.7.refs_8_), channel_id=1, source_target_pairs={{0,3},{1,0},{2,1},{3,2},{4,7},{5,4},{6,5},{7,6},{8,11},{9,8},{10,9... | collective-permute-start | bytes 417800 | tf_op jit(solution)/shard_map/ppermute | solution.py:570
  26.4 0.7 copy-start
  27.1 0.9 %copy-start.1 = (bf16[128,640]{1,0:T(8,128)(2,1)S(1)}, bf16[128,640]{1,0:T(8,128)(2,1)}, u32[]{:S(2)}) copy-start(bf16[128,640]{1,0:T(8,128)(2,1)} %get-tuple-element.6.refs_0_) | copy-start | bytes 491524
  28.0 0.9 %copy-start.2 = (bf16[32,2176]{1,0:T(8,128)(2,1)S(1)}, bf16[32,2176]{1,0:T(8,128)(2,1)}, u32[]{:S(2)}) copy-start(bf16[32,2176]{1,0:T(8,128)(2,1)} %get-tuple-element.7.refs_8_) | copy-start | bytes 417796
  28.9 0.7 copy-start.3
  35.7 12.9 %collective-permute-start.10 = (bf16[32,1024]{1,0:T(8,128)(2,1)S(1)}, bf16[32,1024]{1,0:T(8,128)(2,1)S(1)}, u32[]{:S(2)}, u32[]{:S(2)}) collective-permute-start(bf16[32,1024]{1,0:T(8,128)(2,1)S(1)} %get-tuple-element.9.refs_0_), channel_id=1, source_target_pairs={{0,1},{1,2},{2,3},{3,0},{4,5},{5,6},{6,7},{7,4},{8,9},{9,10},{10,1... | collective-permute-start | bytes 196616 | tf_op jit(solution)/shard_map/ppermute | solution.py:570
  38.0 10.6 %collective-permute-start.11 = (bf16[32,1024]{1,0:T(8,128)(2,1)S(1)}, bf16[32,1024]{1,0:T(8,128)(2,1)S(1)}, u32[]{:S(2)}, u32[]{:S(2)}) collective-permute-start(bf16[32,1024]{1,0:T(8,128)(2,1)S(1)} %get-tuple-element.9.refs_0_), channel_id=1, source_target_pairs={{0,2},{1,3},{2,0},{3,1},{4,6},{5,7},{6,4},{7,5},{8,10},{9,11},{10,... | collective-permute-start | bytes 196616 | tf_op jit(solution)/shard_map/ppermute | solution.py:570
  39.6 9.1 %collective-permute-start.12 = (bf16[32,1024]{1,0:T(8,128)(2,1)S(1)}, bf16[32,1024]{1,0:T(8,128)(2,1)S(1)}, u32[]{:S(2)}, u32[]{:S(2)}) collective-permute-start(bf16[32,1024]{1,0:T(8,128)(2,1)S(1)} %get-tuple-element.9.refs_0_), channel_id=1, source_target_pairs={{0,3},{1,0},{2,1},{3,2},{4,7},{5,4},{6,5},{7,6},{8,11},{9,8},{10,9... | collective-permute-start | bytes 196616 | tf_op jit(solution)/shard_map/ppermute | solution.py:570
  40.1 8.5 %copy-start.4 = (s32[64]{0:T(128)S(1)}, s32[64]{0:T(128)}, u32[]{:S(2)}) copy-start(s32[64]{0:T(128)} %assign_ref.3) | copy-start | bytes 772
  49.8 11.6 %collective-permute-start.13 = (bf16[32,1024]{1,0:T(8,128)(2,1)S(1)}, bf16[32,1024]{1,0:T(8,128)(2,1)S(1)}, u32[]{:S(2)}, u32[]{:S(2)}) collective-permute-start(bf16[32,1024]{1,0:T(8,128)(2,1)S(1)} %select_rows.1), channel_id=1, source_target_pairs={{0,4},{4,0},{8,12},{12,8},{16,20},{20,16},{24,28},{28,24},{1,5},{5... | collective-permute-start | bytes 196616 | tf_op jit(solution)/shard_map/ppermute | solution.py:604
  61.5 17.9 %collective-permute-start.14 = (bf16[64,1024]{1,0:T(8,128)(2,1)S(1)}, bf16[64,1024]{1,0:T(8,128)(2,1)S(1)}, u32[]{:S(2)}, u32[]{:S(2)}) collective-permute-start(bf16[64,1024]{1,0:T(8,128)(2,1)S(1)} %pad_maximum_fusion.refs_0_), channel_id=1, source_target_pairs={{0,8},{4,12},{8,16},{12,20},{16,24},{20,28},{24,0},{28,4},{1,9},{5... | collective-permute-start | bytes 393224 | tf_op jit(solution)/shard_map/ppermute | solution.py:558
  65.4 14.0 %collective-permute-start.15 = (bf16[64,1024]{1,0:T(8,128)(2,1)S(1)}, bf16[64,1024]{1,0:T(8,128)(2,1)S(1)}, u32[]{:S(2)}, u32[]{:S(2)}) collective-permute-start(bf16[64,1024]{1,0:T(8,128)(2,1)S(1)} %pad_maximum_fusion.refs_0_), channel_id=1, source_target_pairs={{0,16},{4,20},{8,24},{12,28},{16,0},{20,4},{24,8},{28,12},{1,17},{... | collective-permute-start | bytes 393224 | tf_op jit(solution)/shard_map/ppermute | solution.py:558
  67.2 12.2 %collective-permute-start.16 = (bf16[64,1024]{1,0:T(8,128)(2,1)S(1)}, bf16[64,1024]{1,0:T(8,128)(2,1)S(1)}, u32[]{:S(2)}, u32[]{:S(2)}) collective-permute-start(bf16[64,1024]{1,0:T(8,128)(2,1)S(1)} %pad_maximum_fusion.refs_0_), channel_id=1, source_target_pairs={{0,24},{4,28},{8,0},{12,4},{16,8},{20,12},{24,16},{28,20},{1,25},{... | collective-permute-start | bytes 393224 | tf_op jit(solution)/shard_map/ppermute | solution.py:558
